TPU v7x, 32 devices: a whole 2x2x4 slice. The times are simulated.
32 devices in a mesh: section: 2 (over core), dp: 8 (over z, x), seq: 2 (over y).
Axes of the slice: x: 2, y: 2, z: 4, core: 2. Of those that a mesh axis runs over, the one named last changes fastest.
Arguments:
- tokens: bfloat16 [4, 8, 1024, 768], P(None, 'dp', 'seq'), may hold values from -6 to 6
- segments: int32 [4, 8, 1024], P(None, 'dp'), may hold values from 0 to 4, as said below
- cotangent: bfloat16 [4, 8, 1024, 768], P(None, 'dp', 'seq'), may hold values from -6 to 6
- joint_weight: bfloat16 [2, 768, 2304], P('section'), may hold values from -0.21875 to 0.21875
- joint_bias: float32 [2, 2304], P('section'), may hold values from -2 to 2
- output_weight: bfloat16 [2, 768, 768], P('section'), may hold values from -0.21875 to 0.21875
- output_bias: float32 [2, 768], P('section'), may hold values from -2 to 2
- up_weight: bfloat16 [2, 768, 3072], P('section'), may hold values from -0.21875 to 0.21875
- up_bias: float32 [2, 3072], P('section'), may hold values from -2 to 2
- down_weight: bfloat16 [2, 3072, 768], P('section'), may hold values from -0.109375 to 0.109375
- down_bias: float32 [2, 768], P('section'), may hold values from -2 to 2
- first_gain: float32 [2, 768], P('section'), may hold values from 0.25 to 1.75
- inner_gain: float32 [2, 768], P('section'), may hold values from 0.25 to 1.75
- second_gain: float32 [2, 768], P('section'), may hold values from 0.25 to 1.75
- hidden_gain: float32 [2, 3072], P('section'), may hold values from 0.25 to 1.75
Outputs:
- hiddens: bfloat16 [2, 4, 8, 1024, 768], P('section', None, 'dp', 'seq')
- input_gradients: float32 [2, 4, 8, 1024, 768], P('section', None, 'dp', 'seq')
- joint_weight_gradient: float32 [2, 768, 2304], P('section', None, ('dp', 'seq'))
- joint_bias_gradient: float32 [2, 2304], P('section', ('dp', 'seq'))
- output_weight_gradient: float32 [2, 768, 768], P('section', None, ('dp', 'seq'))
- output_bias_gradient: float32 [2, 768], P('section', ('dp', 'seq'))
- up_weight_gradient: float32 [2, 768, 3072], P('section', None, ('dp', 'seq'))
- up_bias_gradient: float32 [2, 3072], P('section', ('dp', 'seq'))
- down_weight_gradient: float32 [2, 3072, 768], P('section', None, ('dp', 'seq'))
- down_bias_gradient: float32 [2, 768], P('section', ('dp', 'seq'))
- first_gain_gradient: float32 [2, 768], P('section', ('dp', 'seq'))
- inner_gain_gradient: float32 [2, 768], P('section', ('dp', 'seq'))
- second_gain_gradient: float32 [2, 768], P('section', ('dp', 'seq'))
- hidden_gain_gradient: float32 [2, 3072], P('section', ('dp', 'seq'))
Inputs may be any that keep to these rules, and one draw needn't show every extreme that they name: `segments`: along a row the ids never fall, and the row starts with id 0.
All inputs are finite; a program needn't handle non-finite values.
Results may differ from a plain program's by a relative error of at most 0.015.
Values may be sent and summed in bfloat16 or wider, within the bound.
A program may use at most 512 MiB of HBM per device.

v0:
```python
import jax
import jax.numpy as jnp
from jax import lax
from jax.sharding import PartitionSpec as P

HEAD_DIM = 64


EPSILON = 1e-05
MASKED = -1e30


def passed_along(value, axis, by):
    devices = lax.axis_size(axis)
    pairs = [(i, i + by) for i in range(devices) if 0 <= i + by < devices]
    return lax.ppermute(value, axis, pairs)


def layer_norm(value, gain):
    centered = value - jnp.mean(value, axis=-1, keepdims=True)
    spread = jnp.mean(centered * centered, axis=-1, keepdims=True)
    return centered * lax.rsqrt(spread + EPSILON) * gain


def feed_norm(before, gain):
    return layer_norm(jax.nn.gelu(before, approximate=False), gain)


def rotate(value, cosine, sine):
    middle = value.shape[-1] // 2
    first, second = (value[..., :middle], value[..., middle:])
    return jnp.concatenate(
        [first * cosine - second * sine, second * cosine + first * sine], axis=-1
    )


def rotate_back(incoming, cosine, sine):
    middle = incoming.shape[-1] // 2
    first, second = (incoming[..., :middle], incoming[..., middle:])
    return jnp.concatenate(
        [first * cosine + second * sine, second * cosine - first * sine], axis=-1
    )


def layer_forward(state, labels, weights, part):
    (
        joint_weight,
        joint_bias,
        output_weight,
        output_bias,
        up_weight,
        up_bias,
        down_weight,
        down_bias,
        first_gain,
        inner_gain,
        second_gain,
        hidden_gain,
    ) = weights
    row_count, piece_len, model_width = state.shape
    head_count = model_width // HEAD_DIM
    shape_heads = (row_count, piece_len, head_count, HEAD_DIM)
    offset = part * piece_len
    local_labels = lax.dynamic_slice_in_dim(labels, offset, piece_len, 1)
    starts = jnp.sum((labels[:, None, :] < local_labels[:, :, None]).astype(jnp.int32), axis=-1)
    places = offset + jnp.arange(piece_len, dtype=jnp.int32)[None, :] - starts
    inverse_rate = 1.0 / 10000.0 ** (jnp.arange(HEAD_DIM // 2, dtype=jnp.float32) * 2.0 / HEAD_DIM)
    angle = places.astype(jnp.float32)[:, :, None, None] * inverse_rate
    cosine = jnp.cos(angle)
    sine = jnp.sin(angle)
    normed = layer_norm(state, first_gain).astype(jnp.bfloat16)
    joint = jnp.dot(normed, joint_weight, preferred_element_type=jnp.float32) + joint_bias
    query = rotate(joint[..., :model_width].reshape(shape_heads), cosine, sine).astype(jnp.bfloat16)
    key = rotate(
        joint[..., model_width : 2 * model_width].reshape(shape_heads), cosine, sine
    ).astype(jnp.bfloat16)
    value = joint[..., 2 * model_width :].reshape(shape_heads).astype(jnp.bfloat16)
    keys_all, values_all = (
        lax.all_gather(key, "seq", axis=1, tiled=True),
        lax.all_gather(value, "seq", axis=1, tiled=True),
    )
    match = local_labels[:, None, :, None] == labels[:, None, None, :]
    scores = jnp.einsum(
        "rqhd,rkhd->rhqk", query, keys_all, preferred_element_type=jnp.float32
    ) * HEAD_DIM ** (-0.5)
    scores = jnp.where(match, scores, MASKED)
    peak = jnp.max(scores, axis=-1, keepdims=True)
    raised = jnp.exp(scores - peak)
    total_raised = jnp.sum(raised, axis=-1, keepdims=True)
    shares = raised / total_raised
    log_total = peak + jnp.log(total_raised)
    attended = jnp.einsum(
        "rhqk,rkhd->rqhd",
        shares.astype(jnp.bfloat16),
        values_all,
        preferred_element_type=jnp.float32,
    ).reshape(row_count, piece_len, model_width)
    inner = layer_norm(attended, inner_gain).astype(jnp.bfloat16)
    mixed = state + jnp.dot(inner, output_weight, preferred_element_type=jnp.float32) + output_bias
    normed_two = layer_norm(mixed, second_gain).astype(jnp.bfloat16)
    before = jnp.dot(normed_two, up_weight, preferred_element_type=jnp.float32) + up_bias
    hidden = feed_norm(before, hidden_gain).astype(jnp.bfloat16)
    result = mixed + jnp.dot(hidden, down_weight, preferred_element_type=jnp.float32) + down_bias
    kept = (
        state,
        normed,
        query,
        keys_all,
        values_all,
        cosine,
        sine,
        match,
        shares,
        attended,
        inner,
        mixed,
        normed_two,
        before,
        hidden,
        log_total,
        labels,
    )
    return (result, kept)


def feed_backward(kept, slope_out, weights, totals):
    (
        state,
        normed,
        query,
        keys_all,
        values_all,
        cosine,
        sine,
        match,
        shares,
        attended,
        inner,
        mixed,
        normed_two,
        before,
        hidden,
        log_total,
        labels,
    ) = kept
    (
        joint_weight,
        joint_bias,
        output_weight,
        output_bias,
        up_weight,
        up_bias,
        down_weight,
        down_bias,
        first_gain,
        inner_gain,
        second_gain,
        hidden_gain,
    ) = weights
    slope_low = slope_out.astype(jnp.bfloat16)
    totals[6] = totals[6] + jnp.einsum(
        "rcf,rcd->fd", hidden, slope_low, preferred_element_type=jnp.float32
    )
    totals[7] = totals[7] + jnp.sum(slope_low.astype(jnp.float32), axis=(0, 1))
    slope_hidden = jnp.einsum(
        "rcd,fd->rcf", slope_low, down_weight, preferred_element_type=jnp.float32
    )
    unused, puller = jax.vjp(feed_norm, before, hidden_gain)
    slope_before, slope_gain = puller(slope_hidden)
    totals[11] = totals[11] + slope_gain
    before_low = slope_before.astype(jnp.bfloat16)
    totals[4] = totals[4] + jnp.einsum(
        "rcd,rcf->df", normed_two, before_low, preferred_element_type=jnp.float32
    )
    totals[5] = totals[5] + jnp.sum(before_low.astype(jnp.float32), axis=(0, 1))
    slope_normed = jnp.einsum(
        "rcf,df->rcd", before_low, up_weight, preferred_element_type=jnp.float32
    )
    unused, puller = jax.vjp(layer_norm, mixed, second_gain)
    slope_mixed, slope_gain = puller(slope_normed)
    totals[10] = totals[10] + slope_gain
    return (slope_out + slope_mixed, totals)


def attend_backward(kept, slope_mixed, weights, totals):
    (
        state,
        normed,
        query,
        keys_all,
        values_all,
        cosine,
        sine,
        match,
        shares,
        attended,
        inner,
        mixed,
        normed_two,
        before,
        hidden,
        log_total,
        labels,
    ) = kept
    (
        joint_weight,
        joint_bias,
        output_weight,
        output_bias,
        up_weight,
        up_bias,
        down_weight,
        down_bias,
        first_gain,
        inner_gain,
        second_gain,
        hidden_gain,
    ) = weights
    row_count, piece_len, model_width = state.shape
    head_count = model_width // HEAD_DIM
    scale = HEAD_DIM ** (-0.5)
    slope_low = slope_mixed.astype(jnp.bfloat16)
    totals[2] = totals[2] + jnp.einsum(
        "rcd,rce->de", inner, slope_low, preferred_element_type=jnp.float32
    )
    totals[3] = totals[3] + jnp.sum(slope_low.astype(jnp.float32), axis=(0, 1))
    slope_inner = jnp.einsum(
        "rce,de->rcd", slope_low, output_weight, preferred_element_type=jnp.float32
    )
    unused, puller = jax.vjp(layer_norm, attended, inner_gain)
    slope_attended, slope_gain = puller(slope_inner)
    totals[9] = totals[9] + slope_gain
    slope_heads = slope_attended.astype(jnp.bfloat16).reshape(
        row_count, piece_len, head_count, HEAD_DIM
    )
    slope_shares = jnp.einsum(
        "rqhd,rkhd->rhqk", slope_heads, values_all, preferred_element_type=jnp.float32
    )
    weighted = jnp.sum(shares * slope_shares, axis=-1, keepdims=True)
    slope_scores = (shares * (slope_shares - weighted)).astype(jnp.bfloat16)
    slope_query = (
        jnp.einsum("rhqk,rkhd->rqhd", slope_scores, keys_all, preferred_element_type=jnp.float32)
        * scale
    )
    shares_low = shares.astype(jnp.bfloat16)
    key_part = (
        jnp.einsum("rhqk,rqhd->krhd", slope_scores, query, preferred_element_type=jnp.float32)
        * scale
    )
    value_part = jnp.einsum(
        "rhqk,rqhd->krhd", shares_low, slope_heads, preferred_element_type=jnp.float32
    )
    summed = lax.psum_scatter(
        jnp.concatenate([key_part, value_part], axis=-1).astype(jnp.bfloat16),
        "seq",
        scatter_dimension=0,
        tiled=True,
    ).astype(jnp.float32)
    summed = jnp.transpose(summed, (1, 0, 2, 3))
    key_raw = summed[..., :HEAD_DIM]
    slope_value = summed[..., HEAD_DIM:]
    slope_key = rotate_back(key_raw, cosine, sine)
    slope_query = rotate_back(slope_query, cosine, sine)
    flat = (row_count, piece_len, model_width)
    slope_joint = jnp.concatenate(
        [slope_query.reshape(flat), slope_key.reshape(flat), slope_value.reshape(flat)], axis=-1
    ).astype(jnp.bfloat16)
    totals[0] = totals[0] + jnp.einsum(
        "rcd,rce->de", normed, slope_joint, preferred_element_type=jnp.float32
    )
    totals[1] = totals[1] + jnp.sum(slope_joint.astype(jnp.float32), axis=(0, 1))
    slope_normed = jnp.einsum(
        "rce,de->rcd", slope_joint, joint_weight, preferred_element_type=jnp.float32
    )
    unused, puller = jax.vjp(layer_norm, state, first_gain)
    slope_state, slope_gain = puller(slope_normed)
    totals[8] = totals[8] + slope_gain
    return (slope_mixed + slope_state, totals)


def lift(vector):
    return vector.reshape(1, vector.shape[0])


def shards(
    tokens,
    segments,
    cotangent,
    joint_weight,
    joint_bias,
    output_weight,
    output_bias,
    up_weight,
    up_bias,
    down_weight,
    down_bias,
    first_gain,
    inner_gain,
    second_gain,
    hidden_gain,
):
    weights = tuple(
        (
            item[0]
            for item in (
                joint_weight,
                joint_bias,
                output_weight,
                output_bias,
                up_weight,
                up_bias,
                down_weight,
                down_bias,
                first_gain,
                inner_gain,
                second_gain,
                hidden_gain,
            )
        )
    )
    micro, row_count, piece_len, model_width = tokens.shape
    leading = lax.axis_index("section") == 0
    part = lax.axis_index("seq")
    received = jnp.zeros((row_count, piece_len, model_width), jnp.bfloat16)
    saved = []
    results = []
    for moment in range(micro + 1):
        labels = jnp.where(leading, segments[min(moment, micro - 1)], segments[max(moment - 1, 0)])
        source = jnp.where(leading, tokens[min(moment, micro - 1)], received)
        state = source.astype(jnp.float32)
        result, kept = layer_forward(state, labels, weights, part)
        sent = result.astype(jnp.bfloat16)
        results.append(sent)
        saved.append((state, labels))
        if moment < micro:
            received = passed_along(sent, "section", 1)
    totals = [jnp.zeros(item.shape, jnp.float32) for item in weights]
    back_received = jnp.zeros((row_count, piece_len, model_width), jnp.bfloat16)
    back_results = []
    for moment in range(micro + 1):
        earlier = max(moment - 1, 0)
        later = min(moment + 1, micro)
        state = jnp.where(leading, saved[earlier][0], saved[later][0])
        labels = jnp.where(leading, saved[earlier][1], saved[later][1])
        kept = layer_forward(state, labels, weights, part)[1]
        if moment < micro:
            outer = cotangent[moment].astype(jnp.float32)
        else:
            outer = jnp.zeros((row_count, piece_len, model_width), jnp.float32)
        slope_out = jnp.where(leading, back_received.astype(jnp.float32), outer)
        slope_mixed, totals = feed_backward(kept, slope_out, weights, totals)
        slope_input, totals = attend_backward(kept, slope_mixed, weights, totals)
        back_results.append(slope_input)
        if moment < micro:
            back_received = passed_along(slope_input.astype(jnp.bfloat16), "section", -1)
    reduced = (
        lax.psum_scatter(totals[0], ("dp", "seq"), scatter_dimension=1, tiled=True),
        lax.psum_scatter(lift(totals[1]), ("dp", "seq"), scatter_dimension=1, tiled=True),
        lax.psum_scatter(totals[2], ("dp", "seq"), scatter_dimension=1, tiled=True),
        lax.psum_scatter(lift(totals[3]), ("dp", "seq"), scatter_dimension=1, tiled=True),
        lax.psum_scatter(totals[4], ("dp", "seq"), scatter_dimension=1, tiled=True),
        lax.psum_scatter(lift(totals[5]), ("dp", "seq"), scatter_dimension=1, tiled=True),
        lax.psum_scatter(totals[6], ("dp", "seq"), scatter_dimension=1, tiled=True),
        lax.psum_scatter(lift(totals[7]), ("dp", "seq"), scatter_dimension=1, tiled=True),
        lax.psum_scatter(lift(totals[8]), ("dp", "seq"), scatter_dimension=1, tiled=True),
        lax.psum_scatter(lift(totals[9]), ("dp", "seq"), scatter_dimension=1, tiled=True),
        lax.psum_scatter(lift(totals[10]), ("dp", "seq"), scatter_dimension=1, tiled=True),
        lax.psum_scatter(lift(totals[11]), ("dp", "seq"), scatter_dimension=1, tiled=True),
    )
    hiddens = jnp.stack(
        [jnp.where(leading, results[index], results[index + 1]) for index in range(micro)]
    )[None]
    input_gradients = jnp.stack(
        [jnp.where(leading, back_results[index + 1], back_results[index]) for index in range(micro)]
    )[None]
    return (
        hiddens,
        input_gradients,
        reduced[0][None],
        reduced[1],
        reduced[2][None],
        reduced[3],
        reduced[4][None],
        reduced[5],
        reduced[6][None],
        reduced[7],
        reduced[8],
        reduced[9],
        reduced[10],
        reduced[11],
    )


def solution(mesh):
    return jax.shard_map(
        shards,
        mesh=mesh,
        in_specs=(
            P(None, "dp", "seq", None),
            P(None, "dp", None),
            P(None, "dp", "seq", None),
            P("section", None, None),
            P("section", None),
            P("section", None, None),
            P("section", None),
            P("section", None, None),
            P("section", None),
            P("section", None, None),
            P("section", None),
            P("section", None),
            P("section", None),
            P("section", None),
            P("section", None),
        ),
        out_specs=(
            P("section", None, "dp", "seq", None),
            P("section", None, "dp", "seq", None),
            P("section", None, ("dp", "seq")),
            P("section", ("dp", "seq")),
            P("section", None, ("dp", "seq")),
            P("section", ("dp", "seq")),
            P("section", None, ("dp", "seq")),
            P("section", ("dp", "seq")),
            P("section", None, ("dp", "seq")),
            P("section", ("dp", "seq")),
            P("section", ("dp", "seq")),
            P("section", ("dp", "seq")),
            P("section", ("dp", "seq")),
            P("section", ("dp", "seq")),
        ),
        check_vma=False,
    )
```

profile of v0, /device:TPU:0, one launch (start us, length us, event | category | flops | bytes accessed | tf_op | source)
XLA Modules:
  0.0 3620.2 jit_solution(6159310209676354836)
XLA Ops:
  66.7 20.4 all-gather.23.cloned.1.call-done
  87.1 14.2 fusion.396
  101.3 34.7 fusion.769
  149.8 16.2 fusion.772
  201.3 16.5 all-gather.27.cloned.1.call-done
  217.8 14.2 fusion.393
  232.1 34.7 fusion.773
  279.7 18.6 fusion.776
  330.3 20.3 all-gather.31.cloned.1.call-done
  350.6 14.2 fusion.388
  364.8 34.7 fusion.777
  412.5 18.6 fusion.780
  463.0 20.3 all-gather.35.cloned.1.call-done
  483.4 14.2 fusion.383
  497.6 34.7 fusion.781
  545.3 18.6 fusion.784
  598.3 20.1 all-gather.43.cloned.1.call-done
  618.4 14.2 fusion.371
  632.7 34.7 fusion.785
  682.4 18.7 fusion.757
  743.4 11.6 fusion.436
  754.9 17.5 multiply_reduce_fusion.4
  772.4 16.6 multiply_convert_fusion.4
  810.1 29.2 reduce-scatter.34.cloned.1.call-done
  967.5 13.5 fusion.341
  980.9 34.7 fusion.798
  1015.6 12.9 fusion.799
  1029.0 13.5 fusion.351
  1042.5 35.0 fusion.796
  1077.4 13.7 fusion.331
  1091.1 34.9 fusion.792
  1126.0 13.4 fusion.361
  1139.4 34.7 fusion.794
  1174.1 12.0 fusion.797
  1234.2 62.9 %fusion.737 = (f32[512]{0:T(512)}, f32[512,3072]{1,0:T(8,128)}, f32[512,3072]{1,0:T(8,128)}, f32[512]{0:T(512)S(1)}, f32[512,3072]{1,0:T(8,128)S(1)}, /*index=5*...) fusion(f32[3072]{0:T(1024)S(1)} %bitcast.1354, ...), kind=kOutput, calls=%fused_computation.1355 | convolution fusion | flops 2832726016 | bytes 81816576 | tf_op jit(solution)/shard_map/dot_general | solution.py:101
  1351.0 17.5 multiply_reduce_fusion.3
  1368.4 16.8 multiply_convert_fusion.3
  1402.2 35.0 reduce-scatter.36.cloned.1.call-done
  1507.0 17.4 multiply_reduce_fusion.2
  1524.4 16.6 multiply_convert_fusion.2
  1558.4 34.6 reduce-scatter.38.cloned.1.call-done
  1649.7 11.6 fusion.427
  1661.2 17.4 multiply_reduce_fusion.1
  1678.7 16.6 multiply_convert_fusion.1
  1712.3 35.0 reduce-scatter.40.cloned.1.call-done
  1813.5 17.7 multiply_reduce_fusion
  1831.2 16.6 multiply_convert_fusion
  1974.1 21.7 add_add_fusion.5
  2021.7 20.6 add_add_fusion.6
  2054.4 13.7 fusion.378
  2085.4 14.4 add_add_fusion.7
  2099.8 34.7 fusion.788
  2147.9 18.6 fusion.791
  2173.7 35.7 reduce-scatter.62.cloned.1.call-done
  2210.8 124.7 %reduce-scatter.54.cloned.1.call-done = f32[48,1]{1,0:T(8,128)} async-done(((f32[768,1]{1,0:T(8,128)}), f32[48,1]{1,0:T(8,128)}) %reduce-scatter.54.cloned.1.call-update) | async-done | bytes 208
  2336.8 127.2 %reduce-scatter.66.cloned.1.call-done = f32[192,1]{1,0:T(8,128)} async-done(((f32[3072,1]{1,0:T(8,128)}), f32[192,1]{1,0:T(8,128)}) %reduce-scatter.66.cloned.1.call-update) | async-done | bytes 784
  2465.6 126.7 %reduce-scatter.56.cloned.1.call-done = f32[192,1]{1,0:T(8,128)} async-done(((f32[3072,1]{1,0:T(8,128)}), f32[192,1]{1,0:T(8,128)}) %reduce-scatter.56.cloned.1.call-update) | async-done | bytes 784
  2598.6 118.8 %reduce-scatter.60.cloned.1.call-done = f32[48,1]{1,0:T(8,128)} async-done(((f32[768,1]{1,0:T(8,128)}), f32[48,1]{1,0:T(8,128)}) %reduce-scatter.60.cloned.1.call-update) | async-done | bytes 208
  2718.8 124.7 %reduce-scatter.58.cloned.1.call-done = f32[48,1]{1,0:T(8,128)} async-done(((f32[768,1]{1,0:T(8,128)}), f32[48,1]{1,0:T(8,128)}) %reduce-scatter.58.cloned.1.call-update) | async-done | bytes 208
  2844.8 126.0 %reduce-scatter.52.cloned.1.call-done = f32[144,1]{1,0:T(8,128)} async-done(((f32[2304,1]{1,0:T(8,128)}), f32[144,1]{1,0:T(8,128)}) %reduce-scatter.52.cloned.1.call-update) | async-done | bytes 592
  2972.4 130.8 %reduce-scatter.46.cloned.1.call-done = f32[768,48]{0,1:T(8,128)} async-done(((f32[768,768]{0,1:T(8,128)}), f32[768,48]{0,1:T(8,128)}) %reduce-scatter.46.cloned.1.call-update) | async-done | bytes 147472 | tf_op jit(solution)/shard_map/reduce_scatter | solution.py:359
  3103.2 177.9 %reduce-scatter.50.cloned.1.call-done = f32[3072,48]{0,1:T(8,128)} async-done(((f32[3072,768]{0,1:T(8,128)}), f32[3072,48]{0,1:T(8,128)}) %reduce-scatter.50.cloned.1.call-update) | async-done | bytes 589840 | tf_op jit(solution)/shard_map/reduce_scatter | solution.py:363
  3281.2 176.1 %reduce-scatter.48.cloned.1.call-done = f32[768,192]{0,1:T(8,128)} async-done(((f32[768,3072]{0,1:T(8,128)}), f32[768,192]{0,1:T(8,128)}) %reduce-scatter.48.cloned.1.call-update) | async-done | bytes 589840 | tf_op jit(solution)/shard_map/reduce_scatter | solution.py:361
  3457.2 156.0 %reduce-scatter.44.cloned.1.call-done = f32[768,144]{0,1:T(8,128)} async-done(((f32[768,2304]{0,1:T(8,128)}), f32[768,144]{0,1:T(8,128)}) %reduce-scatter.44.cloned.1.call-update) | async-done | bytes 442384 | tf_op jit(solution)/shard_map/reduce_scatter | solution.py:357
  (1510 shorter events, 1009.4 us)
Async XLA Ops:
  7.2 19.6 copy-start
  7.2 79.9 %all-gather.23.cloned.1.call-start = ((), (), s32[]{:S(2)}) async-start(), calls=%async_computation.18 | async-start | bytes 2359296 | tf_op jit(solution)/shard_map/all_gather | solution.py:79
  13.3 49.0 %copy-start.263 = (s32[1,1,1024]{2,1,0:T(1,128)}, s32[1,1,1024]{2,1,0:T(1,128)S(1)}, u32[]{:S(2)}) copy-start(s32[1,1,1024]{2,1,0:T(1,128)S(1)} %get-tuple-element.355) | copy-start | bytes 12292
  56.9 79.0 %all-gather.21.cloned.1.call-start = ((), (), s32[]{:S(2)}) async-start(), calls=%async_computation.17 | async-start | bytes 2359296 | tf_op jit(solution)/shard_map/all_gather | solution.py:80
  61.7 156.1 %all-gather.27.cloned.1.call-start = ((), (), s32[]{:S(2)}) async-start(), calls=%async_computation.20 | async-start | bytes 2359296 | tf_op jit(solution)/shard_map/all_gather | solution.py:79
  64.0 83.4 %copy-start.204 = (f32[12,64]{1,0:T(8,128)}, f32[12,64]{1,0:T(8,128)S(1)}, u32[]{:S(2)}) copy-start(f32[12,64]{1,0:T(8,128)S(1)} %mul.3346) | copy-start | bytes 9220
  64.7 83.0 %copy-start.402 = (f32[768]{0:T(1024)}, f32[768]{0:T(1024)S(1)}, u32[]{:S(2)}) copy-start(f32[768]{0:T(1024)S(1)} %reduce.311) | copy-start | bytes 9220
  65.4 662.8 %copy-start.102 = (f32[768]{0:T(1024)}, f32[768]{0:T(1024)S(1)}, u32[]{:S(2)}) copy-start(f32[768]{0:T(1024)S(1)} %reduce.312) | copy-start | bytes 9220
  169.6 3.6 collective-permute-start
  190.4 76.3 %all-gather.25.cloned.1.call-start = ((), (), s32[]{:S(2)}) async-start(), calls=%async_computation.19 | async-start | bytes 2359296 | tf_op jit(solution)/shard_map/all_gather | solution.py:80
  200.9 149.7 %all-gather.31.cloned.1.call-start = ((), (), s32[]{:S(2)}) async-start(), calls=%async_computation.22 | async-start | bytes 2359296 | tf_op jit(solution)/shard_map/all_gather | solution.py:79
  279.7 19.5 slice-start.18
  279.7 19.5 slice-start.19
  302.1 3.6 collective-permute-start.1
  323.2 76.3 %all-gather.29.cloned.1.call-start = ((), (), s32[]{:S(2)}) async-start(), calls=%async_computation.21 | async-start | bytes 2359296 | tf_op jit(solution)/shard_map/all_gather | solution.py:80
  329.8 153.6 %all-gather.35.cloned.1.call-start = ((), (), s32[]{:S(2)}) async-start(), calls=%async_computation.24 | async-start | bytes 2359296 | tf_op jit(solution)/shard_map/all_gather | solution.py:79
  412.4 19.5 slice-start.20
  412.5 19.5 slice-start.21
  434.8 3.6 collective-permute-start.2
  456.0 76.3 %all-gather.33.cloned.1.call-start = ((), (), s32[]{:S(2)}) async-start(), calls=%async_computation.23 | async-start | bytes 2359296 | tf_op jit(solution)/shard_map/all_gather | solution.py:80
  462.6 155.9 %all-gather.43.cloned.1.call-start = ((), (), s32[]{:S(2)}) async-start(), calls=%async_computation.28 | async-start | bytes 2359296 | tf_op jit(solution)/shard_map/all_gather | solution.py:79
  545.2 19.5 slice-start.22
  567.6 3.8 collective-permute-start.3
  591.0 76.4 %all-gather.41.cloned.1.call-start = ((), (), s32[]{:S(2)}) async-start(), calls=%async_computation.27 | async-start | bytes 2359296 | tf_op jit(solution)/shard_map/all_gather | solution.py:80
  598.2 241.1 %reduce-scatter.34.cloned.1.call-start = ((), (), s32[]{:S(2)}) async-start(), calls=%async_computation.29 | async-start | bytes 4718592 | tf_op jit(solution)/shard_map/reduce_scatter | solution.py:253
  679.5 21.6 copy-start.162
  682.0 46.3 %copy-start.49 = (f32[1,512,768]{2,1,0:T(8,128)}, f32[1,512,768]{2,1,0:T(8,128)S(1)}, u32[]{:S(2)}) copy-start(f32[1,512,768]{2,1,0:T(8,128)S(1)} %get-tuple-element.465) | copy-start | bytes 4718596
  682.0 46.3 %copy-start.238 = (f32[512]{0:T(512)}, f32[512]{0:T(512)S(1)}, u32[]{:S(2)}) copy-start(f32[512]{0:T(512)S(1)} %broadcast_multiply_fusion.22) | copy-start | bytes 6148
  682.4 45.9 %copy-start.249 = (f32[512]{0:T(512)}, f32[512]{0:T(512)S(1)}, u32[]{:S(2)}) copy-start(f32[512]{0:T(512)S(1)} %fusion.634) | copy-start | bytes 6148
  730.0 216.7 %copy-start.280 = (f32[512]{0:T(512)}, f32[512]{0:T(512)S(1)}, u32[]{:S(2)}) copy-start(f32[512]{0:T(512)S(1)} %negate_multiply_fusion.28) | copy-start | bytes 6148
  795.8 171.7 %all-gather.55.cloned.1.call-start = ((), (), s32[]{:S(2)}) async-start(), calls=%async_computation.37 | async-start | bytes 2359296 | tf_op jit(solution)/shard_map/all_gather | solution.py:79
  796.5 96.4 %copy-start.296 = (f32[512]{0:T(512)}, f32[512]{0:T(512)S(1)}, u32[]{:S(2)}) copy-start(f32[512]{0:T(512)S(1)} %broadcast_multiply_fusion.12) | copy-start | bytes 6148
  867.3 148.3 %all-gather.53.cloned.1.call-start = ((), (), s32[]{:S(2)}) async-start(), calls=%async_computation.36 | async-start | bytes 2359296 | tf_op jit(solution)/shard_map/all_gather | solution.py:80
  873.2 155.8 %all-gather.51.cloned.1.call-start = ((), (), s32[]{:S(2)}) async-start(), calls=%async_computation.34 | async-start | bytes 2359296 | tf_op jit(solution)/shard_map/all_gather | solution.py:79
  892.7 184.8 %all-gather.59.cloned.1.call-start = ((), (), s32[]{:S(2)}) async-start(), calls=%async_computation.40 | async-start | bytes 2359296 | tf_op jit(solution)/shard_map/all_gather | solution.py:79
  913.1 212.8 %all-gather.47.cloned.1.call-start = ((), (), s32[]{:S(2)}) async-start(), calls=%async_computation.31 | async-start | bytes 2359296 | tf_op jit(solution)/shard_map/all_gather | solution.py:79
  936.5 237.7 %all-gather.49.cloned.1.call-start = ((), (), s32[]{:S(2)}) async-start(), calls=%async_computation.33 | async-start | bytes 2359296 | tf_op jit(solution)/shard_map/all_gather | solution.py:80
  941.2 244.9 %all-gather.57.cloned.1.call-start = ((), (), s32[]{:S(2)}) async-start(), calls=%async_computation.39 | async-start | bytes 2359296 | tf_op jit(solution)/shard_map/all_gather | solution.py:80
  946.0 253.8 %all-gather.45.cloned.1.call-start = ((), (), s32[]{:S(2)}) async-start(), calls=%async_computation.30 | async-start | bytes 2359296 | tf_op jit(solution)/shard_map/all_gather | solution.py:80
  950.1 13.9 collective-permute-start.4
  963.5 473.7 %reduce-scatter.36.cloned.1.call-start = ((), (), s32[]{:S(2)}) async-start(), calls=%async_computation.32 | async-start | bytes 4718592 | tf_op jit(solution)/shard_map/reduce_scatter | solution.py:253
  1234.1 62.9 %copy-start.181 = (f32[1,3072]{1,0:T(1,128)S(1)}, f32[1,3072]{1,0:T(1,128)}, u32[]{:S(2)}) copy-start(f32[1,3072]{1,0:T(1,128)} %param.29) | copy-start | bytes 36868
  1234.2 62.9 %copy-start.183 = (bf16[1,512,768]{2,1,0:T(8,128)(2,1)S(1)}, bf16[1,512,768]{2,1,0:T(8,128)(2,1)}, u32[]{:S(2)}) copy-start(bf16[1,512,768]{2,1,0:T(8,128)(2,1)} %get-tuple-element.133) | copy-start | bytes 2359300
  1392.0 201.1 %reduce-scatter.38.cloned.1.call-start = ((), (), s32[]{:S(2)}) async-start(), calls=%async_computation.35 | async-start | bytes 4718592 | tf_op jit(solution)/shard_map/reduce_scatter | solution.py:253
  1452.9 5.0 collective-permute-start.5
  1547.8 199.4 %reduce-scatter.40.cloned.1.call-start = ((), (), s32[]{:S(2)}) async-start(), calls=%async_computation.38 | async-start | bytes 4718592 | tf_op jit(solution)/shard_map/reduce_scatter | solution.py:253
  1606.9 5.1 collective-permute-start.6
  1702.1 216.9 %reduce-scatter.42.cloned.1.call-start = ((), (), s32[]{:S(2)}) async-start(), calls=%async_computation.41 | async-start | bytes 4718592 | tf_op jit(solution)/shard_map/reduce_scatter | solution.py:253
  1761.3 5.0 collective-permute-start.7
  1854.6 199.8 %all-gather.39.cloned.1.call-start = ((), (), s32[]{:S(2)}) async-start(), calls=%async_computation.26 | async-start | bytes 2359296 | tf_op jit(solution)/shard_map/all_gather | solution.py:79
  1873.3 261.3 %all-gather.37.cloned.1.call-start = ((), (), s32[]{:S(2)}) async-start(), calls=%async_computation.25 | async-start | bytes 2359296 | tf_op jit(solution)/shard_map/all_gather | solution.py:80
  1881.7 290.7 %reduce-scatter.64.cloned.1.call-start = ((), (), s32[]{:S(2)}) async-start(), calls=%async_computation.52 | async-start | bytes 417792
  1897.0 312.5 %reduce-scatter.62.cloned.1.call-start = ((), (), s32[]{:S(2)}) async-start(), calls=%async_computation.51 | async-start | bytes 417792
  1898.7 436.8 %reduce-scatter.54.cloned.1.call-start = ((), (), s32[]{:S(2)}) async-start(), calls=%async_computation.47 | async-start | bytes 417792
  1900.5 563.6 %reduce-scatter.66.cloned.1.call-start = ((), (), s32[]{:S(2)}) async-start(), calls=%async_computation.53 | async-start | bytes 1671168
  1904.3 688.0 %reduce-scatter.56.cloned.1.call-start = ((), (), s32[]{:S(2)}) async-start(), calls=%async_computation.48 | async-start | bytes 1671168
  1908.1 809.4 %reduce-scatter.60.cloned.1.call-start = ((), (), s32[]{:S(2)}) async-start(), calls=%async_computation.50 | async-start | bytes 417792
  1928.7 914.8 %reduce-scatter.58.cloned.1.call-start = ((), (), s32[]{:S(2)}) async-start(), calls=%async_computation.49 | async-start | bytes 417792
  1933.5 1037.3 %reduce-scatter.52.cloned.1.call-start = ((), (), s32[]{:S(2)}) async-start(), calls=%async_computation.46 | async-start | bytes 1253376
  1937.8 1165.4 %reduce-scatter.46.cloned.1.call-start = ((), (), s32[]{:S(2)}) async-start(), calls=%async_computation.43 | async-start | bytes 2506752 | tf_op jit(solution)/shard_map/reduce_scatter | solution.py:359
  1944.7 1336.5 %reduce-scatter.50.cloned.1.call-start = ((), (), s32[]{:S(2)}) async-start(), calls=%async_computation.45 | async-start | bytes 10027008 | tf_op jit(solution)/shard_map/reduce_scatter | solution.py:363
  1995.9 1461.3 %reduce-scatter.48.cloned.1.call-start = ((), (), s32[]{:S(2)}) async-start(), calls=%async_computation.44 | async-start | bytes 10027008 | tf_op jit(solution)/shard_map/reduce_scatter | solution.py:361
  2042.4 1570.8 %reduce-scatter.44.cloned.1.call-start = ((), (), s32[]{:S(2)}) async-start(), calls=%async_computation.42 | async-start | bytes 7520256 | tf_op jit(solution)/shard_map/reduce_scatter | solution.py:357
  2147.8 19.5 slice-start.24
  (437 other events, 2541.9 us)
Sparse Core Ops, SparseCore 0:
  57.1 29.9 all-gather.22
  89.2 27.1 all-gather.20
  190.5 27.2 all-gather.26
  219.8 27.1 all-gather.24
  323.3 27.2 all-gather.30
  352.6 27.1 all-gather.28
  456.1 27.2 all-gather.34
  485.5 27.1 all-gather.32
  591.1 27.2 all-gather.42
  620.4 27.1 all-gather.40
  795.9 43.3 reduce-scatter.33
  867.4 27.1 all-gather.54
  896.2 27.1 all-gather.52
  925.0 27.2 all-gather.50
  953.7 27.1 all-gather.58
  983.0 27.1 all-gather.46
  1011.7 27.1 all-gather.48
  1040.4 27.1 all-gather.56
  1069.8 27.1 all-gather.44
  1392.1 45.0 reduce-scatter.35
  1547.9 45.0 reduce-scatter.37
  1702.2 45.0 reduce-scatter.39
  1854.8 44.9 reduce-scatter.41
  1901.3 27.2 all-gather.38
  1930.1 27.2 all-gather.36
  1962.6 121.6 reduce-scatter.63
  2088.8 120.6 reduce-scatter.61
  2214.8 120.6 reduce-scatter.53
  2340.3 123.6 reduce-scatter.65
  2468.7 123.5 reduce-scatter.55
  2596.9 120.4 reduce-scatter.59
  2722.8 120.6 reduce-scatter.57
  2848.1 122.6 reduce-scatter.51
  2976.3 126.8 reduce-scatter.45
  3110.4 170.6 reduce-scatter.49
  3287.3 169.9 reduce-scatter.47
  3463.8 149.2 reduce-scatter.43
where the time goes:
time: 3630 us; the launch traced here: 3620 us
  waiting for transfers between devices  1660 us (46%)
  matrix products  941 us (26%)
  other arithmetic  744 us (20%)
  local copies, waits for them, and re-layouts  233 us (6%)
    unnamed x45, waiting for transfers between devices  785 us
    sub x10, other arithmetic, layer_forward(): raised = jnp.exp(scores - peak)  347 us
    dot_general x10, matrix products, layer_forward(): jnp.dot(normed_two, up_weight, preferred_element_type=jnp.float32) + up_bias  183 us
    reduce_scatter x1, waiting for transfers between devices, shards(): lax.psum_scatter(totals[6], ('dp', 'seq'), scatter_dimension=1, tiled=True)  178 us
    reduce_scatter x1, waiting for transfers between devices, shards(): lax.psum_scatter(totals[4], ('dp', 'seq'), scatter_dimension=1, tiled=True)  176 us
    reduce_scatter x1, waiting for transfers between devices, shards(): lax.psum_scatter(totals[0], ('dp', 'seq'), scatter_dimension=1, tiled=True)  156 us
    dot_general x10, matrix products, layer_forward(): jnp.einsum('rqhd,rkhd->rhqk', query, keys_all, preferred_element_type=jnp...  139 us
    reduce_scatter x5, waiting for transfers between devices, attend_backward(): lax.psum_scatter(jnp.concatenate([key_part, value_part], axis=-1).astype(...  134 us
  transfers between devices with their start and end apart: 45, of which 24 were waited for; matrix products, arithmetic and copies ran while one was open for 27% of the time, Pallas kernels for 0%

commit v1 on v0

--- a/solution.py
+++ b/solution.py
@@ -1,6 +1,11 @@
+import functools
+import math
+
 import jax
 import jax.numpy as jnp
 from jax import lax
+from jax.experimental import pallas as pl
+from jax.experimental.pallas import tpu as pltpu
 from jax.sharding import PartitionSpec as P
 
 HEAD_DIM = 64
@@ -391,9 +396,723 @@
     )
 
 
+F32 = jnp.float32
+BF16 = jnp.bfloat16
+ANY = pl.BlockSpec(memory_space=pl.ANY)
+SMEM = pl.BlockSpec(memory_space=pltpu.SMEM)
+VLIM = 60 * 1024 * 1024
+
+
+def lane_iota(shape):
+    return lax.broadcasted_iota(jnp.int32, shape, len(shape) - 1)
+
+
+def nn(a, b):
+    return lax.dot_general(a, b, (((1,), (0,)), ((), ())), preferred_element_type=F32)
+
+
+def nt(a, b):
+    return lax.dot_general(a, b, (((1,), (1,)), ((), ())), preferred_element_type=F32)
+
+
+def tn(a, b):
+    return lax.dot_general(a, b, (((0,), (0,)), ((), ())), preferred_element_type=F32)
+
+
+def normalize(value):
+    centered = value - jnp.mean(value, axis=-1, keepdims=True)
+    scale = lax.rsqrt(jnp.mean(centered * centered, axis=-1, keepdims=True) + EPSILON)
+    return centered * scale, scale
+
+
+def norm_back(slope, unit, scale):
+    return scale * (
+        slope
+        - jnp.mean(slope, axis=-1, keepdims=True)
+        - unit * jnp.mean(slope * unit, axis=-1, keepdims=True)
+    )
+
+
+def fold(value):
+    rows, columns = value.shape
+    return jnp.sum(value.reshape(rows // 8, 8, columns), axis=0)
+
+
+def split3(value):
+    high = value.astype(BF16)
+    rest = value - high.astype(F32)
+    middle = rest.astype(BF16)
+    low = (rest - middle.astype(F32)).astype(BF16)
+    return high, middle, low
+
+
+def fetch_weights(layer, sec_ref, pairs, sem):
+    @pl.when(pl.program_id(0) == 0)
+    def _():
+        @pl.when(sec_ref[0] == layer)
+        def _():
+            for index, (own, other, here) in enumerate(pairs):
+                pltpu.make_async_copy(own, here, sem.at[index]).start()
+
+        @pl.when(sec_ref[0] != layer)
+        def _():
+            for index, (own, other, here) in enumerate(pairs):
+                pltpu.make_async_copy(other, here, sem.at[index]).start()
+
+        for index, (own, other, here) in enumerate(pairs):
+            pltpu.make_async_copy(own, here, sem.at[index]).wait()
+
+
+def qkv_kernel(layer, sec_ref, x_ref, gain_ref, own_ref, other_ref, bias_ref, cos_ref, sin_ref,
+               lab_ref, n_ref, q_ref, k_ref, v_ref, w_ref, sem):
+    fetch_weights(layer, sec_ref, [(own_ref, other_ref, w_ref)], sem)
+    width = x_ref.shape[-1]
+    unit, scale = normalize(x_ref[...].astype(F32))
+    normed = (unit * gain_ref[...]).astype(BF16)
+    n_ref[...] = normed
+    joint = nn(normed, w_ref[...]) + bias_ref[...]
+    cosine, sine = cos_ref[...], sin_ref[...]
+    lane = lane_iota(cosine.shape)
+    first = lane % HEAD_DIM < HEAD_DIM // 2
+    head = lane < HEAD_DIM
+    labels = lab_ref[...]
+    document = lane - HEAD_DIM
+    known = (document >= 0) & (document < 5)
+    q_feat = jnp.where(known & (document != labels), MASKED, 0.0)
+    ones = (document >= 5) & (document < 8)
+    k_feat = jnp.where((known & (document == labels)) | ones, 1.0, 0.0)
+    v_feat = jnp.where((document >= 0) & (document < 3), 1.0, 0.0)
+    for pair in range(width // 128):
+        for which, (out, feat) in enumerate(((q_ref, q_feat), (k_ref, k_feat), (v_ref, v_feat))):
+            begin = which * width + pair * 128
+            part = joint[:, begin:begin + 128]
+            if which < 2:
+                turned = jnp.where(first, pltpu.roll(part, 96, 1), pltpu.roll(part, 32, 1))
+                part = part * cosine + turned * sine
+            part = part.astype(BF16).astype(F32)
+            if which == 0:
+                part = part * HEAD_DIM ** -0.5
+            out[2 * pair] = jnp.where(head, part, feat).astype(BF16)
+            out[2 * pair + 1] = jnp.where(head, pltpu.roll(part, 64, 1), feat).astype(BF16)
+
+
+def qkv(layer, sec, x, gain, own, other, bias, cosine, sine, labels, tb=256):
+    rows, width = x.shape
+    heads = width // HEAD_DIM
+    const = lambda shape: pl.BlockSpec(shape, lambda i: (0,) * len(shape))
+    tok = lambda n: pl.BlockSpec((tb, n), lambda i: (i, 0))
+    hd = pl.BlockSpec((heads, tb, 128), lambda i: (0, i, 0))
+    return pl.pallas_call(
+        functools.partial(qkv_kernel, layer),
+        grid=(rows // tb,),
+        in_specs=[SMEM, tok(width), const((1, width)), ANY, ANY, const((1, 3 * width)), tok(128), tok(128), tok(1)],
+        out_specs=[tok(width), hd, hd, hd],
+        out_shape=[jax.ShapeDtypeStruct((rows, width), BF16)] + [jax.ShapeDtypeStruct((heads, rows, 128), BF16)] * 3,
+        scratch_shapes=[pltpu.VMEM(own.shape, BF16), pltpu.SemaphoreType.DMA((1,))],
+        compiler_params=pltpu.CompilerParams(vmem_limit_bytes=VLIM),
+        cost_estimate=pl.CostEstimate(flops=2 * rows * width * 3 * width, bytes_accessed=16 * 1024 * 1024, transcendentals=0),
+        name="joint_projection",
+    )(sec, x, gain, own, other, bias, cosine, sine, labels)
+
+
+def attend_kernel(qb, q_ref, k_ref, v_ref, o_ref, ql_ref):
+    rows = q_ref.shape[1]
+    lane = lane_iota((qb, 128))
+    for block in range(rows // qb):
+        at = pl.ds(block * qb, qb)
+        done = []
+        for head in range(2):
+            query = q_ref[head, at, :]
+            scores = nt(query, k_ref[head])
+            peak = jnp.max(scores, axis=-1, keepdims=True)
+            raised = jnp.exp(scores - peak).astype(BF16)
+            sums = nn(raised, v_ref[head])
+            total = sums[:, HEAD_DIM:HEAD_DIM + 1]
+            done.append(sums / total)
+            high, middle, low = split3(-(peak + jnp.log(total)))
+            feat = jnp.where(lane == 69, high.astype(F32), jnp.where(lane == 70, middle.astype(F32), low.astype(F32)))
+            inside = (lane >= 69) & (lane < 72)
+            ql_ref[head, at, :] = jnp.where(inside, feat, query.astype(F32)).astype(BF16)
+        o_ref[at, :] = jnp.where(lane < HEAD_DIM, done[0], pltpu.roll(done[1], 64, 1))
+
+
+def attend(q, k, v, qb=256):
+    heads, rows, _ = q.shape
+    hd = pl.BlockSpec((2, rows, 128), lambda i: (i, 0, 0))
+    return pl.pallas_call(
+        functools.partial(attend_kernel, qb),
+        grid=(heads // 2,),
+        in_specs=[hd, hd, hd],
+        out_specs=[pl.BlockSpec((rows, 128), lambda i: (0, i)), hd],
+        out_shape=[jax.ShapeDtypeStruct((rows, heads * HEAD_DIM), F32), jax.ShapeDtypeStruct(q.shape, BF16)],
+        compiler_params=pltpu.CompilerParams(vmem_limit_bytes=VLIM),
+        cost_estimate=pl.CostEstimate(flops=16 * heads * rows * rows * HEAD_DIM, bytes_accessed=16 * 1024 * 1024, transcendentals=0),
+        name="attention_forward",
+    )(q, k, v)
+
+
+def feed_kernel(layer, sec_ref, at_ref, x_ref, ig_ref, ob_ref, sg_ref, ub_ref, hg_ref, db_ref,
+                wo0, wo1, wu0, wu1, wd0, wd1,
+                out_ref, mixed_ref, hid_ref, gp_ref, st_ref, wo, wu, wd, sem):
+    fetch_weights(layer, sec_ref, [(wo0, wo1, wo), (wu0, wu1, wu), (wd0, wd1, wd)], sem)
+    unit, _ = normalize(at_ref[...])
+    inner = (unit * ig_ref[...]).astype(BF16)
+    mixed = x_ref[...].astype(F32) + nn(inner, wo[...]) + ob_ref[...]
+    mixed_ref[...] = mixed
+    unit, _ = normalize(mixed)
+    normed = (unit * sg_ref[...]).astype(BF16)
+    before = nn(normed, wu[...]) + ub_ref[...]
+    share = 0.5 + 0.5 * lax.erf(before * 0.5 ** 0.5)
+    bell = jnp.exp(before * before * -0.5) * (1.0 / math.sqrt(2.0 * math.pi))
+    gp_ref[...] = (share + before * bell).astype(BF16)
+    unit, scale = normalize(before * share)
+    hidden = (unit * hg_ref[...]).astype(BF16)
+    hid_ref[...] = hidden
+    st_ref[...] = jnp.broadcast_to(scale, st_ref.shape)
+    out_ref[...] = (mixed + nn(hidden, wd[...]) + db_ref[...]).astype(BF16)
+
+
+def feed(layer, sec, attended, x, ig, ob, sg, ub, hg, db, wo, wu, wd, tb=256):
+    rows, width = x.shape
+    wide = ub.shape[-1]
+    const = lambda n: pl.BlockSpec((1, n), lambda i: (0, 0))
+    tok = lambda n: pl.BlockSpec((tb, n), lambda i: (i, 0))
+    S = jax.ShapeDtypeStruct
+    return pl.pallas_call(
+        functools.partial(feed_kernel, layer),
+        grid=(rows // tb,),
+        in_specs=[SMEM, tok(width), tok(width), const(width), const(width), const(width), const(wide), const(wide), const(width)] + [ANY] * 6,
+        out_specs=[tok(width), tok(width), tok(wide), tok(wide), tok(128)],
+        out_shape=[S((rows, width), BF16), S((rows, width), F32), S((rows, wide), BF16), S((rows, wide), BF16), S((rows, 128), F32)],
+        scratch_shapes=[pltpu.VMEM(wo[0].shape, BF16), pltpu.VMEM(wu[0].shape, BF16), pltpu.VMEM(wd[0].shape, BF16), pltpu.SemaphoreType.DMA((3,))],
+        compiler_params=pltpu.CompilerParams(vmem_limit_bytes=VLIM),
+        cost_estimate=pl.CostEstimate(flops=2 * rows * width * (2 * wide + width), bytes_accessed=40 * 1024 * 1024, transcendentals=0),
+        name="feed_forward",
+    )(sec, attended, x, ig, ob, sg, ub, hg, db, *wo, *wu, *wd)
+
+
+def feed_back_kernel(layer, sec_ref, c_ref, hid_ref, gp_ref, st_ref, mixed_ref, at_ref,
+                     ig_ref, sg_ref, hg_ref, wo0, wo1, wu0, wu1, wd0, wd1,
+                     cb_ref, cm_ref, cl_ref, ch_ref, n2_ref, in_ref, wide_ref, thin_ref,
+                     wo, wu, wd, wide_acc, thin_acc, sem):
+    step = pl.program_id(0)
+
+    @pl.when(step == 0)
+    def _():
+        wide_acc[...] = jnp.zeros_like(wide_acc)
+        thin_acc[...] = jnp.zeros_like(thin_acc)
+
+    fetch_weights(layer, sec_ref, [(wo0, wo1, wo), (wu0, wu1, wu), (wd0, wd1, wd)], sem)
+    low = c_ref[...]
+    outer = low.astype(F32)
+    thin_acc[0] += fold(outer)
+    slope = nt(low, wd[...])
+    hidden = hid_ref[...].astype(F32)
+    gain = hg_ref[...]
+    moved = slope * hidden
+    wide_acc[0] += fold(moved)
+    mean_moved = jnp.mean(moved, axis=-1, keepdims=True)
+    slope = slope * gain
+    mean_slope = jnp.mean(slope, axis=-1, keepdims=True)
+    scale = st_ref[:, 0:1]
+    slope = (slope - mean_slope - hidden * (1.0 / gain) * mean_moved) * scale
+    before_low = (slope * gp_ref[...].astype(F32)).astype(BF16)
+    cb_ref[...] = before_low
+    wide_acc[1] += fold(before_low.astype(F32))
+    slope = nt(before_low, wu[...])
+    unit, scale = normalize(mixed_ref[...])
+    n2_ref[...] = (unit * sg_ref[...]).astype(BF16)
+    thin_acc[1] += fold(slope * unit)
+    mixed = outer + norm_back(slope * sg_ref[...], unit, scale)
+    cm_ref[...] = mixed
+    mixed_low = mixed.astype(BF16)
+    cl_ref[...] = mixed_low
+    thin_acc[2] += fold(mixed_low.astype(F32))
+    slope = nt(mixed_low, wo[...])
+    unit, scale = normalize(at_ref[...])
+    in_ref[...] = (unit * ig_ref[...]).astype(BF16)
+    thin_acc[3] += fold(slope * unit)
+    ch_ref[...] = norm_back(slope * ig_ref[...], unit, scale).astype(BF16)
+
+    @pl.when(step == pl.num_programs(0) - 1)
+    def _():
+        inverse = 1.0 / gain
+        wide_ref[0:1, :] = jnp.sum(wide_acc[0], axis=0, keepdims=True) * inverse
+        wide_ref[1:2, :] = jnp.sum(wide_acc[1], axis=0, keepdims=True)
+        for index in range(4):
+            thin_ref[index:index + 1, :] = jnp.sum(thin_acc[index], axis=0, keepdims=True)
+
+
+def feed_back(layer, sec, c, hidden, gp, st, mixed, attended, ig, sg, hg, wo, wu, wd, tb=256):
+    rows, width = c.shape
+    wide = hg.shape[-1]
+    const = lambda n, m=1: pl.BlockSpec((m, n), lambda i: (0, 0))
+    tok = lambda n: pl.BlockSpec((tb, n), lambda i: (i, 0))
+    S = jax.ShapeDtypeStruct
+    return pl.pallas_call(
+        functools.partial(feed_back_kernel, layer),
+        grid=(rows // tb,),
+        in_specs=[SMEM, tok(width), tok(wide), tok(wide), tok(128), tok(width), tok(width), const(width), const(width), const(wide)] + [ANY] * 6,
+        out_specs=[tok(wide), tok(width), tok(width), tok(width), tok(width), tok(width), const(wide, 2), const(width, 4)],
+        out_shape=[S((rows, wide), BF16), S((rows, width), F32), S((rows, width), BF16), S((rows, width), BF16), S((rows, width), BF16), S((rows, width), BF16), S((2, wide), F32), S((4, width), F32)],
+        scratch_shapes=[pltpu.VMEM(wo[0].shape, BF16), pltpu.VMEM(wu[0].shape, BF16), pltpu.VMEM(wd[0].shape, BF16),
+                        pltpu.VMEM((2, 8, wide), F32), pltpu.VMEM((4, 8, width), F32), pltpu.SemaphoreType.DMA((3,))],
+        compiler_params=pltpu.CompilerParams(vmem_limit_bytes=VLIM),
+        cost_estimate=pl.CostEstimate(flops=2 * rows * width * (2 * wide + width), bytes_accessed=50 * 1024 * 1024, transcendentals=0),
+        name="feed_backward",
+    )(sec, c, hidden, gp, st, mixed, attended, ig, sg, hg, *wo, *wu, *wd)
+
+
+def attend_back_kernel(qb, q_ref, k_ref, v_ref, ch_ref, at_ref, cos_ref, sin_ref, cj_ref, kt, vt, qs):
+    rows = q_ref.shape[1]
+    lane = lane_iota((rows, 128))
+    is_head = lane < HEAD_DIM
+    slopes = ch_ref[...].astype(F32)
+    product = slopes * at_ref[...]
+    for head in range(2):
+        mine = is_head if head == 0 else jnp.logical_not(is_head)
+        weighted = jnp.sum(jnp.where(mine, product, 0.0), axis=-1, keepdims=True)
+        high, middle, low = split3(-weighted)
+        feat = jnp.where(lane == 64, high.astype(F32), jnp.where(lane == 65, middle.astype(F32), jnp.where(lane == 66, low.astype(F32), 0.0)))
+        local = slopes if head == 0 else pltpu.roll(slopes, 64, 1)
+        c_aug = jnp.where(is_head, local, feat).astype(BF16)
+        keys, values = k_ref[head], v_ref[head]
+        for block in range(rows // qb):
+            at = pl.ds(block * qb, qb)
+            query = q_ref[head, at, :]
+            incoming = c_aug[block * qb:(block + 1) * qb, :]
+            shares = jnp.exp(nt(query, keys))
+            slope = (shares * nt(incoming, values)).astype(BF16)
+            qs[head, at, :] = nn(slope, keys)
+            key_part = tn(query, slope)[:HEAD_DIM]
+            value_part = tn(incoming, shares.astype(BF16))[:HEAD_DIM]
+            rng = pl.ds(head * HEAD_DIM, HEAD_DIM)
+            if block == 0:
+                kt[rng, :] = key_part
+                vt[rng, :] = value_part
+            else:
+                kt[rng, :] += key_part
+                vt[rng, :] += value_part
+    cosine, sine = cos_ref[...], sin_ref[...]
+    first = lane % HEAD_DIM < HEAD_DIM // 2
+    def back(part):
+        turned = jnp.where(first, pltpu.roll(part, 96, 1), pltpu.roll(part, 32, 1))
+        return (part * cosine - turned * sine).astype(BF16)
+    cj_ref[0] = back(jnp.where(is_head, qs[0], pltpu.roll(qs[1], 64, 1)) * HEAD_DIM ** -0.5)
+    cj_ref[1] = back(kt[...].T)
+    cj_ref[2] = vt[...].T.astype(BF16)
+
+
+def attend_back(q, k, v, ch, attended, cosine, sine, qb=256):
+    heads, rows, _ = q.shape
+    width = heads * HEAD_DIM
+    hd = pl.BlockSpec((2, rows, 128), lambda i: (i, 0, 0))
+    col = pl.BlockSpec((rows, 128), lambda i: (0, i))
+    con = pl.BlockSpec((rows, 128), lambda i: (0, 0))
+    return pl.pallas_call(
+        functools.partial(attend_back_kernel, qb),
+        grid=(heads // 2,),
+        in_specs=[hd, hd, hd, col, col, con, con],
+        out_specs=pl.BlockSpec((3, rows, 128), lambda i: (0, 0, i)),
+        out_shape=jax.ShapeDtypeStruct((3, rows, width), BF16),
+        scratch_shapes=[pltpu.VMEM((128, rows), F32), pltpu.VMEM((128, rows), F32), pltpu.VMEM((2, rows, 128), F32)],
+        compiler_params=pltpu.CompilerParams(vmem_limit_bytes=VLIM),
+        cost_estimate=pl.CostEstimate(flops=40 * heads * rows * rows * HEAD_DIM, bytes_accessed=20 * 1024 * 1024, transcendentals=0),
+        name="attention_backward",
+    )(q, k, v, ch, attended, cosine, sine)
+
+
+def qkv_back_kernel(layer, sec_ref, cj_ref, x_ref, cm_ref, gain_ref, own_ref, other_ref,
+                    ci_ref, small_ref, w_ref, acc, sem):
+    step = pl.program_id(0)
+    fetch_weights(layer, sec_ref, [(own_ref, other_ref, w_ref)], sem)
+
+    @pl.when(step == 0)
+    def _():
+        acc[...] = jnp.zeros_like(acc)
+
+    width = x_ref.shape[-1]
+    slope = nt(cj_ref[0], w_ref[:, 0:width])
+    for which in range(1, 3):
+        slope = slope + nt(cj_ref[which], w_ref[:, which * width:(which + 1) * width])
+    unit, scale = normalize(x_ref[...].astype(F32))
+    acc[0] += fold(slope * unit)
+    for which in range(3):
+        acc[which + 1] += fold(cj_ref[which].astype(F32))
+    ci_ref[...] = (cm_ref[...] + norm_back(slope * gain_ref[...], unit, scale)).astype(BF16)
+
+    @pl.when(step == pl.num_programs(0) - 1)
+    def _():
+        for index in range(4):
+            small_ref[index:index + 1, :] = jnp.sum(acc[index], axis=0, keepdims=True)
+
+
+def qkv_back(layer, sec, cj, x, cm, gain, own, other, tb=256):
+    rows, width = x.shape
+    const = lambda n, m=1: pl.BlockSpec((m, n), lambda i: (0, 0))
+    tok = lambda n: pl.BlockSpec((tb, n), lambda i: (i, 0))
+    S = jax.ShapeDtypeStruct
+    return pl.pallas_call(
+        functools.partial(qkv_back_kernel, layer),
+        grid=(rows // tb,),
+        in_specs=[SMEM, pl.BlockSpec((3, tb, width), lambda i: (0, i, 0)), tok(width), tok(width), const(width), ANY, ANY],
+        out_specs=[tok(width), const(width, 4)],
+        out_shape=[S((rows, width), BF16), S((4, width), F32)],
+        scratch_shapes=[pltpu.VMEM(own.shape, BF16), pltpu.VMEM((4, 8, width), F32), pltpu.SemaphoreType.DMA((1,))],
+        compiler_params=pltpu.CompilerParams(vmem_limit_bytes=VLIM),
+        cost_estimate=pl.CostEstimate(flops=2 * rows * width * 3 * width, bytes_accessed=16 * 1024 * 1024, transcendentals=0),
+        name="joint_backward",
+    )(sec, cj, x, cm, gain, own, other)
+
+
+def tables(labels, places):
+    half = HEAD_DIM // 2
+    lane = jnp.arange(128)
+    rate = 1.0 / 10000.0 ** (jnp.arange(half, dtype=F32) * 2.0 / HEAD_DIM)
+    angle = places.astype(F32)[:, None] * jnp.tile(rate, 4)[None, :]
+    sign = jnp.where(lane % HEAD_DIM < half, -1.0, 1.0).astype(F32)
+    return jnp.cos(angle), jnp.sin(angle) * sign
+
+
+SIZES = ("joint_bias", "output_bias", "up_bias", "down_bias", "first_gain", "inner_gain", "second_gain", "hidden_gain")
+
+
+def feed_grads_kernel(sec_ref, order_ref, cb_ref, hid_ref, c_ref, n2_ref, cm_ref, in_ref, small_ref,
+                      keep_ref, send_ref, c_t, cm_t):
+    step = pl.program_id(0)
+    sec = sec_ref[0]
+    parts = order_ref.shape[0] // 2
+    half = n2_ref.shape[-1] // 2
+    up_rows = cb_ref.shape[-1] // 2
+    thin = c_ref.shape[-1] // parts
+    steps = pl.num_programs(0) // 2
+    outs = (keep_ref, send_ref)
+
+    @pl.when(step == 0)
+    def _():
+        c_t[...] = c_ref[...].T
+        cm_t[...] = cm_ref[...].T
+        for side in range(2):
+            which = sec if side == 0 else 1 - sec
+            for part in range(parts):
+                at = order_ref[side * parts + part]
+                row = small_ref[pl.ds(which * parts + part, 1), 0, :]
+                outs[side][at, up_rows * 2 + thin:, :] = jnp.broadcast_to(row, (16, half)).astype(BF16)
+
+    both = tn(cb_ref[...], n2_ref[...])
+    left, right = both[:, :half], both[:, half:]
+    flip = jnp.full((1, 1), sec) == 0
+    sides = (jnp.where(flip, left, right).astype(BF16), jnp.where(flip, right, left).astype(BF16))
+    for side in range(2):
+        for sub in range(2):
+            at = order_ref[side * parts + step * 2 + sub]
+            outs[side][at, 0:up_rows, :] = sides[side][sub * up_rows:(sub + 1) * up_rows]
+
+    down = nn(c_t[...], hid_ref[...]).astype(BF16)
+    for side in range(2):
+        @pl.when(step // steps == side)
+        def _():
+            rows = pl.ds(pl.multiple_of(up_rows + thin * (step % steps), 16), thin)
+            for part in range(parts):
+                outs[side][order_ref[side * parts + part], rows, :] = down[thin * part:thin * (part + 1)]
+
+        @pl.when(step == side * steps)
+        def _():
+            which = sec if side == 0 else 1 - sec
+            out = nn(cm_t[...], in_ref[:, pl.ds(pl.multiple_of(which * half, 128), half)]).astype(BF16)
+            for part in range(parts):
+                outs[side][order_ref[side * parts + part], 2 * up_rows:2 * up_rows + thin, :] = out[thin * part:thin * (part + 1)]
+
+
+def feed_grads(sec, order, cb, hidden, c, n2, cm, inner, small):
+    rows, width = c.shape
+    wide = cb.shape[-1]
+    parts = order.shape[0] // 2
+    half = width // 2
+    steps = wide // half
+    up_rows = wide // parts
+    total = 2 * up_rows + width // parts + 16
+    full = lambda n: pl.BlockSpec((rows, n), lambda i, s, o: (0, 0))
+    out_spec = pl.BlockSpec((parts, total, half), lambda i, s, o: (0, 0, 0))
+    out_shape = jax.ShapeDtypeStruct((parts, total, half), BF16)
+    return pl.pallas_call(
+        feed_grads_kernel,
+        grid_spec=pltpu.PrefetchScalarGridSpec(
+            num_scalar_prefetch=2,
+            grid=(steps,),
+            in_specs=[
+                pl.BlockSpec((rows, half), lambda i, s, o: (0, i)),
+                pl.BlockSpec((rows, half), lambda i, s, o: (0, jnp.where(i < steps // 2, s[0], 1 - s[0]) * (steps // 2) + i % (steps // 2))),
+                full(width), full(width), full(width), full(width),
+                pl.BlockSpec((2 * parts, 1, half), lambda i, s, o: (0, 0, 0)),
+            ],
+            out_specs=[out_spec, out_spec],
+            scratch_shapes=[pltpu.VMEM((width, rows), BF16), pltpu.VMEM((width, rows), BF16)],
+        ),
+        out_shape=[out_shape, out_shape],
+        compiler_params=pltpu.CompilerParams(vmem_limit_bytes=VLIM),
+        cost_estimate=pl.CostEstimate(flops=2 * rows * width * (2 * wide + width), bytes_accessed=30 * 1024 * 1024, transcendentals=0),
+        name="feed_gradients",
+    )(sec, order, cb, hidden, c, n2, cm, inner, small)
+
+
+def joint_grads_kernel(sec_ref, order_ref, cj_ref, n_ref, small_ref, keep_ref, send_ref, acc):
+    step = pl.program_id(0)
+    sec = sec_ref[0]
+    parts = order_ref.shape[0] // 2
+    width = n_ref.shape[-1]
+    half = width // 2
+    thick = acc.shape[0] // parts
+    outs = (keep_ref, send_ref)
+    acc[pl.ds(pl.multiple_of(step * width, 16), width), :] = tn(cj_ref[0], n_ref[...]).astype(BF16)
+
+    @pl.when(step == pl.num_programs(0) - 1)
+    def _():
+        for side in range(2):
+            which = sec if side == 0 else 1 - sec
+            columns = pl.ds(pl.multiple_of(which * half, 128), half)
+            for part in range(parts):
+                at = order_ref[side * parts + part]
+                outs[side][at, 0:thick, :] = acc[thick * part:thick * (part + 1), columns]
+                row = small_ref[pl.ds(which * parts + part, 1), 0, :]
+                outs[side][at, thick:, :] = jnp.broadcast_to(row, (16, half)).astype(BF16)
+
+
+def joint_grads(sec, order, cj, normed, small):
+    rows, width = normed.shape
+    parts = order.shape[0] // 2
+    half = width // 2
+    thick = 3 * width // parts
+    out_spec = pl.BlockSpec((parts, thick + 16, half), lambda i, s, o: (0, 0, 0))
+    out_shape = jax.ShapeDtypeStruct((parts, thick + 16, half), BF16)
+    return pl.pallas_call(
+        joint_grads_kernel,
+        grid_spec=pltpu.PrefetchScalarGridSpec(
+            num_scalar_prefetch=2,
+            grid=(3,),
+            in_specs=[
+                pl.BlockSpec((1, rows, width), lambda i, s, o: (i, 0, 0)),
+                pl.BlockSpec((rows, width), lambda i, s, o: (0, 0)),
+                pl.BlockSpec((2 * parts, 1, half), lambda i, s, o: (0, 0, 0)),
+            ],
+            out_specs=[out_spec, out_spec],
+            scratch_shapes=[pltpu.VMEM((3 * width, width), BF16)],
+        ),
+        out_shape=[out_shape, out_shape],
+        compiler_params=pltpu.CompilerParams(vmem_limit_bytes=VLIM),
+        cost_estimate=pl.CostEstimate(flops=6 * rows * width * width, bytes_accessed=14 * 1024 * 1024, transcendentals=0),
+        name="joint_gradients",
+    )(sec, order, cj, normed, small)
+
+
+def small_rows(items, parts, half):
+    lined = jnp.concatenate([item.reshape(parts, -1) for item in items], axis=1)
+    lined = lined.reshape(parts, 2, -1).transpose(1, 0, 2)
+    lined = jnp.pad(lined, ((0, 0), (0, 0), (0, half - lined.shape[-1])))
+    return lined.reshape(2 * parts, 1, half)
+
+
+def swap_pairs(change, sizes):
+    sections, dps, seqs = sizes
+    pairs = []
+    for section in range(sections):
+        for dp in range(dps):
+            for seq in range(seqs):
+                a, b, c = change(section, dp, seq)
+                pairs.append(((section * dps + dp) * seqs + seq, (a * dps + b) * seqs + c))
+    return pairs
+
+
+def reduce_chunks(kept, sent, sizes):
+    every = ("section", "dp", "seq")
+    moves = (
+        lambda s, d, q: (s, d ^ 1, q) if s == 0 else (s, d, q ^ 1),
+        lambda s, d, q: (s, d, q ^ 1) if s == 0 else (s, d ^ 1, q),
+        lambda s, d, q: (s, d ^ 2, q),
+        lambda s, d, q: (s, d ^ 4, q),
+    )
+    arrived = lax.ppermute(sent, "section", [(0, 1), (1, 0)])
+    for move in moves:
+        middle = kept.shape[0] // 2
+        sent = (kept[middle:].astype(F32) + arrived[middle:].astype(F32)).astype(BF16)
+        held = kept[:middle].astype(F32) + arrived[:middle].astype(F32)
+        arrived = lax.ppermute(sent, every, swap_pairs(move, sizes))
+        kept = held if middle == 1 else held.astype(BF16)
+    return kept[0] + arrived[0].astype(F32)
+
+
+def row_step(
+    sizes,
+    tokens,
+    segments,
+    cotangent,
+    joint_weight,
+    joint_bias,
+    output_weight,
+    output_bias,
+    up_weight,
+    up_bias,
+    down_weight,
+    down_bias,
+    first_gain,
+    inner_gain,
+    second_gain,
+    hidden_gain,
+):
+    micro, row_count, piece, width = tokens.shape
+    rows = 2 * piece
+    wide = up_weight.shape[-1]
+    parts = sizes[1] * sizes[2]
+    half = width // 2
+    section = lax.axis_index("section")
+    part = lax.axis_index("seq")
+    data = lax.axis_index("dp")
+    sec = section.reshape(1).astype(jnp.int32)
+    mine = 2 * section + part
+    swap = [(0, 1), (1, 0)]
+
+    def pick(array, index):
+        return lax.dynamic_index_in_dim(array, index, 0, keepdims=False)
+
+    flat = tokens.reshape(micro * row_count, piece, width)
+    beside = lax.ppermute(pick(flat, mine ^ 1), "seq", swap)
+    state = jnp.concatenate([pick(flat, mine), beside], axis=0)
+    both = [(own[0], lax.ppermute(own[0], "section", swap)) for own in (joint_weight, output_weight, up_weight, down_weight)]
+    joint_pair, output_pair, up_pair, down_pair = both
+    own = jnp.concatenate([joint_bias, output_bias, up_bias, down_bias, first_gain, inner_gain, second_gain, hidden_gain], axis=1)
+    other = lax.ppermute(own, "section", swap)
+    packs = (jnp.where(section == 0, own, other), jnp.where(section == 0, other, own))
+    flat = cotangent.reshape(micro * row_count, piece, width)
+    beside = lax.ppermute(pick(flat, mine ^ 1), "seq", swap)
+    slope = jnp.concatenate([pick(flat, mine), beside], axis=0)
+
+    whole = pick(segments.reshape(micro * row_count, rows), mine)
+    starts = jnp.sum((whole[None, :] < whole[:, None]).astype(jnp.int32), axis=1)
+    places = jnp.arange(rows, dtype=jnp.int32) - starts
+    turn = lambda a: jnp.where(part == 0, a, jnp.roll(a, piece))
+    cosine, sine = tables(None, turn(places))
+    labels = turn(whole).reshape(rows, 1)
+
+    mx, my, mz = data % 2, part, data // 2
+    index = jnp.arange(parts, dtype=jnp.int32)
+    cx, cy, cz = (index // 2) % 2 ^ mx, index % 2 ^ my, index // 4 ^ mz
+    depth = cz % 2 * 2 + cz // 2
+    order_x, order_y = (cx * 2 + cy) * 4 + depth, (cy * 2 + cx) * 4 + depth
+    order = jnp.where(section == 0, jnp.concatenate([order_x, order_y]), jnp.concatenate([order_y, order_x]))
+
+    lengths = (3 * width, width, wide, width, width, width, width, wide)
+
+    def cut(pack, which):
+        begin = sum(lengths[:which])
+        return pack[:, begin:begin + lengths[which]]
+
+    kept = []
+    hiddens = []
+    for layer in range(2):
+        pack = packs[layer]
+        jb, ob, ub, db, fg, ig, sg, hg = (cut(pack, which) for which in range(8))
+        normed, q, k, v = qkv(layer, sec, state, fg, *joint_pair, jb, cosine, sine, labels)
+        attended, query = attend(q, k, v)
+        result, mixed, hidden, bend, stats = feed(layer, sec, attended, state, ig, ob, sg, ub, hg, db, output_pair, up_pair, down_pair)
+        kept.append((state, normed, query, k, v, attended, mixed, hidden, bend, stats))
+        hiddens.append(result)
+        state = result
+
+    done = [None, None]
+    grads = [None, None]
+    for layer in (1, 0):
+        pack = packs[layer]
+        jb, ob, ub, db, fg, ig, sg, hg = (cut(pack, which) for which in range(8))
+        state, normed, query, k, v, attended, mixed, hidden, bend, stats = kept[layer]
+        cb, cm, cm_low, ch, n2, inner, wide_sums, thin_sums = feed_back(
+            layer, sec, slope, hidden, bend, stats, mixed, attended, ig, sg, hg, output_pair, up_pair, down_pair)
+        small = small_rows((thin_sums[2], wide_sums[1], thin_sums[0], thin_sums[3], thin_sums[1], wide_sums[0]), parts, half)
+        feed_part = reduce_chunks(*feed_grads(sec, order, cb, hidden, slope, n2, cm_low, inner, small), sizes)
+        cj = attend_back(query, k, v, ch, attended, cosine, sine)
+        back, sums = qkv_back(layer, sec, cj, state, cm, fg, *joint_pair)
+        small = small_rows((sums[1:].reshape(-1), sums[0]), parts, half)
+        joint_part = reduce_chunks(*joint_grads(sec, order, cj, normed, small), sizes)
+        grads[layer] = jnp.concatenate([feed_part, joint_part], axis=0)
+        done[layer] = back
+        slope = back
+
+    def spread(pieces):
+        every = ("section", "seq")
+        got = [None] * 4
+        for fs in range(2):
+            for fq in range(2):
+                owed = [item[piece * fq:piece * (fq + 1)] for item in pieces]
+                if fs == 0:
+                    block = jnp.where(section == 0, owed[0], owed[1])
+                else:
+                    block = jnp.where(section == 0, owed[1], owed[0])
+                if fs or fq:
+                    pairs = [(2 * s + q, 2 * (s ^ fs) + (q ^ fq)) for s in range(2) for q in range(2)]
+                    block = lax.ppermute(block, every, pairs)
+                got[2 * fs + fq] = block
+        stacked = jnp.stack(got)
+        return jnp.stack([pick(stacked, mine ^ index) for index in range(4)]).reshape(1, micro, row_count, piece, width)
+
+    hiddens = spread(hiddens)
+    input_gradients = spread(done).astype(F32)
+
+    ours = jnp.where(section == 0, grads[0], grads[1])
+    theirs = lax.ppermute(jnp.where(section == 0, grads[1], grads[0]), "section", swap)
+    left = jnp.where(section == 0, ours, theirs)
+    right = jnp.where(section == 0, theirs, ours)
+    up_rows, thin, thick = wide // parts, width // parts, 3 * width // parts
+
+    def rows_of(begin, count):
+        return jnp.concatenate([left[begin:begin + count], right[begin:begin + count]], axis=1)
+
+    up_grad = rows_of(0, up_rows).T
+    at = up_rows
+    steps = up_rows // thin
+    sides = [item[at:at + up_rows].reshape(steps, thin, half).transpose(0, 2, 1).reshape(steps * half, thin) for item in (left, right)]
+    down_grad = jnp.concatenate(sides, axis=0)
+    at += up_rows
+    output_grad = rows_of(at, thin).T
+    at += thin
+    sizes_small = (thin, up_rows, thin, thin, thin, up_rows)
+    used = sum(sizes_small) // 2
+    line = jnp.concatenate([left[at, :used], right[at, :used]])
+    at += 16
+    ends = [sum(sizes_small[:i + 1]) for i in range(len(sizes_small))]
+    ob, ub, db, ig, sg, hg = (line[end - size:end] for end, size in zip(ends, sizes_small))
+    joint_grad = rows_of(at, thick).T
+    at += thick
+    used = (thick + thin) // 2
+    line = jnp.concatenate([left[at, :used], right[at, :used]])
+    jb, fg = line[:thick], line[thick:]
+    return (
+        hiddens,
+        input_gradients,
+        joint_grad[None],
+        jb[None],
+        output_grad[None],
+        ob[None],
+        up_grad[None],
+        ub[None],
+        down_grad[None],
+        db[None],
+        fg[None],
+        ig[None],
+        sg[None],
+        hg[None],
+    )
+
+
+def choose(sizes, *arrays):
+    micro, row_count, piece, width = arrays[0].shape
+    if sizes == (2, 8, 2) and micro * row_count == 4:
+        return row_step(sizes, *arrays)
+    return shards(*arrays)
+
+
 def solution(mesh):
+    axes = ("section", "dp", "seq")
     return jax.shard_map(
-        shards,
+        functools.partial(choose, tuple(mesh.shape[name] for name in axes)),
         mesh=mesh,
         in_specs=(
             P(None, "dp", "seq", None),

time: 3630 us -> 685 us (0.19)
  waiting for transfers between devices: 1660 us -> 186 us
  matrix products: 941 us -> 0 us
  other arithmetic: 744 us -> 52 us
  Pallas kernels: 0 us -> 360 us
  local copies, waits for them, and re-layouts: 233 us -> 33.4 us
    dot_general x115 -> x0, matrix products: 941 us -> none  [the longest x10 183 us: layer_forward(): jnp.dot(normed_two, up_weight, preferred_element_type=jnp.float32) + up_bias]
    unnamed x45 -> x0, waiting for transfers between devices: 785 us -> none
    reduce_scatter x9 -> x0, waiting for transfers between devices: 775 us -> none  [the longest x1 178 us: shards(): lax.psum_scatter(totals[6], ('dp', 'seq'), scatter_dimension=1, tiled=True)]
    pallas_call x0 -> x16, Pallas kernels: none -> 360 us  [the longest x2 69.7 us: attend_back(): pl.pallas_call(functools.partial(attend_back_kernel, qb), grid=(heads //...]
    sub x10 -> x1, other arithmetic: 347 us -> 0.01 us  [row_step(): places = jnp.arange(rows, dtype=jnp.int32) - starts]
    ppermute x8 -> x34, waiting for transfers between devices: 6.95 us -> 186 us  [the longest x6 114 us: spread(): block = lax.ppermute(block, every, pairs)]
    reduce_sum x83 -> x1, other arithmetic: 153 us -> 0.56 us  [row_step(): jnp.sum((whole[None, :] < whole[:, None]).astype(jnp.int32), axis=1)]
    slice x55 -> x24, local copies, waits for them, and re-layouts: 128 us -> 10.2 us  [the longest x6 3.62 us: cut(): return pack[:, begin:begin + lengths[which]]]
  transfers between devices with their start and end apart: 45 -> 34, of which waited for: 24 -> 10; matrix products, arithmetic and copies ran while one was open for 27% -> 10% of each run, Pallas kernels for 0% -> 19%
where the time goes in v1:
time: 685 us; the launch traced here: 674 us
  Pallas kernels  360 us (53%)
  waiting for transfers between devices  186 us (27%)
  other arithmetic  52 us (8%)
  starting transfers between devices  41.2 us (6%)
  local copies, waits for them, and re-layouts  33.4 us (5%)
    ppermute x6, waiting for transfers between devices, spread(): block = lax.ppermute(block, every, pairs)  114 us
    pallas_call x2, Pallas kernels, attend_back(): pl.pallas_call(functools.partial(attend_back_kernel, qb), grid=(heads //...  69.7 us
    pallas_call x2, Pallas kernels, feed_back(): pl.pallas_call(functools.partial(feed_back_kernel, layer), grid=(rows //...  61.6 us
    ppermute x16, waiting for transfers between devices, reduce_chunks(): arrived = lax.ppermute(sent, every, swap_pairs(move, sizes))  59.4 us
    pallas_call x2, Pallas kernels, feed(): pl.pallas_call(functools.partial(feed_kernel, layer), grid=(rows // tb,),...  59.2 us
    pallas_call x2, Pallas kernels, attend(): pl.pallas_call(functools.partial(attend_kernel, qb), grid=(heads // 2,),...  54 us
    pallas_call x2, Pallas kernels, feed_grads(): pl.pallas_call(feed_grads_kernel, grid_spec=pltpu.PrefetchScalarGridSpec(...  50.3 us
    convert_element_type x12, other arithmetic, reduce_chunks(): kept = held if middle == 1 else held.astype(BF16)  24.4 us
  transfers between devices with their start and end apart: 34, of which 10 were waited for; matrix products, arithmetic and copies ran while one was open for 10% of the time, Pallas kernels for 19%

profile of v1, /device:TPU:0, one launch (start us, length us, event | category | flops | bytes accessed | tf_op | source)
XLA Modules:
  0.0 673.9 jit_solution(16353100718113113316)
XLA Ops:
  0.7 2.6 dynamic-slice_bitcast_fusion.7
  3.4 3.0 collective-permute-start
  17.6 1.0 copy.52
  18.6 1.0 copy.51
  19.7 2.8 dynamic-slice_bitcast_fusion.5
  22.4 1.9 broadcast_select_fusion.8.lab_ref
  24.4 3.8 fusion.2
  28.8 0.9 broadcast_select_fusion.9
  33.3 2.6 pad_maximum_fusion.2.x_ref
  35.9 12.5 %collective-permute-done.9 = bf16[512,768]{1,0:T(8,128)(2,1)S(1)} collective-permute-done((bf16[512,768]{1,0:T(8,128)(2,1)}, bf16[512,768]{1,0:T(8,128)(2,1)S(1)}, u32[]{:S(2)}, u32[]{:S(2)}) %collective-permute-start.9) | collective-permute-done | bytes 786464 | tf_op jit(solution)/shard_map/ppermute | solution.py:986
  48.5 1.3 pad_maximum_fusion.3.c_ref
  49.7 1.8 copy-done
  51.5 11.9 %joint_projection.2 = (bf16[1024,768]{1,0:T(8,128)(2,1)}, bf16[12,1024,128]{2,1,0:T(8,128)(2,1)}, bf16[12,1024,128]{2,1,0:T(8,128)(2,1)}, bf16[12,1024,128]{2,1,0:T(8,128)(2,1)}) custom-call(s32[1]{0:T(128)} %bitcast.sec_ref, bf16[1024,768]{1,0:T(8,128)(2,1)} %pad_maximum_fusion.2.x_ref, f32[1,768]{1,0:T(1,128)} %get-tuple-element.250.gain_ref, ...), custom_call_target="tpu_custom_call" | custom-call | flops 3623878656 | bytes 16777216 | tf_op jit(solution)/shard_map/joint_projection/pallas_call | solution.py:505
  63.4 27.0 %attention_forward.2 = (f32[1024,768]{1,0:T(8,128)}, bf16[12,1024,128]{2,1,0:T(8,128)(2,1)}) custom-call(bf16[12,1024,128]{2,1,0:T(8,128)(2,1)} %get-tuple-element.64.q_ref, bf16[12,1024,128]{2,1,0:T(8,128)(2,1)} %get-tuple-element.65.k_ref, bf16[12,1024,128]{2,1,0:T(8,128)(2,1)} %get-tuple-element.66.v_ref), custom_call_target="tpu_custom_call" | custom-call | flops 12884901888 | bytes 16777216 | tf_op jit(solution)/shard_map/attention_forward/pallas_call | solution.py:542
  90.5 29.6 %feed_forward.2 = (bf16[1024,768]{1,0:T(8,128)(2,1)}, f32[1024,768]{1,0:T(8,128)}, bf16[1024,3072]{1,0:T(8,128)(2,1)}, bf16[1024,3072]{1,0:T(8,128)(2,1)}, f32[1024,128]{1,0:T(8,128)}) custom-call(s32[1]{0:T(128)} %bitcast.sec_ref, f32[1024,768]{1,0:T(8,128)} %get-tuple-element.67.at_ref, bf16[1024,768]{1,0:T(8,128)(2,1)} %pad_maximum_fusion.2.x_ref, ...), custom_call_target="tpu_custom_call" | custom-call | flops 10871635968 | bytes 41943040 | tf_op jit(solution)/shard_map/feed_forward/pallas_call | solution.py:581
  120.0 12.2 %joint_projection.3 = (bf16[1024,768]{1,0:T(8,128)(2,1)}, bf16[12,1024,128]{2,1,0:T(8,128)(2,1)}, bf16[12,1024,128]{2,1,0:T(8,128)(2,1)}, bf16[12,1024,128]{2,1,0:T(8,128)(2,1)}) custom-call(s32[1]{0:T(128)} %bitcast.sec_ref, bf16[1024,768]{1,0:T(8,128)(2,1)} %get-tuple-element.68.x_ref, f32[1,768]{1,0:T(1,128)} %get-tuple-element.243.gain_ref, ...), custom_call_target="tpu_custom_call" | custom-call | flops 3623878656 | bytes 16777216 | tf_op jit(solution)/shard_map/joint_projection/pallas_call | solution.py:505
  132.2 27.0 %attention_forward.3 = (f32[1024,768]{1,0:T(8,128)}, bf16[12,1024,128]{2,1,0:T(8,128)(2,1)}) custom-call(bf16[12,1024,128]{2,1,0:T(8,128)(2,1)} %get-tuple-element.69.q_ref, bf16[12,1024,128]{2,1,0:T(8,128)(2,1)} %get-tuple-element.70.k_ref, bf16[12,1024,128]{2,1,0:T(8,128)(2,1)} %get-tuple-element.71.v_ref), custom_call_target="tpu_custom_call" | custom-call | flops 12884901888 | bytes 16777216 | tf_op jit(solution)/shard_map/attention_forward/pallas_call | solution.py:542
  159.2 29.6 %feed_forward.3 = (bf16[1024,768]{1,0:T(8,128)(2,1)}, f32[1024,768]{1,0:T(8,128)}, bf16[1024,3072]{1,0:T(8,128)(2,1)}, bf16[1024,3072]{1,0:T(8,128)(2,1)}, f32[1024,128]{1,0:T(8,128)}) custom-call(s32[1]{0:T(128)} %bitcast.sec_ref, f32[1024,768]{1,0:T(8,128)} %get-tuple-element.72.at_ref, bf16[1024,768]{1,0:T(8,128)(2,1)} %get-tuple-element.68.x_ref, ...), custom_call_target="tpu_custom_call" | custom-call | flops 10871635968 | bytes 41943040 | tf_op jit(solution)/shard_map/feed_forward/pallas_call | solution.py:581
  188.8 30.9 %feed_backward.2 = (bf16[1024,3072]{1,0:T(8,128)(2,1)}, f32[1024,768]{1,0:T(8,128)}, bf16[1024,768]{1,0:T(8,128)(2,1)}, bf16[1024,768]{1,0:T(8,128)(2,1)}, bf16[...) custom-call(s32[1]{0:T(128)} %bitcast.sec_ref, ...), custom_call_target="tpu_custom_call" | custom-call | flops 10871635968 | bytes 52428800 | tf_op jit(solution)/shard_map/feed_backward/pallas_call | solution.py:652
  219.7 34.9 %attention_backward.2.cj_ref = bf16[3,1024,768]{2,1,0:T(8,128)(2,1)} custom-call(bf16[12,1024,128]{2,1,0:T(8,128)(2,1)} %get-tuple-element.75.q_ref, bf16[12,1024,128]{2,1,0:T(8,128)(2,1)} %get-tuple-element.70.k_ref, bf16[12,1024,128]{2,1,0:T(8,128)(2,1)} %get-tuple-element.71.v_ref, bf16[1024,768]{1,0:T(8,128)(2,1)} %get-tuple-element.80.ch_ref, ...), custom_call_target="tpu_custom_call" | custom-call | flops 32212254720 | bytes 20971520 | tf_op jit(solution)/shard_map/attention_backward/pallas_call | solution.py:712
  254.6 11.1 %joint_backward.2 = (bf16[1024,768]{1,0:T(8,128)(2,1)}, f32[4,768]{1,0:T(4,128)}) custom-call(s32[1]{0:T(128)} %bitcast.sec_ref, bf16[3,1024,768]{2,1,0:T(8,128)(2,1)} %attention_backward.2.cj_ref, bf16[1024,768]{1,0:T(8,128)(2,1)} %get-tuple-element.68.x_ref, f32[1024,768]{1,0:T(8,128)} %get-tuple-element.81.cm_ref, f32[1,768]{1,0:T(1,128)} %get-tuple-element.243.gain_ref, ...), custom_call_target="tpu_custom_call" | custom-call | flops 3623878656 | bytes 16777216 | tf_op jit(solution)/shard_map/joint_backward/pallas_call | solution.py:755
  265.6 30.7 %feed_backward.3 = (bf16[1024,3072]{1,0:T(8,128)(2,1)}, f32[1024,768]{1,0:T(8,128)}, bf16[1024,768]{1,0:T(8,128)(2,1)}, bf16[1024,768]{1,0:T(8,128)(2,1)}, bf16[...) custom-call(s32[1]{0:T(128)} %bitcast.sec_ref, ...), custom_call_target="tpu_custom_call" | custom-call | flops 10871635968 | bytes 52428800 | tf_op jit(solution)/shard_map/feed_backward/pallas_call | solution.py:652
  296.4 0.9 slice_reduce_fusion
  297.5 1.0 slice_reduce_fusion.10
  299.7 25.1 %feed_gradients.2 = (bf16[16,448,384]{2,1,0:T(8,128)(2,1)}, bf16[16,448,384]{2,1,0:T(8,128)(2,1)}) custom-call(s32[1]{0:T(128)} %bitcast.sec_ref, s32[32]{0:T(128)} %broadcast_select_fusion.11.order_ref, bf16[1024,3072]{1,0:T(8,128)(2,1)} %get-tuple-element.90.cb_ref, bf16[1024,3072]{1,0:T(8,128)(2,1)} %get-tuple-element.83.hid_ref, ...), custom_call_target="tpu_custom_call" | custom-call | flops 10871635968 | bytes 31457280 | tf_op jit(solution)/shard_map/feed_gradients/pallas_call | solution.py:838
  326.1 25.2 %feed_gradients.3 = (bf16[16,448,384]{2,1,0:T(8,128)(2,1)}, bf16[16,448,384]{2,1,0:T(8,128)(2,1)}) custom-call(s32[1]{0:T(128)} %bitcast.sec_ref, s32[32]{0:T(128)} %broadcast_select_fusion.11.order_ref, bf16[1024,3072]{1,0:T(8,128)(2,1)} %get-tuple-element.102.cb_ref, bf16[1024,3072]{1,0:T(8,128)(2,1)} %get-tuple-element.76.hid_ref, ...), custom_call_target="tpu_custom_call" | custom-call | flops 10871635968 | bytes 31457280 | tf_op jit(solution)/shard_map/feed_gradients/pallas_call | solution.py:838
  351.9 34.8 %attention_backward.3.cj_ref = bf16[3,1024,768]{2,1,0:T(8,128)(2,1)} custom-call(bf16[12,1024,128]{2,1,0:T(8,128)(2,1)} %get-tuple-element.74.q_ref, bf16[12,1024,128]{2,1,0:T(8,128)(2,1)} %get-tuple-element.65.k_ref, bf16[12,1024,128]{2,1,0:T(8,128)(2,1)} %get-tuple-element.66.v_ref, bf16[1024,768]{1,0:T(8,128)(2,1)} %get-tuple-element.87.ch_ref, ...), custom_call_target="tpu_custom_call" | custom-call | flops 32212254720 | bytes 20971520 | tf_op jit(solution)/shard_map/attention_backward/pallas_call | solution.py:712
  386.7 11.1 %joint_backward.3 = (bf16[1024,768]{1,0:T(8,128)(2,1)}, f32[4,768]{1,0:T(4,128)}) custom-call(s32[1]{0:T(128)} %bitcast.sec_ref, bf16[3,1024,768]{2,1,0:T(8,128)(2,1)} %attention_backward.3.cj_ref, bf16[1024,768]{1,0:T(8,128)(2,1)} %pad_maximum_fusion.2.x_ref, f32[1024,768]{1,0:T(8,128)} %get-tuple-element.88.cm_ref, f32[1,768]{1,0:T(1,128)} %get-tuple-element.250.gain_ref, ...), custom_call_target="tpu_custom_call" | custom-call | flops 3623878656 | bytes 16777216 | tf_op jit(solution)/shard_map/joint_backward/pallas_call | solution.py:755
  400.2 9.5 %joint_gradients.2 = (bf16[16,160,384]{2,1,0:T(8,128)(2,1)}, bf16[16,160,384]{2,1,0:T(8,128)(2,1)}) custom-call(s32[1]{0:T(128)} %bitcast.sec_ref, s32[32]{0:T(128)} %broadcast_select_fusion.11.order_ref, bf16[3,1024,768]{2,1,0:T(8,128)(2,1)} %attention_backward.3.cj_ref, bf16[1024,768]{1,0:T(8,128)(2,1)} %get-tuple-element.98.n_ref, ...), custom_call_target="tpu_custom_call" | custom-call | flops 3623878656 | bytes 14680064 | tf_op jit(solution)/shard_map/joint_gradients/pallas_call | solution.py:888
  410.9 9.4 %joint_gradients.3 = (bf16[16,160,384]{2,1,0:T(8,128)(2,1)}, bf16[16,160,384]{2,1,0:T(8,128)(2,1)}) custom-call(s32[1]{0:T(128)} %bitcast.sec_ref, s32[32]{0:T(128)} %broadcast_select_fusion.11.order_ref, bf16[3,1024,768]{2,1,0:T(8,128)(2,1)} %attention_backward.2.cj_ref, bf16[1024,768]{1,0:T(8,128)(2,1)} %get-tuple-element.110.n_ref, ...), custom_call_target="tpu_custom_call" | custom-call | flops 3623878656 | bytes 14680064 | tf_op jit(solution)/shard_map/joint_gradients/pallas_call | solution.py:888
  420.8 1.1 select_bitcast_fusion
  422.2 6.1 add_convert_fusion.3
  428.3 1.7 collective-permute-start.14
  430.1 5.1 add_convert_fusion.1
  435.8 6.5 collective-permute-done.10
  442.8 3.3 add_convert_fusion.11
  446.1 0.9 copy-done.10
  447.0 1.7 collective-permute-start.19
  448.7 2.2 select_bitcast_fusion.1
  450.8 66.5 %collective-permute-done.12 = bf16[512,768]{1,0:T(8,128)(2,1)} collective-permute-done((bf16[512,768]{1,0:T(8,128)(2,1)}, bf16[512,768]{1,0:T(8,128)(2,1)}, u32[]{:S(2)}, u32[]{:S(2)}) %collective-permute-start.12) | collective-permute-done | bytes 786464 | tf_op jit(solution)/shard_map/ppermute | solution.py:1051
  517.7 1.6 pad_maximum_fusion.1
  519.4 2.1 add_convert_fusion.9
  521.5 1.8 collective-permute-start.29
  523.3 1.4 add_convert_fusion.19
  524.8 12.8 %collective-permute-start.8 = (bf16[512,768]{1,0:T(8,128)(2,1)S(1)}, bf16[512,768]{1,0:T(8,128)(2,1)S(1)}, u32[]{:S(2)}, u32[]{:S(2)}) collective-permute-start(bf16[512,768]{1,0:T(8,128)(2,1)S(1)} %get-tuple-element.211), channel_id=1, source_target_pairs={{0,17},{1,16},{16,1},{17,0},{2,19},{3,18},{18,3},{19,2},{4,21},{5,... | collective-permute-start | bytes 2359304 | tf_op jit(solution)/shard_map/ppermute | solution.py:1051
  537.6 2.6 add_convert_fusion.7
  540.5 2.5 add_convert_fusion.5
  543.0 1.8 collective-permute-start.20
  545.4 1.8 collective-permute-start.30
  547.2 40.5 %collective-permute-done.8 = bf16[512,768]{1,0:T(8,128)(2,1)S(1)} collective-permute-done((bf16[512,768]{1,0:T(8,128)(2,1)S(1)}, bf16[512,768]{1,0:T(8,128)(2,1)S(1)}, u32[]{:S(2)}, u32[]{:S(2)}) %collective-permute-start.8) | collective-permute-done | bytes 786464 | tf_op jit(solution)/shard_map/ppermute | solution.py:1051
  588.2 3.9 collective-permute-done.20
  592.2 1.6 collective-permute-start.21
  593.8 18.2 %collective-permute-done.30 = bf16[4,160,384]{2,1,0:T(8,128)(2,1)S(1)} collective-permute-done((bf16[4,160,384]{2,1,0:T(8,128)(2,1)S(1)}, bf16[4,160,384]{2,1,0:T(8,128)(2,1)S(1)}, u32[]{:S(2)}, u32[]{:S(2)}) %collective-permute-start.30) | collective-permute-done | bytes 491552 | tf_op jit(solution)/shard_map/ppermute | solution.py:939
  612.2 1.6 collective-permute-start.31
  613.9 2.7 collective-permute-start.22
  617.8 1.6 collective-permute-start.26
  619.5 5.8 collective-permute-done.31
  625.3 1.8 collective-permute-start.32
  627.1 11.2 %collective-permute-done.16 = bf16[2,448,384]{2,1,0:T(8,128)(2,1)S(1)} collective-permute-done((bf16[2,448,384]{2,1,0:T(8,128)(2,1)S(1)}, bf16[2,448,384]{2,1,0:T(8,128)(2,1)S(1)}, u32[]{:S(2)}, u32[]{:S(2)}) %collective-permute-start.16) | collective-permute-done | bytes 688160 | tf_op jit(solution)/shard_map/ppermute | solution.py:939
  638.4 1.5 collective-permute-start.17
  639.9 9.6 %collective-permute-done.26 = bf16[2,448,384]{2,1,0:T(8,128)(2,1)S(1)} collective-permute-done((bf16[2,448,384]{2,1,0:T(8,128)(2,1)S(1)}, bf16[2,448,384]{2,1,0:T(8,128)(2,1)S(1)}, u32[]{:S(2)}, u32[]{:S(2)}) %collective-permute-start.26) | collective-permute-done | bytes 688160 | tf_op jit(solution)/shard_map/ppermute | solution.py:939
  650.6 10.7 %collective-permute-done.27 = bf16[1,448,384]{2,1,0:T(8,128)(2,1)S(1)} collective-permute-done((bf16[1,448,384]{2,1,0:T(8,128)(2,1)S(1)}, bf16[1,448,384]{2,1,0:T(8,128)(2,1)S(1)}, u32[]{:S(2)}, u32[]{:S(2)}) %collective-permute-start.27) | collective-permute-done | bytes 344096 | tf_op jit(solution)/shard_map/ppermute | solution.py:939
  662.0 3.0 maximum_convert_fusion
  665.0 1.9 maximum_bitcast_fusion
  (202 shorter events, 36.0 us)
Async XLA Ops:
  0.6 5.7 copy-start.17
  0.7 6.3 copy-start.19
  0.7 6.9 %copy-start.15 = (f32[1,3072]{1,0:T(1,128)S(1)}, f32[1,3072]{1,0:T(1,128)}, u32[]{:S(2)}) copy-start(f32[1,3072]{1,0:T(1,128)} %param.23) | copy-start | bytes 36868
  0.7 7.5 %copy-start.20 = (f32[1,768]{1,0:T(1,128)S(1)}, f32[1,768]{1,0:T(1,128)}, u32[]{:S(2)}) copy-start(f32[1,768]{1,0:T(1,128)} %param.25) | copy-start | bytes 9220
  0.7 8.0 %copy-start.21 = (f32[1,768]{1,0:T(1,128)S(1)}, f32[1,768]{1,0:T(1,128)}, u32[]{:S(2)}) copy-start(f32[1,768]{1,0:T(1,128)} %param.26) | copy-start | bytes 9220
  0.7 8.6 %copy-start.22 = (f32[1,768]{1,0:T(1,128)S(1)}, f32[1,768]{1,0:T(1,128)}, u32[]{:S(2)}) copy-start(f32[1,768]{1,0:T(1,128)} %param.27) | copy-start | bytes 9220
  0.7 9.2 %copy-start.23 = (f32[1,768]{1,0:T(1,128)S(1)}, f32[1,768]{1,0:T(1,128)}, u32[]{:S(2)}) copy-start(f32[1,768]{1,0:T(1,128)} %param.28) | copy-start | bytes 9220
  0.7 9.8 %copy-start.16 = (f32[1,3072]{1,0:T(1,128)S(1)}, f32[1,3072]{1,0:T(1,128)}, u32[]{:S(2)}) copy-start(f32[1,3072]{1,0:T(1,128)} %param.29) | copy-start | bytes 36868
  3.4 29.9 %collective-permute-start = (bf16[512,768]{1,0:T(8,128)(2,1)}, bf16[512,768]{1,0:T(8,128)(2,1)}, u32[]{:S(2)}, u32[]{:S(2)}) collective-permute-start(bf16[512,768]{1,0:T(8,128)(2,1)} %get-tuple-element.213), channel_id=1, source_target_pairs={{0,1},{1,0},{2,3},{3,2},{4,5},{5,4},{6,7},{7,6},{8,9},{9,8},{10,11... | collective-permute-start | bytes 2359304 | tf_op jit(solution)/shard_map/ppermute | solution.py:978
  11.1 17.7 %collective-permute-start.1 = (f32[1,12288]{1,0:T(1,128)}, f32[1,12288]{1,0:T(1,128)}, u32[]{:S(2)}, u32[]{:S(2)}) collective-permute-start(f32[1,12288]{1,0:T(1,128)} %constant_dynamic-update-slice_fusion), channel_id=1, source_target_pairs={{0,16},{16,0},{1,17},{17,1},{2,18},{18,2},{3,19},{19,3},{4,20},{20... | collective-permute-start | bytes 147464 | tf_op jit(solution)/shard_map/ppermute | solution.py:983
  11.1 38.6 %collective-permute-start.2 = (bf16[768,2304]{1,0:T(8,128)(2,1)}, bf16[768,2304]{1,0:T(8,128)(2,1)S(1)}, u32[]{:S(2)}, u32[]{:S(2)}) collective-permute-start(bf16[768,2304]{1,0:T(8,128)(2,1)} %bitcast.94), channel_id=1, source_target_pairs={{0,16},{16,0},{1,17},{17,1},{2,18},{18,2},{3,19},{19,3},{4,20},{20... | collective-permute-start | bytes 10616840 | tf_op jit(solution)/shard_map/ppermute | solution.py:980
  11.6 78.9 %collective-permute-start.4 = (bf16[768,3072]{1,0:T(8,128)(2,1)}, bf16[768,3072]{1,0:T(8,128)(2,1)}, u32[]{:S(2)}, u32[]{:S(2)}) collective-permute-start(bf16[768,3072]{1,0:T(8,128)(2,1)} %bitcast.84), channel_id=1, source_target_pairs={{0,16},{16,0},{1,17},{17,1},{2,18},{18,2},{3,19},{19,3},{4,20},{20... | collective-permute-start | bytes 14155784 | tf_op jit(solution)/shard_map/ppermute | solution.py:980
  11.6 78.9 %collective-permute-start.5 = (bf16[3072,768]{1,0:T(8,128)(2,1)}, bf16[3072,768]{1,0:T(8,128)(2,1)}, u32[]{:S(2)}, u32[]{:S(2)}) collective-permute-start(bf16[3072,768]{1,0:T(8,128)(2,1)} %bitcast.89), channel_id=1, source_target_pairs={{0,16},{16,0},{1,17},{17,1},{2,18},{18,2},{3,19},{19,3},{4,20},{20... | collective-permute-start | bytes 14155784 | tf_op jit(solution)/shard_map/ppermute | solution.py:980
  19.7 2.8 copy-start.18
  24.4 24.1 %copy-start.4 = (bf16[512,768]{1,0:T(8,128)(2,1)S(1)}, bf16[512,768]{1,0:T(8,128)(2,1)}, u32[]{:S(2)}) copy-start(bf16[512,768]{1,0:T(8,128)(2,1)} %get-tuple-element.202) | copy-start | bytes 2359300
  28.8 19.7 %collective-permute-start.9 = (bf16[512,768]{1,0:T(8,128)(2,1)}, bf16[512,768]{1,0:T(8,128)(2,1)S(1)}, u32[]{:S(2)}, u32[]{:S(2)}) collective-permute-start(bf16[512,768]{1,0:T(8,128)(2,1)} %get-tuple-element.203), channel_id=1, source_target_pairs={{0,1},{1,0},{2,3},{3,2},{4,5},{5,4},{6,7},{7,6},{8,9},{9,8},{10,11... | collective-permute-start | bytes 2359304 | tf_op jit(solution)/shard_map/ppermute | solution.py:986
  33.3 57.1 %collective-permute-start.3 = (bf16[768,768]{1,0:T(8,128)(2,1)}, bf16[768,768]{1,0:T(8,128)(2,1)}, u32[]{:S(2)}, u32[]{:S(2)}) collective-permute-start(bf16[768,768]{1,0:T(8,128)(2,1)} %bitcast.101), channel_id=1, source_target_pairs={{0,16},{16,0},{1,17},{17,1},{2,18},{18,2},{3,19},{19,3},{4,20},{20... | collective-permute-start | bytes 3538952 | tf_op jit(solution)/shard_map/ppermute | solution.py:980
  49.7 1.8 copy-start
  265.6 30.8 %copy-start.12 = (f32[2,3072]{1,0:T(2,128)S(1)}, f32[2,3072]{1,0:T(2,128)}, u32[]{:S(2)}) copy-start(f32[2,3072]{1,0:T(2,128)} %get-tuple-element.107) | copy-start | bytes 73732
  299.7 25.2 %copy-start.14 = (f32[4,768]{1,0:T(4,128)S(1)}, f32[4,768]{1,0:T(4,128)}, u32[]{:S(2)}) copy-start(f32[4,768]{1,0:T(4,128)} %get-tuple-element.106) | copy-start | bytes 36868
  324.7 97.5 %collective-permute-start.13 = (bf16[16,448,384]{2,1,0:T(8,128)(2,1)}, bf16[16,448,384]{2,1,0:T(8,128)(2,1)}, u32[]{:S(2)}, u32[]{:S(2)}) collective-permute-start(bf16[16,448,384]{2,1,0:T(8,128)(2,1)} %get-tuple-element.97), channel_id=1, source_target_pairs={{0,16},{16,0},{1,17},{17,1},{2,18},{18,2},{3,19},{19,3},{4,20},{20... | collective-permute-start | bytes 16515080 | tf_op jit(solution)/shard_map/ppermute | solution.py:934
  351.4 78.7 %collective-permute-start.23 = (bf16[16,448,384]{2,1,0:T(8,128)(2,1)}, bf16[16,448,384]{2,1,0:T(8,128)(2,1)}, u32[]{:S(2)}, u32[]{:S(2)}) collective-permute-start(bf16[16,448,384]{2,1,0:T(8,128)(2,1)} %get-tuple-element.109), channel_id=1, source_target_pairs={{0,16},{16,0},{1,17},{17,1},{2,18},{18,2},{3,19},{19,3},{4,20},{20... | collective-permute-start | bytes 16515080 | tf_op jit(solution)/shard_map/ppermute | solution.py:934
  400.2 9.6 %copy-start.13 = (f32[4,768]{1,0:T(4,128)S(1)}, f32[4,768]{1,0:T(4,128)}, u32[]{:S(2)}) copy-start(f32[4,768]{1,0:T(4,128)} %get-tuple-element.111) | copy-start | bytes 36868
  409.7 32.6 %collective-permute-start.18 = (bf16[16,160,384]{2,1,0:T(8,128)(2,1)}, bf16[16,160,384]{2,1,0:T(8,128)(2,1)}, u32[]{:S(2)}, u32[]{:S(2)}) collective-permute-start(bf16[16,160,384]{2,1,0:T(8,128)(2,1)} %get-tuple-element.101), channel_id=1, source_target_pairs={{0,16},{16,0},{1,17},{17,1},{2,18},{18,2},{3,19},{19,3},{4,20},{20... | collective-permute-start | bytes 5898248 | tf_op jit(solution)/shard_map/ppermute | solution.py:934
  410.9 9.9 %copy-start.2 = (bf16[1024,768]{1,0:T(8,128)(2,1)S(1)}, bf16[1024,768]{1,0:T(8,128)(2,1)}, u32[]{:S(2)}) copy-start(bf16[1024,768]{1,0:T(8,128)(2,1)} %get-tuple-element.82.c_ref) | copy-start | bytes 4718596
  410.9 9.9 %copy-start.7 = (bf16[1024,768]{1,0:T(8,128)(2,1)S(1)}, bf16[1024,768]{1,0:T(8,128)(2,1)}, u32[]{:S(2)}) copy-start(bf16[1024,768]{1,0:T(8,128)(2,1)} %get-tuple-element.89) | copy-start | bytes 4718596
  420.3 98.9 %collective-permute-start.28 = (bf16[16,160,384]{2,1,0:T(8,128)(2,1)}, bf16[16,160,384]{2,1,0:T(8,128)(2,1)}, u32[]{:S(2)}, u32[]{:S(2)}) collective-permute-start(bf16[16,160,384]{2,1,0:T(8,128)(2,1)} %get-tuple-element.113), channel_id=1, source_target_pairs={{0,16},{16,0},{1,17},{17,1},{2,18},{18,2},{3,19},{19,3},{4,20},{20... | collective-permute-start | bytes 5898248 | tf_op jit(solution)/shard_map/ppermute | solution.py:934
  421.9 20.4 %collective-permute-start.10 = (bf16[512,768]{1,0:T(8,128)(2,1)S(1)}, bf16[512,768]{1,0:T(8,128)(2,1)S(1)}, u32[]{:S(2)}, u32[]{:S(2)}) collective-permute-start(bf16[512,768]{1,0:T(8,128)(2,1)S(1)} %get-tuple-element.199), channel_id=1, source_target_pairs={{0,1},{1,0},{16,17},{17,16},{2,3},{3,2},{18,19},{19,18},{4,5},{5,4... | collective-permute-start | bytes 2359304 | tf_op jit(solution)/shard_map/ppermute | solution.py:1051
  422.2 7.8 %slice-start = ((s8[5505024]{0:T(1024)(128)(4,1)}), s8[4194304]{0:T(1024)(128)(4,1)S(1)}, s32[]{:S(2)}) async-start(s8[5505024]{0:T(1024)(128)(4,1)} %bitcast.99), calls=%async_computation | async-start | bytes 8388608
  422.2 7.8 %slice-start.1 = ((s8[5505024]{0:T(1024)(128)(4,1)}), s8[1310720]{0:T(1024)(128)(4,1)S(1)}, s32[]{:S(2)}) async-start(s8[5505024]{0:T(1024)(128)(4,1)} %bitcast.99), calls=%async_computation.1 | async-start | bytes 2621440
  428.3 96.5 %collective-permute-start.14 = (bf16[8,448,384]{2,1,0:T(8,128)(2,1)}, bf16[8,448,384]{2,1,0:T(8,128)(2,1)}, u32[]{:S(2)}, u32[]{:S(2)}) collective-permute-start(bf16[8,448,384]{2,1,0:T(8,128)(2,1)} %get-tuple-element.183), channel_id=1, source_target_pairs={{0,2},{1,3},{2,0},{3,1},{4,6},{5,7},{6,4},{7,5},{8,10},{9,11},{10,... | collective-permute-start | bytes 8257544 | tf_op jit(solution)/shard_map/ppermute | solution.py:939
  430.1 12.7 %copy-start.6 = (bf16[16,160,384]{2,1,0:T(8,128)(2,1)S(1)}, bf16[16,160,384]{2,1,0:T(8,128)(2,1)}, u32[]{:S(2)}) copy-start(bf16[16,160,384]{2,1,0:T(8,128)(2,1)} %get-tuple-element.100) | copy-start | bytes 5898244
  435.2 105.0 %collective-permute-start.24 = (bf16[8,448,384]{2,1,0:T(8,128)(2,1)}, bf16[8,448,384]{2,1,0:T(8,128)(2,1)}, u32[]{:S(2)}, u32[]{:S(2)}) collective-permute-start(bf16[8,448,384]{2,1,0:T(8,128)(2,1)} %get-tuple-element.185), channel_id=1, source_target_pairs={{0,2},{1,3},{2,0},{3,1},{4,6},{5,7},{6,4},{7,5},{8,10},{9,11},{10,... | collective-permute-start | bytes 8257544 | tf_op jit(solution)/shard_map/ppermute | solution.py:939
  442.4 3.7 copy-start.8
  442.4 3.7 collective-permute-start.11
  442.4 75.0 %collective-permute-start.12 = (bf16[512,768]{1,0:T(8,128)(2,1)}, bf16[512,768]{1,0:T(8,128)(2,1)}, u32[]{:S(2)}, u32[]{:S(2)}) collective-permute-start(bf16[512,768]{1,0:T(8,128)(2,1)} %get-tuple-element.201), channel_id=1, source_target_pairs={{0,17},{1,16},{16,1},{17,0},{2,19},{3,18},{18,3},{19,2},{4,21},{5,... | collective-permute-start | bytes 2359304 | tf_op jit(solution)/shard_map/ppermute | solution.py:1051
  446.1 0.9 copy-start.10
  447.0 74.6 %collective-permute-start.19 = (bf16[8,160,384]{2,1,0:T(8,128)(2,1)}, bf16[8,160,384]{2,1,0:T(8,128)(2,1)}, u32[]{:S(2)}, u32[]{:S(2)}) collective-permute-start(bf16[8,160,384]{2,1,0:T(8,128)(2,1)} %get-tuple-element.191), channel_id=1, source_target_pairs={{0,2},{1,3},{2,0},{3,1},{4,6},{5,7},{6,4},{7,5},{8,10},{9,11},{10,... | collective-permute-start | bytes 2949128 | tf_op jit(solution)/shard_map/ppermute | solution.py:939
  448.7 69.0 %copy-start.9 = (bf16[512,768]{1,0:T(8,128)(2,1)S(1)}, bf16[512,768]{1,0:T(8,128)(2,1)}, u32[]{:S(2)}) copy-start(bf16[512,768]{1,0:T(8,128)(2,1)} %copy-done.8) | copy-start | bytes 2359300
  448.7 69.0 %copy-start.11 = (bf16[512,768]{1,0:T(8,128)(2,1)S(1)}, bf16[512,768]{1,0:T(8,128)(2,1)}, u32[]{:S(2)}) copy-start(bf16[512,768]{1,0:T(8,128)(2,1)} %copy-done.10) | copy-start | bytes 2359300
  517.4 25.7 %collective-permute-start.6 = (bf16[512,768]{1,0:T(8,128)(2,1)S(1)}, bf16[512,768]{1,0:T(8,128)(2,1)S(1)}, u32[]{:S(2)}, u32[]{:S(2)}) collective-permute-start(bf16[512,768]{1,0:T(8,128)(2,1)S(1)} %get-tuple-element.209), channel_id=1, source_target_pairs={{0,1},{1,0},{16,17},{17,16},{2,3},{3,2},{18,19},{19,18},{4,5},{5,4... | collective-permute-start | bytes 2359304 | tf_op jit(solution)/shard_map/ppermute | solution.py:1051
  517.7 1.8 copy-start.5
  519.2 26.2 %collective-permute-start.7 = (bf16[512,768]{1,0:T(8,128)(2,1)S(1)}, bf16[512,768]{1,0:T(8,128)(2,1)S(1)}, u32[]{:S(2)}, u32[]{:S(2)}) collective-permute-start(bf16[512,768]{1,0:T(8,128)(2,1)S(1)} %get-tuple-element.210), channel_id=1, source_target_pairs={{0,16},{1,17},{16,0},{17,1},{2,18},{3,19},{18,2},{19,3},{4,20},{5,... | collective-permute-start | bytes 2359304 | tf_op jit(solution)/shard_map/ppermute | solution.py:1051
  519.4 3.9 copy-start.3
  521.5 23.3 %collective-permute-start.29 = (bf16[8,160,384]{2,1,0:T(8,128)(2,1)S(1)}, bf16[8,160,384]{2,1,0:T(8,128)(2,1)S(1)}, u32[]{:S(2)}, u32[]{:S(2)}) collective-permute-start(bf16[8,160,384]{2,1,0:T(8,128)(2,1)S(1)} %get-tuple-element.193), channel_id=1, source_target_pairs={{0,2},{1,3},{2,0},{3,1},{4,6},{5,7},{6,4},{7,5},{8,10},{9,11},{10,... | collective-permute-start | bytes 2949128 | tf_op jit(solution)/shard_map/ppermute | solution.py:939
  524.8 63.0 %collective-permute-start.8 = (bf16[512,768]{1,0:T(8,128)(2,1)S(1)}, bf16[512,768]{1,0:T(8,128)(2,1)S(1)}, u32[]{:S(2)}, u32[]{:S(2)}) collective-permute-start(bf16[512,768]{1,0:T(8,128)(2,1)S(1)} %get-tuple-element.211), channel_id=1, source_target_pairs={{0,17},{1,16},{16,1},{17,0},{2,19},{3,18},{18,3},{19,2},{4,21},{5,... | collective-permute-start | bytes 2359304 | tf_op jit(solution)/shard_map/ppermute | solution.py:1051
  537.6 2.9 copy-start.1
  540.2 76.4 %collective-permute-start.15 = (bf16[4,448,384]{2,1,0:T(8,128)(2,1)S(1)}, bf16[4,448,384]{2,1,0:T(8,128)(2,1)S(1)}, u32[]{:S(2)}, u32[]{:S(2)}) collective-permute-start(bf16[4,448,384]{2,1,0:T(8,128)(2,1)S(1)} %get-tuple-element.187), channel_id=1, source_target_pairs={{0,1},{1,0},{2,3},{3,2},{4,5},{5,4},{6,7},{7,6},{8,9},{9,8},{10,11... | collective-permute-start | bytes 4128776 | tf_op jit(solution)/shard_map/ppermute | solution.py:939
  543.0 49.0 %collective-permute-start.20 = (bf16[4,160,384]{2,1,0:T(8,128)(2,1)S(1)}, bf16[4,160,384]{2,1,0:T(8,128)(2,1)S(1)}, u32[]{:S(2)}, u32[]{:S(2)}) collective-permute-start(bf16[4,160,384]{2,1,0:T(8,128)(2,1)S(1)} %get-tuple-element.221), channel_id=1, source_target_pairs={{0,1},{1,0},{2,3},{3,2},{4,5},{5,4},{6,7},{7,6},{8,9},{9,8},{10,11... | collective-permute-start | bytes 1474568 | tf_op jit(solution)/shard_map/ppermute | solution.py:939
  544.9 72.6 %collective-permute-start.25 = (bf16[4,448,384]{2,1,0:T(8,128)(2,1)S(1)}, bf16[4,448,384]{2,1,0:T(8,128)(2,1)S(1)}, u32[]{:S(2)}, u32[]{:S(2)}) collective-permute-start(bf16[4,448,384]{2,1,0:T(8,128)(2,1)S(1)} %get-tuple-element.189), channel_id=1, source_target_pairs={{0,1},{1,0},{2,3},{3,2},{4,5},{5,4},{6,7},{7,6},{8,9},{9,8},{10,11... | collective-permute-start | bytes 4128776 | tf_op jit(solution)/shard_map/ppermute | solution.py:939
  545.4 66.6 %collective-permute-start.30 = (bf16[4,160,384]{2,1,0:T(8,128)(2,1)S(1)}, bf16[4,160,384]{2,1,0:T(8,128)(2,1)S(1)}, u32[]{:S(2)}, u32[]{:S(2)}) collective-permute-start(bf16[4,160,384]{2,1,0:T(8,128)(2,1)S(1)} %get-tuple-element.223), channel_id=1, source_target_pairs={{0,1},{1,0},{2,3},{3,2},{4,5},{5,4},{6,7},{7,6},{8,9},{9,8},{10,11... | collective-permute-start | bytes 1474568 | tf_op jit(solution)/shard_map/ppermute | solution.py:939
  592.2 21.7 %collective-permute-start.21 = (bf16[2,160,384]{2,1,0:T(8,128)(2,1)S(1)}, bf16[2,160,384]{2,1,0:T(8,128)(2,1)S(1)}, u32[]{:S(2)}, u32[]{:S(2)}) collective-permute-start(bf16[2,160,384]{2,1,0:T(8,128)(2,1)S(1)} %get-tuple-element.225), channel_id=1, source_target_pairs={{0,4},{1,5},{2,6},{3,7},{4,0},{5,1},{6,2},{7,3},{8,12},{9,13},{10,... | collective-permute-start | bytes 737288 | tf_op jit(solution)/shard_map/ppermute | solution.py:939
  612.2 13.1 %collective-permute-start.31 = (bf16[2,160,384]{2,1,0:T(8,128)(2,1)S(1)}, bf16[2,160,384]{2,1,0:T(8,128)(2,1)S(1)}, u32[]{:S(2)}, u32[]{:S(2)}) collective-permute-start(bf16[2,160,384]{2,1,0:T(8,128)(2,1)S(1)} %get-tuple-element.227), channel_id=1, source_target_pairs={{0,4},{1,5},{2,6},{3,7},{4,0},{5,1},{6,2},{7,3},{8,12},{9,13},{10,... | collective-permute-start | bytes 737288 | tf_op jit(solution)/shard_map/ppermute | solution.py:939
  613.9 13.2 %collective-permute-start.22 = (bf16[1,160,384]{2,1,0:T(8,128)(2,1)S(1)}, bf16[1,160,384]{2,1,0:T(8,128)(2,1)S(1)}, u32[]{:S(2)}, u32[]{:S(2)}) collective-permute-start(bf16[1,160,384]{2,1,0:T(8,128)(2,1)S(1)} %add_convert_fusion.27), channel_id=1, source_target_pairs={{0,8},{1,9},{2,10},{3,11},{4,12},{5,13},{6,14},{7,15},{8,0},{9,1},... | collective-permute-start | bytes 368648 | tf_op jit(solution)/shard_map/ppermute | solution.py:939
  616.9 21.4 %collective-permute-start.16 = (bf16[2,448,384]{2,1,0:T(8,128)(2,1)S(1)}, bf16[2,448,384]{2,1,0:T(8,128)(2,1)S(1)}, u32[]{:S(2)}, u32[]{:S(2)}) collective-permute-start(bf16[2,448,384]{2,1,0:T(8,128)(2,1)S(1)} %get-tuple-element.217), channel_id=1, source_target_pairs={{0,4},{1,5},{2,6},{3,7},{4,0},{5,1},{6,2},{7,3},{8,12},{9,13},{10,... | collective-permute-start | bytes 2064392 | tf_op jit(solution)/shard_map/ppermute | solution.py:939
  617.8 31.7 %collective-permute-start.26 = (bf16[2,448,384]{2,1,0:T(8,128)(2,1)S(1)}, bf16[2,448,384]{2,1,0:T(8,128)(2,1)S(1)}, u32[]{:S(2)}, u32[]{:S(2)}) collective-permute-start(bf16[2,448,384]{2,1,0:T(8,128)(2,1)S(1)} %get-tuple-element.219), channel_id=1, source_target_pairs={{0,4},{1,5},{2,6},{3,7},{4,0},{5,1},{6,2},{7,3},{8,12},{9,13},{10,... | collective-permute-start | bytes 2064392 | tf_op jit(solution)/shard_map/ppermute | solution.py:939
  625.3 25.1 %collective-permute-start.32 = (bf16[1,160,384]{2,1,0:T(8,128)(2,1)S(1)}, bf16[1,160,384]{2,1,0:T(8,128)(2,1)S(1)}, u32[]{:S(2)}, u32[]{:S(2)}) collective-permute-start(bf16[1,160,384]{2,1,0:T(8,128)(2,1)S(1)} %add_convert_fusion.26), channel_id=1, source_target_pairs={{0,8},{1,9},{2,10},{3,11},{4,12},{5,13},{6,14},{7,15},{8,0},{9,1},... | collective-permute-start | bytes 368648 | tf_op jit(solution)/shard_map/ppermute | solution.py:939
  638.4 12.1 %collective-permute-start.17 = (bf16[1,448,384]{2,1,0:T(8,128)(2,1)S(1)}, bf16[1,448,384]{2,1,0:T(8,128)(2,1)S(1)}, u32[]{:S(2)}, u32[]{:S(2)}) collective-permute-start(bf16[1,448,384]{2,1,0:T(8,128)(2,1)S(1)} %add_convert_fusion.21), channel_id=1, source_target_pairs={{0,8},{1,9},{2,10},{3,11},{4,12},{5,13},{6,14},{7,15},{8,0},{9,1},... | collective-permute-start | bytes 1032200 | tf_op jit(solution)/shard_map/ppermute | solution.py:939
  649.6 11.6 %collective-permute-start.27 = (bf16[1,448,384]{2,1,0:T(8,128)(2,1)S(1)}, bf16[1,448,384]{2,1,0:T(8,128)(2,1)S(1)}, u32[]{:S(2)}, u32[]{:S(2)}) collective-permute-start(bf16[1,448,384]{2,1,0:T(8,128)(2,1)S(1)} %add_convert_fusion.20), channel_id=1, source_target_pairs={{0,8},{1,9},{2,10},{3,11},{4,12},{5,13},{6,14},{7,15},{8,0},{9,1},... | collective-permute-start | bytes 1032200 | tf_op jit(solution)/shard_map/ppermute | solution.py:939
  661.4 5.4 collective-permute-start.33

commit v2 on v1

--- a/solution.py
+++ b/solution.py
@@ -446,31 +446,60 @@
     return high, middle, low
 
 
+JOINT_BIAS, OUTPUT_BIAS, UP_BIAS, DOWN_BIAS, FIRST_GAIN, INNER_GAIN, SECOND_GAIN, HIDDEN_GAIN = range(8)
+
+
+def vectors_of(pack_ref, width, *numbers):
+    wide = 4 * width
+    lengths = (3 * width, width, wide, width, width, width, width, wide)
+    views = []
+    for number in numbers:
+        views.append(pack_ref.at[0, :, pl.ds(sum(lengths[:number]), lengths[number])])
+    return views
+
+
+def pack_spec(layer, pack):
+    return pl.BlockSpec((1, 1, pack.shape[-1]), lambda *_: (layer, 0, 0))
+
+
 def fetch_weights(layer, sec_ref, pairs, sem):
-    @pl.when(pl.program_id(0) == 0)
+    first = pl.program_id(0) == 0
+
+    @pl.when(first & (sec_ref[0] == layer))
     def _():
-        @pl.when(sec_ref[0] == layer)
+        for index, (own, other, here) in enumerate(pairs):
+            pltpu.make_async_copy(own, here, sem.at[index]).start()
+
+    @pl.when(first & (sec_ref[0] != layer))
+    def _():
+        for index, (own, other, here) in enumerate(pairs):
+            pltpu.make_async_copy(other, here, sem.at[index]).start()
+
+    def arrive(index):
+        @pl.when(first)
         def _():
-            for index, (own, other, here) in enumerate(pairs):
-                pltpu.make_async_copy(own, here, sem.at[index]).start()
-
-        @pl.when(sec_ref[0] != layer)
-        def _():
-            for index, (own, other, here) in enumerate(pairs):
-                pltpu.make_async_copy(other, here, sem.at[index]).start()
-
-        for index, (own, other, here) in enumerate(pairs):
+            own, other, here = pairs[index]
             pltpu.make_async_copy(own, here, sem.at[index]).wait()
 
-
-def qkv_kernel(layer, sec_ref, x_ref, gain_ref, own_ref, other_ref, bias_ref, cos_ref, sin_ref,
-               lab_ref, n_ref, q_ref, k_ref, v_ref, w_ref, sem):
-    fetch_weights(layer, sec_ref, [(own_ref, other_ref, w_ref)], sem)
+    return arrive
+
+
+def gelu_parts(value):
+    share = 0.5 + 0.5 * lax.erf(value * 0.5 ** 0.5)
+    bell = jnp.exp2(value * value * (-0.5 * math.log2(math.e)))
+    return value * share, share + value * bell * (1.0 / math.sqrt(2.0 * math.pi))
+
+
+def qkv_kernel(layer, blocks, sec_ref, mine_ref, x_ref, y_ref, pack_ref, own_ref, other_ref, cos_ref, sin_ref,
+               lab_ref, s_ref, n_ref, q_ref, k_ref, v_ref, w_ref, sem):
+    arrive = fetch_weights(layer, sec_ref, [(own_ref, other_ref, w_ref)], sem)
     width = x_ref.shape[-1]
-    unit, scale = normalize(x_ref[...].astype(F32))
+    gain_ref, bias_ref = vectors_of(pack_ref, width, FIRST_GAIN, JOINT_BIAS)
+    state = jnp.where(jnp.full((1, 1), pl.program_id(0)) < blocks, x_ref[0], y_ref[...])
+    s_ref[...] = state
+    unit, scale = normalize(state.astype(F32))
     normed = (unit * gain_ref[...]).astype(BF16)
     n_ref[...] = normed
-    joint = nn(normed, w_ref[...]) + bias_ref[...]
     cosine, sine = cos_ref[...], sin_ref[...]
     lane = lane_iota(cosine.shape)
     first = lane % HEAD_DIM < HEAD_DIM // 2
@@ -482,58 +511,97 @@
     ones = (document >= 5) & (document < 8)
     k_feat = jnp.where((known & (document == labels)) | ones, 1.0, 0.0)
     v_feat = jnp.where((document >= 0) & (document < 3), 1.0, 0.0)
-    for pair in range(width // 128):
-        for which, (out, feat) in enumerate(((q_ref, q_feat), (k_ref, k_feat), (v_ref, v_feat))):
-            begin = which * width + pair * 128
-            part = joint[:, begin:begin + 128]
+    kinds = ((q_ref, q_feat), (k_ref, k_feat), (v_ref, v_feat))
+    step = 256
+    chunks = 3 * width // step
+
+    def product(chunk):
+        at = pl.ds(chunk * step, step)
+        return nn(normed, w_ref[:, at]) + bias_ref[:, at]
+
+    arrive(0)
+    later = product(0)
+    for chunk in range(chunks):
+        joint = later
+        if chunk + 1 < chunks:
+            later = product(chunk + 1)
+        for sub in range(step // 128):
+            pair = chunk * step // 128 + sub
+            which = pair * 128 // width
+            out, feat = kinds[which]
+            pair = pair - which * width // 128
+            part = joint[:, sub * 128:(sub + 1) * 128]
             if which < 2:
                 turned = jnp.where(first, pltpu.roll(part, 96, 1), pltpu.roll(part, 32, 1))
                 part = part * cosine + turned * sine
-            part = part.astype(BF16).astype(F32)
             if which == 0:
                 part = part * HEAD_DIM ** -0.5
             out[2 * pair] = jnp.where(head, part, feat).astype(BF16)
             out[2 * pair + 1] = jnp.where(head, pltpu.roll(part, 64, 1), feat).astype(BF16)
 
 
-def qkv(layer, sec, x, gain, own, other, bias, cosine, sine, labels, tb=256):
-    rows, width = x.shape
+def qkv(layer, sec, x, pack, own, other, cosine, sine, labels, mine, tb=256):
+    if isinstance(x, tuple):
+        x, y = x
+        blocks = x.shape[1] // tb
+        rows, width = 2 * x.shape[1], x.shape[2]
+    else:
+        rows, width = x.shape
+        blocks = rows // tb
+        x, y = x[None], x
+        mine = jnp.int32(0)
     heads = width // HEAD_DIM
-    const = lambda shape: pl.BlockSpec(shape, lambda i: (0,) * len(shape))
-    tok = lambda n: pl.BlockSpec((tb, n), lambda i: (i, 0))
-    hd = pl.BlockSpec((heads, tb, 128), lambda i: (0, i, 0))
+    const = lambda shape: pl.BlockSpec(shape, lambda i, s, m: (0,) * len(shape))
+    tok = lambda n: pl.BlockSpec((tb, n), lambda i, s, m: (i, 0))
+    hd = pl.BlockSpec((heads, tb, 128), lambda i, s, m: (0, i, 0))
     return pl.pallas_call(
-        functools.partial(qkv_kernel, layer),
-        grid=(rows // tb,),
-        in_specs=[SMEM, tok(width), const((1, width)), ANY, ANY, const((1, 3 * width)), tok(128), tok(128), tok(1)],
-        out_specs=[tok(width), hd, hd, hd],
-        out_shape=[jax.ShapeDtypeStruct((rows, width), BF16)] + [jax.ShapeDtypeStruct((heads, rows, 128), BF16)] * 3,
-        scratch_shapes=[pltpu.VMEM(own.shape, BF16), pltpu.SemaphoreType.DMA((1,))],
+        functools.partial(qkv_kernel, layer, blocks),
+        grid_spec=pltpu.PrefetchScalarGridSpec(
+            num_scalar_prefetch=2,
+            grid=(rows // tb,),
+            in_specs=[pl.BlockSpec((1, tb, width), lambda i, s, m: (m[0], jnp.minimum(i, blocks - 1), 0)),
+                      pl.BlockSpec((tb, width), lambda i, s, m: (jnp.maximum(i - blocks, 0), 0)),
+                      pack_spec(layer, pack), ANY, ANY, tok(128), tok(128), tok(128)],
+            out_specs=[tok(width), tok(width), hd, hd, hd],
+            scratch_shapes=[pltpu.VMEM(own.shape, BF16), pltpu.SemaphoreType.DMA((1,))],
+        ),
+        out_shape=[jax.ShapeDtypeStruct((rows, width), BF16)] * 2 + [jax.ShapeDtypeStruct((heads, rows, 128), BF16)] * 3,
         compiler_params=pltpu.CompilerParams(vmem_limit_bytes=VLIM),
         cost_estimate=pl.CostEstimate(flops=2 * rows * width * 3 * width, bytes_accessed=16 * 1024 * 1024, transcendentals=0),
         name="joint_projection",
-    )(sec, x, gain, own, other, bias, cosine, sine, labels)
+    )(sec, mine.reshape(1).astype(jnp.int32), x, y, pack, own, other, cosine, sine, labels)
 
 
 def attend_kernel(qb, q_ref, k_ref, v_ref, o_ref, ql_ref):
     rows = q_ref.shape[1]
     lane = lane_iota((qb, 128))
-    for block in range(rows // qb):
+    inside = (lane >= 69) & (lane < 72)
+    work = [(head, block) for block in range(rows // qb) for head in range(2)]
+    ready = {}
+
+    def score(index):
+        if index < len(work):
+            head, block = work[index]
+            ready[index] = nt(q_ref[head, pl.ds(block * qb, qb), :], k_ref[head])
+
+    score(0)
+    score(1)
+    done = []
+    for index, (head, block) in enumerate(work):
+        score(index + 2)
+        scores = ready.pop(index)
         at = pl.ds(block * qb, qb)
-        done = []
-        for head in range(2):
-            query = q_ref[head, at, :]
-            scores = nt(query, k_ref[head])
-            peak = jnp.max(scores, axis=-1, keepdims=True)
-            raised = jnp.exp(scores - peak).astype(BF16)
-            sums = nn(raised, v_ref[head])
-            total = sums[:, HEAD_DIM:HEAD_DIM + 1]
-            done.append(sums / total)
-            high, middle, low = split3(-(peak + jnp.log(total)))
-            feat = jnp.where(lane == 69, high.astype(F32), jnp.where(lane == 70, middle.astype(F32), low.astype(F32)))
-            inside = (lane >= 69) & (lane < 72)
-            ql_ref[head, at, :] = jnp.where(inside, feat, query.astype(F32)).astype(BF16)
-        o_ref[at, :] = jnp.where(lane < HEAD_DIM, done[0], pltpu.roll(done[1], 64, 1))
+        peak = jnp.max(scores, axis=-1, keepdims=True)
+        raised = jnp.exp(scores - peak).astype(BF16)
+        sums = nn(raised, v_ref[head])
+        total = sums[:, HEAD_DIM:HEAD_DIM + 1]
+        done.append(sums * (1.0 / total))
+        high, middle, low = split3(-(peak + jnp.log(total)))
+        feat = jnp.where(lane == 69, high.astype(F32), jnp.where(lane == 70, middle.astype(F32), low.astype(F32)))
+        ql_ref[head, at, :] = jnp.where(inside, feat, q_ref[head, at, :].astype(F32)).astype(BF16)
+        if head == 1:
+            o_ref[at, :] = jnp.where(lane < HEAD_DIM, done[0], pltpu.roll(done[1], 64, 1))
+            done = []
 
 
 def attend(q, k, v, qb=256):
@@ -551,187 +619,262 @@
     )(q, k, v)
 
 
-def feed_kernel(layer, sec_ref, at_ref, x_ref, ig_ref, ob_ref, sg_ref, ub_ref, hg_ref, db_ref,
+def feed_kernel(layer, sec_ref, at_ref, x_ref, pack_ref,
                 wo0, wo1, wu0, wu1, wd0, wd1,
-                out_ref, mixed_ref, hid_ref, gp_ref, st_ref, wo, wu, wd, sem):
-    fetch_weights(layer, sec_ref, [(wo0, wo1, wo), (wu0, wu1, wu), (wd0, wd1, wd)], sem)
+                out_ref, mixed_ref, hid_ref, gp_ref, st_ref, wo, wu, wd, bent, sem):
+    arrive = fetch_weights(layer, sec_ref, [(wo0, wo1, wo), (wu0, wu1, wu), (wd0, wd1, wd)], sem)
+    ig_ref, ob_ref, sg_ref, ub_ref, hg_ref, db_ref = vectors_of(
+        pack_ref, x_ref.shape[-1], INNER_GAIN, OUTPUT_BIAS, SECOND_GAIN, UP_BIAS, HIDDEN_GAIN, DOWN_BIAS)
+    wide = hg_ref.shape[-1]
     unit, _ = normalize(at_ref[...])
     inner = (unit * ig_ref[...]).astype(BF16)
+    arrive(0)
     mixed = x_ref[...].astype(F32) + nn(inner, wo[...]) + ob_ref[...]
     mixed_ref[...] = mixed
     unit, _ = normalize(mixed)
     normed = (unit * sg_ref[...]).astype(BF16)
-    before = nn(normed, wu[...]) + ub_ref[...]
-    share = 0.5 + 0.5 * lax.erf(before * 0.5 ** 0.5)
-    bell = jnp.exp(before * before * -0.5) * (1.0 / math.sqrt(2.0 * math.pi))
-    gp_ref[...] = (share + before * bell).astype(BF16)
-    unit, scale = normalize(before * share)
-    hidden = (unit * hg_ref[...]).astype(BF16)
-    hid_ref[...] = hidden
+    step = 512
+    chunks = wide // step
+
+    def rise(chunk):
+        at = pl.ds(chunk * step, step)
+        return nn(normed, wu[:, at]) + ub_ref[:, at]
+
+    arrive(1)
+    later = rise(0)
+    total = 0.0
+    for chunk in range(chunks):
+        before = later
+        if chunk + 1 < chunks:
+            later = rise(chunk + 1)
+        at = pl.ds(chunk * step, step)
+        value, bend = gelu_parts(before)
+        gp_ref[:, at] = bend.astype(BF16)
+        bent[:, at] = value
+        total = total + jnp.sum(value, axis=-1, keepdims=True)
+    mean = total * (1.0 / wide)
+    spread = 0.0
+    for chunk in range(chunks):
+        centered = bent[:, pl.ds(chunk * step, step)] - mean
+        spread = spread + jnp.sum(centered * centered, axis=-1, keepdims=True)
+    scale = lax.rsqrt(spread * (1.0 / wide) + EPSILON)
     st_ref[...] = jnp.broadcast_to(scale, st_ref.shape)
-    out_ref[...] = (mixed + nn(hidden, wd[...]) + db_ref[...]).astype(BF16)
-
-
-def feed(layer, sec, attended, x, ig, ob, sg, ub, hg, db, wo, wu, wd, tb=256):
+    arrive(2)
+    result = mixed + db_ref[...]
+    for chunk in range(chunks):
+        at = pl.ds(chunk * step, step)
+        hidden = ((bent[:, at] - mean) * scale * hg_ref[:, at]).astype(BF16)
+        hid_ref[:, at] = hidden
+    result = result + nn(hid_ref[...], wd[...])
+    out_ref[...] = result.astype(BF16)
+
+
+def feed(layer, sec, attended, x, pack, wo, wu, wd, tb=512):
     rows, width = x.shape
-    wide = ub.shape[-1]
-    const = lambda n: pl.BlockSpec((1, n), lambda i: (0, 0))
+    wide = wd[0].shape[0]
     tok = lambda n: pl.BlockSpec((tb, n), lambda i: (i, 0))
     S = jax.ShapeDtypeStruct
     return pl.pallas_call(
         functools.partial(feed_kernel, layer),
         grid=(rows // tb,),
-        in_specs=[SMEM, tok(width), tok(width), const(width), const(width), const(width), const(wide), const(wide), const(width)] + [ANY] * 6,
+        in_specs=[SMEM, tok(width), tok(width), pack_spec(layer, pack)] + [ANY] * 6,
         out_specs=[tok(width), tok(width), tok(wide), tok(wide), tok(128)],
         out_shape=[S((rows, width), BF16), S((rows, width), F32), S((rows, wide), BF16), S((rows, wide), BF16), S((rows, 128), F32)],
-        scratch_shapes=[pltpu.VMEM(wo[0].shape, BF16), pltpu.VMEM(wu[0].shape, BF16), pltpu.VMEM(wd[0].shape, BF16), pltpu.SemaphoreType.DMA((3,))],
+        scratch_shapes=[pltpu.VMEM(wo[0].shape, BF16), pltpu.VMEM(wu[0].shape, BF16), pltpu.VMEM(wd[0].shape, BF16), pltpu.VMEM((tb, wide), F32), pltpu.SemaphoreType.DMA((3,))],
         compiler_params=pltpu.CompilerParams(vmem_limit_bytes=VLIM),
         cost_estimate=pl.CostEstimate(flops=2 * rows * width * (2 * wide + width), bytes_accessed=40 * 1024 * 1024, transcendentals=0),
         name="feed_forward",
-    )(sec, attended, x, ig, ob, sg, ub, hg, db, *wo, *wu, *wd)
+    )(sec, attended, x, pack, *wo, *wu, *wd)
 
 
 def feed_back_kernel(layer, sec_ref, c_ref, hid_ref, gp_ref, st_ref, mixed_ref, at_ref,
-                     ig_ref, sg_ref, hg_ref, wo0, wo1, wu0, wu1, wd0, wd1,
+                     pack_ref, wo0, wo1, wu0, wu1, wd0, wd1,
                      cb_ref, cm_ref, cl_ref, ch_ref, n2_ref, in_ref, wide_ref, thin_ref,
-                     wo, wu, wd, wide_acc, thin_acc, sem):
-    step = pl.program_id(0)
-
-    @pl.when(step == 0)
+                     wo, wu, wd, sloped, wide_acc, thin_acc, sem):
+    now = pl.program_id(0)
+    ig_ref, sg_ref, hg_ref = vectors_of(pack_ref, c_ref.shape[-1], INNER_GAIN, SECOND_GAIN, HIDDEN_GAIN)
+
+    @pl.when(now == 0)
     def _():
         wide_acc[...] = jnp.zeros_like(wide_acc)
         thin_acc[...] = jnp.zeros_like(thin_acc)
 
-    fetch_weights(layer, sec_ref, [(wo0, wo1, wo), (wu0, wu1, wu), (wd0, wd1, wd)], sem)
+    arrive = fetch_weights(layer, sec_ref, [(wo0, wo1, wo), (wu0, wu1, wu), (wd0, wd1, wd)], sem)
     low = c_ref[...]
     outer = low.astype(F32)
     thin_acc[0] += fold(outer)
-    slope = nt(low, wd[...])
-    hidden = hid_ref[...].astype(F32)
-    gain = hg_ref[...]
-    moved = slope * hidden
-    wide_acc[0] += fold(moved)
-    mean_moved = jnp.mean(moved, axis=-1, keepdims=True)
-    slope = slope * gain
-    mean_slope = jnp.mean(slope, axis=-1, keepdims=True)
+    wide = hg_ref.shape[-1]
+    step = 512
+    chunks = wide // step
+
+    def fall(chunk):
+        return nt(low, wd[pl.ds(chunk * step, step), :])
+
+    arrive(2)
+    later = fall(0)
+    sum_moved = 0.0
+    sum_slope = 0.0
+    for chunk in range(chunks):
+        slope = later
+        if chunk + 1 < chunks:
+            later = fall(chunk + 1)
+        at = pl.ds(chunk * step, step)
+        moved = slope * hid_ref[:, at].astype(F32)
+        wide_acc[0, :, at] += fold(moved)
+        sum_moved = sum_moved + jnp.sum(moved, axis=-1, keepdims=True)
+        slope = slope * hg_ref[:, at]
+        sum_slope = sum_slope + jnp.sum(slope, axis=-1, keepdims=True)
+        sloped[:, at] = slope
     scale = st_ref[:, 0:1]
-    slope = (slope - mean_slope - hidden * (1.0 / gain) * mean_moved) * scale
-    before_low = (slope * gp_ref[...].astype(F32)).astype(BF16)
-    cb_ref[...] = before_low
-    wide_acc[1] += fold(before_low.astype(F32))
-    slope = nt(before_low, wu[...])
+    mean_moved = sum_moved * (1.0 / wide)
+    mean_slope = sum_slope * (1.0 / wide)
+    arrive(1)
+    slope_two = 0.0
+    for chunk in range(chunks):
+        at = pl.ds(chunk * step, step)
+        unit = hid_ref[:, at].astype(F32) * (1.0 / hg_ref[:, at])
+        slope = (sloped[:, at] - mean_slope - unit * mean_moved) * scale
+        before_low = (slope * gp_ref[:, at].astype(F32)).astype(BF16)
+        cb_ref[:, at] = before_low
+        wide_acc[1, :, at] += fold(before_low.astype(F32))
+        slope_two = slope_two + nt(before_low, wu[:, at])
     unit, scale = normalize(mixed_ref[...])
     n2_ref[...] = (unit * sg_ref[...]).astype(BF16)
-    thin_acc[1] += fold(slope * unit)
-    mixed = outer + norm_back(slope * sg_ref[...], unit, scale)
+    thin_acc[1] += fold(slope_two * unit)
+    mixed = outer + norm_back(slope_two * sg_ref[...], unit, scale)
     cm_ref[...] = mixed
     mixed_low = mixed.astype(BF16)
     cl_ref[...] = mixed_low
     thin_acc[2] += fold(mixed_low.astype(F32))
+    arrive(0)
     slope = nt(mixed_low, wo[...])
     unit, scale = normalize(at_ref[...])
     in_ref[...] = (unit * ig_ref[...]).astype(BF16)
     thin_acc[3] += fold(slope * unit)
     ch_ref[...] = norm_back(slope * ig_ref[...], unit, scale).astype(BF16)
 
-    @pl.when(step == pl.num_programs(0) - 1)
+    @pl.when(now == pl.num_programs(0) - 1)
     def _():
-        inverse = 1.0 / gain
+        inverse = 1.0 / hg_ref[...]
         wide_ref[0:1, :] = jnp.sum(wide_acc[0], axis=0, keepdims=True) * inverse
         wide_ref[1:2, :] = jnp.sum(wide_acc[1], axis=0, keepdims=True)
         for index in range(4):
             thin_ref[index:index + 1, :] = jnp.sum(thin_acc[index], axis=0, keepdims=True)
 
 
-def feed_back(layer, sec, c, hidden, gp, st, mixed, attended, ig, sg, hg, wo, wu, wd, tb=256):
+def feed_back(layer, sec, c, hidden, gp, st, mixed, attended, pack, wo, wu, wd, tb=256):
     rows, width = c.shape
-    wide = hg.shape[-1]
+    wide = wd[0].shape[0]
     const = lambda n, m=1: pl.BlockSpec((m, n), lambda i: (0, 0))
     tok = lambda n: pl.BlockSpec((tb, n), lambda i: (i, 0))
     S = jax.ShapeDtypeStruct
     return pl.pallas_call(
         functools.partial(feed_back_kernel, layer),
         grid=(rows // tb,),
-        in_specs=[SMEM, tok(width), tok(wide), tok(wide), tok(128), tok(width), tok(width), const(width), const(width), const(wide)] + [ANY] * 6,
+        in_specs=[SMEM, tok(width), tok(wide), tok(wide), tok(128), tok(width), tok(width), pack_spec(layer, pack)] + [ANY] * 6,
         out_specs=[tok(wide), tok(width), tok(width), tok(width), tok(width), tok(width), const(wide, 2), const(width, 4)],
         out_shape=[S((rows, wide), BF16), S((rows, width), F32), S((rows, width), BF16), S((rows, width), BF16), S((rows, width), BF16), S((rows, width), BF16), S((2, wide), F32), S((4, width), F32)],
         scratch_shapes=[pltpu.VMEM(wo[0].shape, BF16), pltpu.VMEM(wu[0].shape, BF16), pltpu.VMEM(wd[0].shape, BF16),
-                        pltpu.VMEM((2, 8, wide), F32), pltpu.VMEM((4, 8, width), F32), pltpu.SemaphoreType.DMA((3,))],
+                        pltpu.VMEM((tb, wide), F32), pltpu.VMEM((2, 8, wide), F32), pltpu.VMEM((4, 8, width), F32), pltpu.SemaphoreType.DMA((3,))],
         compiler_params=pltpu.CompilerParams(vmem_limit_bytes=VLIM),
         cost_estimate=pl.CostEstimate(flops=2 * rows * width * (2 * wide + width), bytes_accessed=50 * 1024 * 1024, transcendentals=0),
         name="feed_backward",
-    )(sec, c, hidden, gp, st, mixed, attended, ig, sg, hg, *wo, *wu, *wd)
-
-
-def attend_back_kernel(qb, q_ref, k_ref, v_ref, ch_ref, at_ref, cos_ref, sin_ref, cj_ref, kt, vt, qs):
+    )(sec, c, hidden, gp, st, mixed, attended, pack, *wo, *wu, *wd)
+
+
+def attend_back_kernel(qb, q_ref, k_ref, v_ref, ch_ref, at_ref, cos_ref, sin_ref, cj_ref, kt, vt, qs, shares_ref, slope_ref):
     rows = q_ref.shape[1]
     lane = lane_iota((rows, 128))
     is_head = lane < HEAD_DIM
     slopes = ch_ref[...].astype(F32)
     product = slopes * at_ref[...]
+    incoming = []
     for head in range(2):
         mine = is_head if head == 0 else jnp.logical_not(is_head)
         weighted = jnp.sum(jnp.where(mine, product, 0.0), axis=-1, keepdims=True)
         high, middle, low = split3(-weighted)
         feat = jnp.where(lane == 64, high.astype(F32), jnp.where(lane == 65, middle.astype(F32), jnp.where(lane == 66, low.astype(F32), 0.0)))
         local = slopes if head == 0 else pltpu.roll(slopes, 64, 1)
-        c_aug = jnp.where(is_head, local, feat).astype(BF16)
-        keys, values = k_ref[head], v_ref[head]
-        for block in range(rows // qb):
-            at = pl.ds(block * qb, qb)
-            query = q_ref[head, at, :]
-            incoming = c_aug[block * qb:(block + 1) * qb, :]
-            shares = jnp.exp(nt(query, keys))
-            slope = (shares * nt(incoming, values)).astype(BF16)
-            qs[head, at, :] = nn(slope, keys)
-            key_part = tn(query, slope)[:HEAD_DIM]
-            value_part = tn(incoming, shares.astype(BF16))[:HEAD_DIM]
+        incoming.append(jnp.where(is_head, local, feat).astype(BF16))
+    blocks = rows // qb
+    work = [(head, block) for head in range(2) for block in range(blocks)]
+    ready = {}
+
+    def score(index):
+        if index < len(work):
+            head, block = work[index]
+            at = block * qb
+            ready[index] = (
+                nt(q_ref[head, pl.ds(at, qb), :], k_ref[head]),
+                nt(incoming[head][at:at + qb], v_ref[head]),
+            )
+
+    score(0)
+    for index, (head, block) in enumerate(work):
+        score(index + 1)
+        scores, turned = ready.pop(index)
+        shares = jnp.exp(scores)
+        slope = (shares * turned).astype(BF16)
+        at = pl.ds(block * qb, qb)
+        slope_ref[head, at, :] = slope
+        shares_ref[head, at, :] = shares.astype(BF16)
+        qs[head, at, :] = nn(slope, k_ref[head])
+        if block == blocks - 1:
             rng = pl.ds(head * HEAD_DIM, HEAD_DIM)
-            if block == 0:
-                kt[rng, :] = key_part
-                vt[rng, :] = value_part
-            else:
-                kt[rng, :] += key_part
-                vt[rng, :] += value_part
+            kt[rng, :] = nn(q_ref[head].T[:HEAD_DIM], slope_ref[head])
+            vt[rng, :] = nn(incoming[head].T[:HEAD_DIM], shares_ref[head])
     cosine, sine = cos_ref[...], sin_ref[...]
     first = lane % HEAD_DIM < HEAD_DIM // 2
+
     def back(part):
         turned = jnp.where(first, pltpu.roll(part, 96, 1), pltpu.roll(part, 32, 1))
         return (part * cosine - turned * sine).astype(BF16)
+
     cj_ref[0] = back(jnp.where(is_head, qs[0], pltpu.roll(qs[1], 64, 1)) * HEAD_DIM ** -0.5)
     cj_ref[1] = back(kt[...].T)
     cj_ref[2] = vt[...].T.astype(BF16)
 
 
-def attend_back(q, k, v, ch, attended, cosine, sine, qb=256):
+def attend_back(q, k, v, ch, attended, cosine, sine, begin=0, count=None, into=None, qb=256):
     heads, rows, _ = q.shape
     width = heads * HEAD_DIM
-    hd = pl.BlockSpec((2, rows, 128), lambda i: (i, 0, 0))
-    col = pl.BlockSpec((rows, 128), lambda i: (0, i))
+    count = heads // 2 - begin if count is None else count
+    hd = pl.BlockSpec((2, rows, 128), lambda i: (i + begin, 0, 0))
+    col = pl.BlockSpec((rows, 128), lambda i: (0, i + begin))
     con = pl.BlockSpec((rows, 128), lambda i: (0, 0))
+    body = functools.partial(attend_back_kernel, qb)
+    extra = () if into is None else (into,)
+
+    def kernel(*refs):
+        body(*refs[:7], *refs[7 + len(extra):])
+
     return pl.pallas_call(
-        functools.partial(attend_back_kernel, qb),
-        grid=(heads // 2,),
-        in_specs=[hd, hd, hd, col, col, con, con],
-        out_specs=pl.BlockSpec((3, rows, 128), lambda i: (0, 0, i)),
+        kernel,
+        grid=(count,),
+        in_specs=[hd, hd, hd, col, col, con, con] + [ANY] * len(extra),
+        out_specs=pl.BlockSpec((3, rows, 128), lambda i: (0, 0, i + begin)),
         out_shape=jax.ShapeDtypeStruct((3, rows, width), BF16),
-        scratch_shapes=[pltpu.VMEM((128, rows), F32), pltpu.VMEM((128, rows), F32), pltpu.VMEM((2, rows, 128), F32)],
+        input_output_aliases={7: 0} if extra else {},
+        scratch_shapes=[pltpu.VMEM((128, rows), F32), pltpu.VMEM((128, rows), F32), pltpu.VMEM((2, rows, 128), F32),
+                        pltpu.VMEM((2, rows, rows), BF16), pltpu.VMEM((2, rows, rows), BF16)],
         compiler_params=pltpu.CompilerParams(vmem_limit_bytes=VLIM),
-        cost_estimate=pl.CostEstimate(flops=40 * heads * rows * rows * HEAD_DIM, bytes_accessed=20 * 1024 * 1024, transcendentals=0),
+        cost_estimate=pl.CostEstimate(flops=80 * count * rows * rows * HEAD_DIM, bytes_accessed=3 * count * 1024 * 1024, transcendentals=0),
         name="attention_backward",
-    )(q, k, v, ch, attended, cosine, sine)
-
-
-def qkv_back_kernel(layer, sec_ref, cj_ref, x_ref, cm_ref, gain_ref, own_ref, other_ref,
+    )(q, k, v, ch, attended, cosine, sine, *extra)
+
+
+def qkv_back_kernel(layer, sec_ref, cj_ref, x_ref, cm_ref, pack_ref, own_ref, other_ref,
                     ci_ref, small_ref, w_ref, acc, sem):
     step = pl.program_id(0)
-    fetch_weights(layer, sec_ref, [(own_ref, other_ref, w_ref)], sem)
+    arrive = fetch_weights(layer, sec_ref, [(own_ref, other_ref, w_ref)], sem)
 
     @pl.when(step == 0)
     def _():
         acc[...] = jnp.zeros_like(acc)
 
     width = x_ref.shape[-1]
+    (gain_ref,) = vectors_of(pack_ref, width, FIRST_GAIN)
+    arrive(0)
     slope = nt(cj_ref[0], w_ref[:, 0:width])
     for which in range(1, 3):
         slope = slope + nt(cj_ref[which], w_ref[:, which * width:(which + 1) * width])
@@ -747,7 +890,7 @@
             small_ref[index:index + 1, :] = jnp.sum(acc[index], axis=0, keepdims=True)
 
 
-def qkv_back(layer, sec, cj, x, cm, gain, own, other, tb=256):
+def qkv_back(layer, sec, cj, x, cm, pack, own, other, tb=256):
     rows, width = x.shape
     const = lambda n, m=1: pl.BlockSpec((m, n), lambda i: (0, 0))
     tok = lambda n: pl.BlockSpec((tb, n), lambda i: (i, 0))
@@ -755,29 +898,17 @@
     return pl.pallas_call(
         functools.partial(qkv_back_kernel, layer),
         grid=(rows // tb,),
-        in_specs=[SMEM, pl.BlockSpec((3, tb, width), lambda i: (0, i, 0)), tok(width), tok(width), const(width), ANY, ANY],
+        in_specs=[SMEM, pl.BlockSpec((3, tb, width), lambda i: (0, i, 0)), tok(width), tok(width), pack_spec(layer, pack), ANY, ANY],
         out_specs=[tok(width), const(width, 4)],
         out_shape=[S((rows, width), BF16), S((4, width), F32)],
         scratch_shapes=[pltpu.VMEM(own.shape, BF16), pltpu.VMEM((4, 8, width), F32), pltpu.SemaphoreType.DMA((1,))],
         compiler_params=pltpu.CompilerParams(vmem_limit_bytes=VLIM),
         cost_estimate=pl.CostEstimate(flops=2 * rows * width * 3 * width, bytes_accessed=16 * 1024 * 1024, transcendentals=0),
         name="joint_backward",
-    )(sec, cj, x, cm, gain, own, other)
-
-
-def tables(labels, places):
-    half = HEAD_DIM // 2
-    lane = jnp.arange(128)
-    rate = 1.0 / 10000.0 ** (jnp.arange(half, dtype=F32) * 2.0 / HEAD_DIM)
-    angle = places.astype(F32)[:, None] * jnp.tile(rate, 4)[None, :]
-    sign = jnp.where(lane % HEAD_DIM < half, -1.0, 1.0).astype(F32)
-    return jnp.cos(angle), jnp.sin(angle) * sign
-
-
-SIZES = ("joint_bias", "output_bias", "up_bias", "down_bias", "first_gain", "inner_gain", "second_gain", "hidden_gain")
-
-
-def feed_grads_kernel(sec_ref, order_ref, cb_ref, hid_ref, c_ref, n2_ref, cm_ref, in_ref, small_ref,
+    )(sec, cj, x, cm, pack, own, other)
+
+
+def feed_grads_kernel(sec_ref, order_ref, cb_ref, hid_ref, c_ref, n2_ref, cm_ref, in_ref, wide_ref, thin_ref,
                       keep_ref, send_ref, c_t, cm_t):
     step = pl.program_id(0)
     sec = sec_ref[0]
@@ -787,44 +918,42 @@
     thin = c_ref.shape[-1] // parts
     steps = pl.num_programs(0) // 2
     outs = (keep_ref, send_ref)
+    sides = [pl.ds(pl.multiple_of(which * half, 128), half) for which in (sec, 1 - sec)]
 
     @pl.when(step == 0)
     def _():
         c_t[...] = c_ref[...].T
         cm_t[...] = cm_ref[...].T
-        for side in range(2):
-            which = sec if side == 0 else 1 - sec
-            for part in range(parts):
-                at = order_ref[side * parts + part]
-                row = small_ref[pl.ds(which * parts + part, 1), 0, :]
-                outs[side][at, up_rows * 2 + thin:, :] = jnp.broadcast_to(row, (16, half)).astype(BF16)
-
-    both = tn(cb_ref[...], n2_ref[...])
-    left, right = both[:, :half], both[:, half:]
-    flip = jnp.full((1, 1), sec) == 0
-    sides = (jnp.where(flip, left, right).astype(BF16), jnp.where(flip, right, left).astype(BF16))
+        for window in range(parts // 2):
+            at = pl.ds(window * half, half)
+            far = pl.ds(window // (parts // 4) * half, half)
+            rows = jnp.concatenate([wide_ref[:, at], thin_ref[:, far], jnp.zeros((10, half), F32)], axis=0).astype(BF16)
+            for side in range(2):
+                for sub in range(2):
+                    outs[side][order_ref[side * parts + window * 2 + sub], up_rows * 2 + thin:, :] = rows
+
     for side in range(2):
+        up = tn(cb_ref[...], n2_ref[:, sides[side]]).astype(BF16)
         for sub in range(2):
             at = order_ref[side * parts + step * 2 + sub]
-            outs[side][at, 0:up_rows, :] = sides[side][sub * up_rows:(sub + 1) * up_rows]
+            outs[side][at, 0:up_rows, :] = up[sub * up_rows:(sub + 1) * up_rows]
 
     down = nn(c_t[...], hid_ref[...]).astype(BF16)
+    rows = pl.ds(pl.multiple_of(up_rows + thin * (step % steps), 16), thin)
     for side in range(2):
         @pl.when(step // steps == side)
         def _():
-            rows = pl.ds(pl.multiple_of(up_rows + thin * (step % steps), 16), thin)
             for part in range(parts):
                 outs[side][order_ref[side * parts + part], rows, :] = down[thin * part:thin * (part + 1)]
 
         @pl.when(step == side * steps)
         def _():
-            which = sec if side == 0 else 1 - sec
-            out = nn(cm_t[...], in_ref[:, pl.ds(pl.multiple_of(which * half, 128), half)]).astype(BF16)
+            out = nn(cm_t[...], in_ref[:, sides[side]]).astype(BF16)
             for part in range(parts):
                 outs[side][order_ref[side * parts + part], 2 * up_rows:2 * up_rows + thin, :] = out[thin * part:thin * (part + 1)]
 
 
-def feed_grads(sec, order, cb, hidden, c, n2, cm, inner, small):
+def feed_grads(sec, order, cb, hidden, c, n2, cm, inner, wide_sums, thin_sums):
     rows, width = c.shape
     wide = cb.shape[-1]
     parts = order.shape[0] // 2
@@ -832,7 +961,7 @@
     steps = wide // half
     up_rows = wide // parts
     total = 2 * up_rows + width // parts + 16
-    full = lambda n: pl.BlockSpec((rows, n), lambda i, s, o: (0, 0))
+    full = lambda n, m=rows: pl.BlockSpec((m, n), lambda i, s, o: (0, 0))
     out_spec = pl.BlockSpec((parts, total, half), lambda i, s, o: (0, 0, 0))
     out_shape = jax.ShapeDtypeStruct((parts, total, half), BF16)
     return pl.pallas_call(
@@ -843,8 +972,7 @@
             in_specs=[
                 pl.BlockSpec((rows, half), lambda i, s, o: (0, i)),
                 pl.BlockSpec((rows, half), lambda i, s, o: (0, jnp.where(i < steps // 2, s[0], 1 - s[0]) * (steps // 2) + i % (steps // 2))),
-                full(width), full(width), full(width), full(width),
-                pl.BlockSpec((2 * parts, 1, half), lambda i, s, o: (0, 0, 0)),
+                full(width), full(width), full(width), full(width), full(wide, 2), full(width, 4),
             ],
             out_specs=[out_spec, out_spec],
             scratch_shapes=[pltpu.VMEM((width, rows), BF16), pltpu.VMEM((width, rows), BF16)],
@@ -853,32 +981,40 @@
         compiler_params=pltpu.CompilerParams(vmem_limit_bytes=VLIM),
         cost_estimate=pl.CostEstimate(flops=2 * rows * width * (2 * wide + width), bytes_accessed=30 * 1024 * 1024, transcendentals=0),
         name="feed_gradients",
-    )(sec, order, cb, hidden, c, n2, cm, inner, small)
-
-
-def joint_grads_kernel(sec_ref, order_ref, cj_ref, n_ref, small_ref, keep_ref, send_ref, acc):
+    )(sec, order, cb, hidden, c, n2, cm, inner, wide_sums, thin_sums)
+
+
+def joint_grads_kernel(sec_ref, order_ref, cj_ref, n_ref, sums_ref, keep_ref, send_ref):
     step = pl.program_id(0)
     sec = sec_ref[0]
     parts = order_ref.shape[0] // 2
     width = n_ref.shape[-1]
     half = width // 2
-    thick = acc.shape[0] // parts
+    thick = 3 * width // parts
     outs = (keep_ref, send_ref)
-    acc[pl.ds(pl.multiple_of(step * width, 16), width), :] = tn(cj_ref[0], n_ref[...]).astype(BF16)
-
-    @pl.when(step == pl.num_programs(0) - 1)
+    for side, which in enumerate((sec, 1 - sec)):
+        sums = tn(cj_ref[0], n_ref[:, pl.ds(pl.multiple_of(which * half, 128), half)]).astype(BF16)
+        for block in range(3):
+            @pl.when(step == block)
+            def _():
+                for part in range(parts):
+                    low, high = max(thick * part, width * block), min(thick * (part + 1), width * (block + 1))
+                    if low < high:
+                        at = order_ref[side * parts + part]
+                        outs[side][at, low - thick * part:high - thick * part, :] = sums[low - width * block:high - width * block]
+
+    @pl.when(step == 0)
     def _():
-        for side in range(2):
-            which = sec if side == 0 else 1 - sec
-            columns = pl.ds(pl.multiple_of(which * half, 128), half)
-            for part in range(parts):
-                at = order_ref[side * parts + part]
-                outs[side][at, 0:thick, :] = acc[thick * part:thick * (part + 1), columns]
-                row = small_ref[pl.ds(which * parts + part, 1), 0, :]
-                outs[side][at, thick:, :] = jnp.broadcast_to(row, (16, half)).astype(BF16)
-
-
-def joint_grads(sec, order, cj, normed, small):
+        for part in range(parts):
+            window = thick * part // half
+            rows = [sums_ref[1 + w // 2:2 + w // 2, w % 2 * half:w % 2 * half + half] for w in (window, min(window + 1, 5))]
+            far = part // (parts // 2) * half
+            rows = jnp.concatenate(rows + [sums_ref[0:1, far:far + half], jnp.zeros((13, half), F32)], axis=0).astype(BF16)
+            for side in range(2):
+                outs[side][order_ref[side * parts + part], thick:, :] = rows
+
+
+def joint_grads(sec, order, cj, normed, sums):
     rows, width = normed.shape
     parts = order.shape[0] // 2
     half = width // 2
@@ -893,23 +1029,60 @@
             in_specs=[
                 pl.BlockSpec((1, rows, width), lambda i, s, o: (i, 0, 0)),
                 pl.BlockSpec((rows, width), lambda i, s, o: (0, 0)),
-                pl.BlockSpec((2 * parts, 1, half), lambda i, s, o: (0, 0, 0)),
+                pl.BlockSpec((4, width), lambda i, s, o: (0, 0)),
             ],
             out_specs=[out_spec, out_spec],
-            scratch_shapes=[pltpu.VMEM((3 * width, width), BF16)],
         ),
         out_shape=[out_shape, out_shape],
         compiler_params=pltpu.CompilerParams(vmem_limit_bytes=VLIM),
         cost_estimate=pl.CostEstimate(flops=6 * rows * width * width, bytes_accessed=14 * 1024 * 1024, transcendentals=0),
         name="joint_gradients",
-    )(sec, order, cj, normed, small)
-
-
-def small_rows(items, parts, half):
-    lined = jnp.concatenate([item.reshape(parts, -1) for item in items], axis=1)
-    lined = lined.reshape(parts, 2, -1).transpose(1, 0, 2)
-    lined = jnp.pad(lined, ((0, 0), (0, 0), (0, half - lined.shape[-1])))
-    return lined.reshape(2 * parts, 1, half)
+    )(sec, order, cj, normed, sums)
+
+
+def prepare_kernel(lengths, mine_ref, part_ref, seg_ref, rate_ref, *refs):
+    vectors, (cos_ref, sin_ref, lab_ref, pack_ref) = refs[:len(lengths)], refs[len(lengths):]
+    begin = 0
+    for vector, length in zip(vectors, lengths):
+        pack_ref[:, begin:begin + length] = vector[...]
+        begin += length
+    rows = seg_ref.shape[-1]
+    piece = rows // 2
+    second = jnp.full((1, 1), part_ref[0]) == 1
+    row = seg_ref[0].astype(F32)
+    turned = jnp.where(second, jnp.concatenate([row[:, piece:], row[:, :piece]], axis=1), row)
+    labels = jnp.broadcast_to(turned, (128, rows)).T
+    starts = jnp.zeros_like(labels)
+    for document in range(1, 5):
+        count = jnp.sum(jnp.where(row < document, 1.0, 0.0), axis=1, keepdims=True)
+        starts = jnp.where(labels == document, count, starts)
+    time = lax.broadcasted_iota(jnp.int32, labels.shape, 0).astype(F32)
+    shift = jnp.where(second, jnp.where(time < piece, piece * 1.0, -piece * 1.0), 0.0)
+    angle = (time + shift - starts) * rate_ref[...]
+    lane = lane_iota(labels.shape)
+    cos_ref[...] = jnp.cos(angle)
+    sin_ref[...] = jnp.sin(angle) * jnp.where(lane % HEAD_DIM < HEAD_DIM // 2, -1.0, 1.0)
+    lab_ref[...] = labels.astype(jnp.int32)
+
+
+def prepare(mine, part, segments, vectors):
+    rows = segments.shape[-1]
+    lengths = tuple(vector.shape[-1] for vector in vectors)
+    half = HEAD_DIM // 2
+    rate = jnp.tile(1.0 / 10000.0 ** (jnp.arange(half, dtype=F32) * 2.0 / HEAD_DIM), 4)[None]
+    whole = lambda m, n: pl.BlockSpec((m, n), lambda i, a, b: (0, 0))
+    return pl.pallas_call(
+        functools.partial(prepare_kernel, lengths),
+        grid_spec=pltpu.PrefetchScalarGridSpec(
+            num_scalar_prefetch=2,
+            grid=(1,),
+            in_specs=[pl.BlockSpec((1, 1, rows), lambda i, a, b: (a[0], 0, 0)), whole(1, 128)] + [whole(1, length) for length in lengths],
+            out_specs=[whole(rows, 128), whole(rows, 128), whole(rows, 128), whole(1, sum(lengths))],
+        ),
+        out_shape=[jax.ShapeDtypeStruct((rows, 128), F32)] * 2 + [jax.ShapeDtypeStruct((rows, 128), jnp.int32), jax.ShapeDtypeStruct((1, sum(lengths)), F32)],
+        compiler_params=pltpu.CompilerParams(vmem_limit_bytes=VLIM),
+        name="row_tables",
+    )(mine.reshape(1).astype(jnp.int32), part.reshape(1).astype(jnp.int32), segments, rate, *vectors)
 
 
 def swap_pairs(change, sizes):
@@ -923,22 +1096,64 @@
     return pairs
 
 
-def reduce_chunks(kept, sent, sizes):
-    every = ("section", "dp", "seq")
-    moves = (
-        lambda s, d, q: (s, d ^ 1, q) if s == 0 else (s, d, q ^ 1),
-        lambda s, d, q: (s, d, q ^ 1) if s == 0 else (s, d ^ 1, q),
-        lambda s, d, q: (s, d ^ 2, q),
-        lambda s, d, q: (s, d ^ 4, q),
-    )
-    arrived = lax.ppermute(sent, "section", [(0, 1), (1, 0)])
-    for move in moves:
+FEED, JOINT = range(2)
+
+
+class Reduction:
+    def __init__(self, kept, sent, sizes):
+        self.sizes = sizes
+        self.kept, self.sent = kept, sent
+        self.stage = 0
+        self.result = None
+
+    def send(self):
+        if self.stage == 0:
+            self.arrived = lax.ppermute(self.sent, "section", [(0, 1), (1, 0)])
+        else:
+            moves = (
+                lambda s, d, q: (s, d ^ 1, q) if s == 0 else (s, d, q ^ 1),
+                lambda s, d, q: (s, d, q ^ 1) if s == 0 else (s, d ^ 1, q),
+                lambda s, d, q: (s, d ^ 2, q),
+                lambda s, d, q: (s, d ^ 4, q),
+            )
+            self.arrived = lax.ppermute(self.sent, ("section", "dp", "seq"), swap_pairs(moves[self.stage - 1], self.sizes))
+        self.stage += 1
+
+    def add(self):
+        kept, arrived = self.kept, self.arrived
         middle = kept.shape[0] // 2
-        sent = (kept[middle:].astype(F32) + arrived[middle:].astype(F32)).astype(BF16)
-        held = kept[:middle].astype(F32) + arrived[:middle].astype(F32)
-        arrived = lax.ppermute(sent, every, swap_pairs(move, sizes))
-        kept = held if middle == 1 else held.astype(BF16)
-    return kept[0] + arrived[0].astype(F32)
+        if middle == 0:
+            self.result = kept[0].astype(F32) + arrived[0].astype(F32)
+            return
+        self.sent = (kept[middle:].astype(F32) + arrived[middle:].astype(F32)).astype(BF16)
+        self.kept = (kept[:middle].astype(F32) + arrived[:middle].astype(F32)).astype(BF16)
+
+    def finish(self):
+        if self.result is not None:
+            return self.result
+        while self.stage < 5:
+            self.add()
+            self.send()
+        self.add()
+        return self.result
+
+
+def advance(value, *moving):
+    for item in moving:
+        if item.stage:
+            item.add()
+    if all(item.stage == 5 for item in moving):
+        results = [item.result for item in moving]
+        value, results = lax.optimization_barrier((value, results))
+        for item, result in zip(moving, results):
+            item.result = result
+        return value
+    parts = [array for item in moving for array in (item.kept, item.sent)]
+    value, parts = lax.optimization_barrier((value, parts))
+    for index, item in enumerate(moving):
+        item.kept, item.sent = parts[2 * index:2 * index + 2]
+        item.send()
+    return value
 
 
 def row_step(
@@ -974,24 +1189,14 @@
     def pick(array, index):
         return lax.dynamic_index_in_dim(array, index, 0, keepdims=False)
 
-    flat = tokens.reshape(micro * row_count, piece, width)
-    beside = lax.ppermute(pick(flat, mine ^ 1), "seq", swap)
-    state = jnp.concatenate([pick(flat, mine), beside], axis=0)
+    flat_tokens = tokens.reshape(micro * row_count, piece, width)
+    beside = lax.ppermute(pick(flat_tokens, mine ^ 1), "seq", swap)
     both = [(own[0], lax.ppermute(own[0], "section", swap)) for own in (joint_weight, output_weight, up_weight, down_weight)]
     joint_pair, output_pair, up_pair, down_pair = both
-    own = jnp.concatenate([joint_bias, output_bias, up_bias, down_bias, first_gain, inner_gain, second_gain, hidden_gain], axis=1)
+    cosine, sine, labels, own = prepare(mine, part, segments.reshape(micro * row_count, 1, rows), (
+        joint_bias, output_bias, up_bias, down_bias, first_gain, inner_gain, second_gain, hidden_gain))
     other = lax.ppermute(own, "section", swap)
-    packs = (jnp.where(section == 0, own, other), jnp.where(section == 0, other, own))
-    flat = cotangent.reshape(micro * row_count, piece, width)
-    beside = lax.ppermute(pick(flat, mine ^ 1), "seq", swap)
-    slope = jnp.concatenate([pick(flat, mine), beside], axis=0)
-
-    whole = pick(segments.reshape(micro * row_count, rows), mine)
-    starts = jnp.sum((whole[None, :] < whole[:, None]).astype(jnp.int32), axis=1)
-    places = jnp.arange(rows, dtype=jnp.int32) - starts
-    turn = lambda a: jnp.where(part == 0, a, jnp.roll(a, piece))
-    cosine, sine = tables(None, turn(places))
-    labels = turn(whole).reshape(rows, 1)
+    pack = jnp.where(section == 0, jnp.stack([own, other]), jnp.stack([other, own]))
 
     mx, my, mz = data % 2, part, data // 2
     index = jnp.arange(parts, dtype=jnp.int32)
@@ -1000,66 +1205,96 @@
     order_x, order_y = (cx * 2 + cy) * 4 + depth, (cy * 2 + cx) * 4 + depth
     order = jnp.where(section == 0, jnp.concatenate([order_x, order_y]), jnp.concatenate([order_y, order_x]))
 
-    lengths = (3 * width, width, wide, width, width, width, width, wide)
-
-    def cut(pack, which):
-        begin = sum(lengths[:which])
-        return pack[:, begin:begin + lengths[which]]
-
     kept = []
     hiddens = []
     for layer in range(2):
-        pack = packs[layer]
-        jb, ob, ub, db, fg, ig, sg, hg = (cut(pack, which) for which in range(8))
-        normed, q, k, v = qkv(layer, sec, state, fg, *joint_pair, jb, cosine, sine, labels)
+        if layer == 0:
+            state, normed, q, k, v = qkv(layer, sec, (flat_tokens, beside), pack, *joint_pair, cosine, sine, labels, mine)
+            state, cotangent = lax.optimization_barrier((state, cotangent))
+            flat = cotangent.reshape(micro * row_count, piece, width)
+            slope = jnp.concatenate([pick(flat, mine), lax.ppermute(pick(flat, mine ^ 1), "seq", swap)], axis=0)
+        else:
+            _, normed, q, k, v = qkv(layer, sec, state, pack, *joint_pair, cosine, sine, labels, mine)
         attended, query = attend(q, k, v)
-        result, mixed, hidden, bend, stats = feed(layer, sec, attended, state, ig, ob, sg, ub, hg, db, output_pair, up_pair, down_pair)
+        result, mixed, hidden, bend, stats = feed(layer, sec, attended, state, pack, output_pair, up_pair, down_pair)
         kept.append((state, normed, query, k, v, attended, mixed, hidden, bend, stats))
         hiddens.append(result)
         state = result
 
-    done = [None, None]
-    grads = [None, None]
+    def halves(item):
+        return item[:piece], item[piece:]
+
+    every = ("section", "seq")
+    blocks = []
+    for fs, fq in ((0, 1), (1, 0), (1, 1)):
+        first, second = (halves(item)[fq] for item in hiddens)
+        owed = jnp.where(section == fs, first, second)
+        blocks.append((owed, [(2 * s + q, 2 * (s ^ fs) + (q ^ fq)) for s in range(2) for q in range(2)]))
+    slope, owed = lax.optimization_barrier((slope, [block for block, pairs in blocks]))
+    gathered = [lax.ppermute(block, every, pairs) for block, (_, pairs) in zip(owed, blocks)]
+    own = jnp.where(section == 0, halves(hiddens[0])[0], halves(hiddens[1])[0])
+
+    def place(blocks):
+        stacked = jnp.stack(blocks)
+        return jnp.stack([pick(stacked, mine ^ index) for index in range(4)]).reshape(1, micro, row_count, piece, width)
+
+    def deliver(layer, back):
+        own, other = halves(back)
+        moves = (
+            (other, [(2 * layer + q, 2 * layer + (q ^ 1)) for q in range(2)]),
+            (own, [(2 * (1 - layer) + q, 2 * layer + q) for q in range(2)]),
+            (other, [(2 * (1 - layer) + q, 2 * layer + (q ^ 1)) for q in range(2)]),
+        )
+        return [own] + [lax.ppermute(block, every, pairs) for block, pairs in moves]
+
+    flights = {}
+    delivered = [None, None]
+
     for layer in (1, 0):
-        pack = packs[layer]
-        jb, ob, ub, db, fg, ig, sg, hg = (cut(pack, which) for which in range(8))
         state, normed, query, k, v, attended, mixed, hidden, bend, stats = kept[layer]
         cb, cm, cm_low, ch, n2, inner, wide_sums, thin_sums = feed_back(
-            layer, sec, slope, hidden, bend, stats, mixed, attended, ig, sg, hg, output_pair, up_pair, down_pair)
-        small = small_rows((thin_sums[2], wide_sums[1], thin_sums[0], thin_sums[3], thin_sums[1], wide_sums[0]), parts, half)
-        feed_part = reduce_chunks(*feed_grads(sec, order, cb, hidden, slope, n2, cm_low, inner, small), sizes)
-        cj = attend_back(query, k, v, ch, attended, cosine, sine)
-        back, sums = qkv_back(layer, sec, cj, state, cm, fg, *joint_pair)
-        small = small_rows((sums[1:].reshape(-1), sums[0]), parts, half)
-        joint_part = reduce_chunks(*joint_grads(sec, order, cj, normed, small), sizes)
-        grads[layer] = jnp.concatenate([feed_part, joint_part], axis=0)
-        done[layer] = back
+            layer, sec, slope, hidden, bend, stats, mixed, attended, pack, output_pair, up_pair, down_pair)
+        if layer == 0:
+            cb = advance(cb, flights[FEED, 1], flights[JOINT, 1])
+        flights[FEED, layer] = Reduction(*feed_grads(sec, order, cb, hidden, slope, n2, cm_low, inner, wide_sums, thin_sums), sizes)
+        if layer == 1:
+            ch = advance(ch, flights[FEED, 1])
+            cj = attend_back(query, k, v, ch, attended, cosine, sine)
+            cj, gathered = lax.optimization_barrier((cj, gathered))
+            cj = advance(cj, flights[FEED, 1])
+        else:
+            ch, delivered[1] = lax.optimization_barrier((ch, delivered[1]))
+            ch = advance(ch, flights[FEED, 0], flights[FEED, 1], flights[JOINT, 1])
+            count = query.shape[0] // 4
+            cj = attend_back(query, k, v, ch, attended, cosine, sine, 0, count)
+            cj = advance(cj, flights[FEED, 0], flights[FEED, 1], flights[JOINT, 1])
+            cj = attend_back(query, k, v, ch, attended, cosine, sine, count, None, cj)
+            cj = advance(cj, flights[FEED, 1])
+            cj = advance(cj, flights[JOINT, 1], flights[FEED, 0])
+        back, sums = qkv_back(layer, sec, cj, state, cm, pack, *joint_pair)
+        delivered[layer] = deliver(layer, back)
+        if layer == 0:
+            cj = advance(cj, flights[JOINT, 1])
+            cj = advance(cj, flights[FEED, 0])
+        flights[JOINT, layer] = Reduction(*joint_grads(sec, order, cj, normed, sums), sizes)
+        if layer == 1:
+            back = advance(back, flights[JOINT, 1])
         slope = back
-
-    def spread(pieces):
-        every = ("section", "seq")
-        got = [None] * 4
-        for fs in range(2):
-            for fq in range(2):
-                owed = [item[piece * fq:piece * (fq + 1)] for item in pieces]
-                if fs == 0:
-                    block = jnp.where(section == 0, owed[0], owed[1])
-                else:
-                    block = jnp.where(section == 0, owed[1], owed[0])
-                if fs or fq:
-                    pairs = [(2 * s + q, 2 * (s ^ fs) + (q ^ fq)) for s in range(2) for q in range(2)]
-                    block = lax.ppermute(block, every, pairs)
-                got[2 * fs + fq] = block
-        stacked = jnp.stack(got)
-        return jnp.stack([pick(stacked, mine ^ index) for index in range(4)]).reshape(1, micro, row_count, piece, width)
-
-    hiddens = spread(hiddens)
-    input_gradients = spread(done).astype(F32)
-
-    ours = jnp.where(section == 0, grads[0], grads[1])
-    theirs = lax.ppermute(jnp.where(section == 0, grads[1], grads[0]), "section", swap)
-    left = jnp.where(section == 0, ours, theirs)
-    right = jnp.where(section == 0, theirs, ours)
+    last, before = flights[JOINT, 0], flights[FEED, 0]
+    last.send()
+    last.add()
+    before.kept, _ = lax.optimization_barrier((before.kept, last.sent))
+    last.send()
+    hiddens = place([own] + gathered)
+    input_gradients = place([jnp.where(section == 0, a, b) for a, b in zip(*delivered)]).astype(F32)
+
+    def settle(name):
+        grads = [flights[name, layer].finish() for layer in range(2)]
+        ours = jnp.where(section == 0, grads[0], grads[1])
+        theirs = lax.ppermute(jnp.where(section == 0, grads[1], grads[0]), "section", swap)
+        return jnp.where(section == 0, ours, theirs), jnp.where(section == 0, theirs, ours)
+
+    left, right = settle(FEED)
     up_rows, thin, thick = wide // parts, width // parts, 3 * width // parts
 
     def rows_of(begin, count):
@@ -1073,17 +1308,18 @@
     at += up_rows
     output_grad = rows_of(at, thin).T
     at += thin
-    sizes_small = (thin, up_rows, thin, thin, thin, up_rows)
-    used = sum(sizes_small) // 2
-    line = jnp.concatenate([left[at, :used], right[at, :used]])
-    at += 16
-    ends = [sum(sizes_small[:i + 1]) for i in range(len(sizes_small))]
-    ob, ub, db, ig, sg, hg = (line[end - size:end] for end, size in zip(ends, sizes_small))
-    joint_grad = rows_of(at, thick).T
-    at += thick
-    used = (thick + thin) // 2
-    line = jnp.concatenate([left[at, :used], right[at, :used]])
-    jb, fg = line[:thick], line[thick:]
+    index = 2 * data + part
+
+    def piece_of(row, count):
+        return lax.dynamic_slice_in_dim(row, index * count % half, count)
+
+    hg, ub = (piece_of(left[at + number], up_rows) for number in range(2))
+    db, sg, ob, ig = (piece_of(left[at + 2 + number], thin) for number in range(4))
+    left, right = settle(JOINT)
+    joint_grad = rows_of(0, thick).T
+    at = thick
+    jb = lax.dynamic_slice_in_dim(jnp.concatenate([left[at], left[at + 1]]), index * thick % half, thick)
+    fg = piece_of(left[at + 2], thin)
     return (
         hiddens,
         input_gradients,

time: 685 us -> 547 us (0.80)
  waiting for transfers between devices: 186 us -> 65.5 us
  local copies, waits for them, and re-layouts: 33.4 us -> 16.1 us
    ppermute x29 -> x33, waiting for transfers between devices: 186 us -> 56.5 us  [the longest x16 49.4 us: send(): lax.ppermute(self.sent, ('section', 'dp', 'seq'), swap_pairs(moves[self.s...]
    pallas_call x2, Pallas kernels: 54 us -> 41.3 us  [attend(): pl.pallas_call(functools.partial(attend_kernel, qb), grid=(heads // 2,),...]
    pallas_call x4 -> x6, Pallas kernels: 93.8 us -> 104 us  [the longest x3 73.9 us: attend_back(): pl.pallas_call(kernel, grid=(count,), in_specs=[hd, hd, hd, col, col, con...]
    convert_element_type x18 -> x17, other arithmetic: 27.6 us -> 37.4 us  [the longest x13 32.1 us: add(): (kept[middle:].astype(F32) + arrived[middle:].astype(F32)).astype(BF16)]
    pallas_call x2, Pallas kernels: 59.2 us -> 49.5 us  [feed(): pl.pallas_call(functools.partial(feed_kernel, layer), grid=(rows // tb,),...]
    ppermute x1, waiting for transfers between devices: 0.01 us -> 8.99 us  [row_step(): other = lax.ppermute(own, 'section', swap)]
    slice x18 -> x3, local copies, waits for them, and re-layouts: 10.1 us -> 2.69 us  [the longest x1 2.66 us: halves(): return (item[:piece], item[piece:])]
    ppermute x29 -> x33, starting transfers between devices: 40.2 us -> 41.8 us  [the longest x16 20.9 us: send(): lax.ppermute(self.sent, ('section', 'dp', 'seq'), swap_pairs(moves[self.s...]
  transfers between devices with their start and end apart: 34 -> 38, of which waited for: 10 -> 11; matrix products, arithmetic and copies ran while one was open for 10% -> 8% of each run, Pallas kernels for 19% -> 38%
where the time goes in v2:
time: 547 us; the launch traced here: 540 us
  Pallas kernels  355 us (65%)
  waiting for transfers between devices  65.5 us (12%)
  other arithmetic  57.6 us (11%)
  starting transfers between devices  43.4 us (8%)
  local copies, waits for them, and re-layouts  16.1 us (3%)
    pallas_call x3, Pallas kernels, attend_back(): pl.pallas_call(kernel, grid=(count,), in_specs=[hd, hd, hd, col, col, con...  73.9 us
    pallas_call x2, Pallas kernels, feed_back(): pl.pallas_call(functools.partial(feed_back_kernel, layer), grid=(rows //...  63.1 us
    pallas_call x2, Pallas kernels, feed_grads(): pl.pallas_call(feed_grads_kernel, grid_spec=pltpu.PrefetchScalarGridSpec(...  53.2 us
    pallas_call x2, Pallas kernels, feed(): pl.pallas_call(functools.partial(feed_kernel, layer), grid=(rows // tb,),...  49.5 us
    ppermute x16, waiting for transfers between devices, send(): lax.ppermute(self.sent, ('section', 'dp', 'seq'), swap_pairs(moves[self.s...  49.4 us
    pallas_call x2, Pallas kernels, attend(): pl.pallas_call(functools.partial(attend_kernel, qb), grid=(heads // 2,),...  41.3 us
    convert_element_type x13, other arithmetic, add(): (kept[middle:].astype(F32) + arrived[middle:].astype(F32)).astype(BF16)  32.1 us
    pallas_call x2, Pallas kernels, qkv(): pl.pallas_call(functools.partial(qkv_kernel, layer, blocks), grid_spec=pl...  25.8 us
  transfers between devices with their start and end apart: 38, of which 11 were waited for; matrix products, arithmetic and copies ran while one was open for 8% of the time, Pallas kernels for 38%

profile of v2, /device:TPU:0, one launch (start us, length us, event | category | flops | bytes accessed | tf_op | source)
XLA Modules:
  0.0 539.6 jit_solution(5310821731291874995)
XLA Ops:
  1.7 2.1 dynamic-slice_bitcast_fusion.6
  3.7 2.6 collective-permute-start
  6.9 4.2 row_tables.1
  11.9 9.0 %collective-permute-done.1 = f32[1,12288]{1,0:T(1,128)} collective-permute-done((f32[1,12288]{1,0:T(1,128)}, f32[1,12288]{1,0:T(1,128)}, u32[]{:S(2)}, u32[]{:S(2)}) %collective-permute-start.1) | collective-permute-done | bytes 49184 | tf_op jit(solution)/shard_map/ppermute | solution.py:1198
  21.3 1.7 broadcast_select_fusion.5.pack_ref
  23.0 1.8 collective-permute-done.y_ref
  24.8 1.8 copy-done
  26.6 12.9 %joint_projection.2 = (bf16[1024,768]{1,0:T(8,128)(2,1)}, bf16[1024,768]{1,0:T(8,128)(2,1)}, bf16[12,1024,128]{2,1,0:T(8,128)(2,1)}, bf16[12,1024,128]{2,1,0:T(8,128)(2,1)}, bf16[12,1024,128]{2,1,0:T(8,128)(2,1)}) custom-call(s32[1]{0:T(128)} %bitcast.sec_ref, s32[1]{0:T(128)} %bitcast.1.mine_ref, bf16[4,512,768]{2,1,0:T(8,128)(2,1)} %bitcast.110, ...), custom_call_target="tpu_custom_call" | custom-call | flops 3623878656 | bytes 16777216 | tf_op jit(solution)/shard_map/joint_projection/pallas_call | solution.py:557
  39.4 1.5 dynamic-slice_bitcast_fusion.5
  40.9 1.8 collective-permute-start.6
  42.7 20.5 %attention_forward.2 = (f32[1024,768]{1,0:T(8,128)}, bf16[12,1024,128]{2,1,0:T(8,128)(2,1)}) custom-call(bf16[12,1024,128]{2,1,0:T(8,128)(2,1)} %get-tuple-element.129.q_ref, bf16[12,1024,128]{2,1,0:T(8,128)(2,1)} %get-tuple-element.130.k_ref.refs_1_, bf16[12,1024,128]{2,1,0:T(8,128)(2,1)} %get-tuple-element.131.v_ref.refs_2_), custom_call_target="tpu_custom_call" | custom-call | flops 12884901888 | bytes 16777216 | tf_op jit(solution)/shard_map/attention_forward/pallas_call | solution.py:610
  63.3 1.3 pad_maximum_fusion.2.c_ref
  64.6 24.7 %feed_forward.2 = (bf16[1024,768]{1,0:T(8,128)(2,1)}, f32[1024,768]{1,0:T(8,128)}, bf16[1024,3072]{1,0:T(8,128)(2,1)}, bf16[1024,3072]{1,0:T(8,128)(2,1)}, f32[1024,128]{1,0:T(8,128)}) custom-call(s32[1]{0:T(128)} %bitcast.sec_ref, f32[1024,768]{1,0:T(8,128)} %get-tuple-element.132.at_ref.refs_4_, bf16[1024,768]{1,0:T(8,128)(2,1)} %get-tuple-element.134.x_ref, ...), custom_call_target="tpu_custom_call" | custom-call | flops 10871635968 | bytes 41943040 | tf_op jit(solution)/shard_map/feed_forward/pallas_call | solution.py:677
  89.3 13.0 %joint_projection.3 = (bf16[1024,768]{1,0:T(8,128)(2,1)}, bf16[1024,768]{1,0:T(8,128)(2,1)}, bf16[12,1024,128]{2,1,0:T(8,128)(2,1)}, bf16[12,1024,128]{2,1,0:T(8,128)(2,1)}, bf16[12,1024,128]{2,1,0:T(8,128)(2,1)}) custom-call(s32[1]{0:T(128)} %bitcast.sec_ref, s32[1]{0:T(128)} %constant.155.clone.1.mine_ref, bf16[1,1024,768]{2,1,0:T(8,128)(2,1)} %bitcast.97, ...), custom_call_target="tpu_custom_call" | custom-call | flops 3623878656 | bytes 16777216 | tf_op jit(solution)/shard_map/joint_projection/pallas_call | solution.py:557
  102.3 20.8 %attention_forward.3 = (f32[1024,768]{1,0:T(8,128)}, bf16[12,1024,128]{2,1,0:T(8,128)(2,1)}) custom-call(bf16[12,1024,128]{2,1,0:T(8,128)(2,1)} %get-tuple-element.136.q_ref, bf16[12,1024,128]{2,1,0:T(8,128)(2,1)} %get-tuple-element.137.k_ref.refs_1_, bf16[12,1024,128]{2,1,0:T(8,128)(2,1)} %get-tuple-element.138.v_ref.refs_2_), custom_call_target="tpu_custom_call" | custom-call | flops 12884901888 | bytes 16777216 | tf_op jit(solution)/shard_map/attention_forward/pallas_call | solution.py:610
  123.1 24.8 %feed_forward.3 = (bf16[1024,768]{1,0:T(8,128)(2,1)}, f32[1024,768]{1,0:T(8,128)}, bf16[1024,3072]{1,0:T(8,128)(2,1)}, bf16[1024,3072]{1,0:T(8,128)(2,1)}, f32[1024,128]{1,0:T(8,128)}) custom-call(s32[1]{0:T(128)} %bitcast.sec_ref, f32[1024,768]{1,0:T(8,128)} %get-tuple-element.139.at_ref.refs_4_, bf16[1024,768]{1,0:T(8,128)(2,1)} %get-tuple-element.135.y_ref.x_ref, ...), custom_call_target="tpu_custom_call" | custom-call | flops 10871635968 | bytes 41943040 | tf_op jit(solution)/shard_map/feed_forward/pallas_call | solution.py:677
  147.9 2.8 select_bitcast_fusion.4
  150.7 31.4 %feed_backward.2 = (bf16[1024,3072]{1,0:T(8,128)(2,1)}, f32[1024,768]{1,0:T(8,128)}, bf16[1024,768]{1,0:T(8,128)(2,1)}, bf16[1024,768]{1,0:T(8,128)(2,1)}, bf16[...) custom-call(s32[1]{0:T(128)} %bitcast.sec_ref, ...), custom_call_target="tpu_custom_call" | custom-call | flops 10871635968 | bytes 52428800 | tf_op jit(solution)/shard_map/feed_backward/pallas_call | solution.py:771
  182.1 26.6 %feed_gradients.2 = (bf16[16,448,384]{2,1,0:T(8,128)(2,1)}, bf16[16,448,384]{2,1,0:T(8,128)(2,1)}) custom-call(s32[1]{0:T(128)} %bitcast.sec_ref, s32[32]{0:T(128)} %broadcast_select_fusion.7.order_ref, bf16[1024,3072]{1,0:T(8,128)(2,1)} %get-tuple-element.149.cb_ref, bf16[1024,3072]{1,0:T(8,128)(2,1)} %get-tuple-element.144.hid_ref, ...), custom_call_target="tpu_custom_call" | custom-call | flops 10871635968 | bytes 31457280 | tf_op jit(solution)/shard_map/feed_gradients/pallas_call | solution.py:967
  209.3 1.7 collective-permute-start.9
  210.9 35.5 %attention_backward.3.cj_ref = bf16[3,1024,768]{2,1,0:T(8,128)(2,1)} custom-call(bf16[12,1024,128]{2,1,0:T(8,128)(2,1)} %get-tuple-element.141.refs_0_, bf16[12,1024,128]{2,1,0:T(8,128)(2,1)} %get-tuple-element.137.k_ref.refs_1_, bf16[12,1024,128]{2,1,0:T(8,128)(2,1)} %get-tuple-element.138.v_ref.refs_2_, bf16[1024,768]{1,0:T(8,128)(2,1)} %get-tuple-element.157.refs_3_, ...), custom_call_target="tpu_custom_call" | custom-call | flops 32212254720 | bytes 18874368 | tf_op jit(solution)/shard_map/attention_backward/pallas_call | solution.py:851
  248.5 6.0 %add_convert_fusion.2 = (bf16[8,448,384]{2,1,0:T(8,128)(2,1)}, bf16[8,448,384]{2,1,0:T(8,128)(2,1)S(1)}) fusion(bf16[16,448,384]{2,1,0:T(8,128)(2,1)} %collective-permute-done.10, bf16[16,448,384]{2,1,0:T(8,128)(2,1)} %get-tuple-element.166), kind=kLoop, calls=%fused_computation.2 | loop fusion | flops 11010048 | bytes 16515072 | tf_op jit(solution)/shard_map/convert_element_type | solution.py:1128
  254.5 1.5 collective-permute-start.14
  256.0 11.1 %joint_backward.2 = (bf16[1024,768]{1,0:T(8,128)(2,1)}, f32[4,768]{1,0:T(4,128)}) custom-call(s32[1]{0:T(128)} %bitcast.sec_ref, bf16[3,1024,768]{2,1,0:T(8,128)(2,1)} %attention_backward.3.cj_ref, bf16[1024,768]{1,0:T(8,128)(2,1)} %get-tuple-element.135.y_ref.x_ref, f32[1024,768]{1,0:T(8,128)} %get-tuple-element.169.cm_ref, ...), custom_call_target="tpu_custom_call" | custom-call | flops 3623878656 | bytes 16777216 | tf_op jit(solution)/shard_map/joint_backward/pallas_call | solution.py:898
  267.1 11.0 %joint_gradients.2 = (bf16[16,160,384]{2,1,0:T(8,128)(2,1)}, bf16[16,160,384]{2,1,0:T(8,128)(2,1)}) custom-call(s32[1]{0:T(128)} %bitcast.sec_ref, s32[32]{0:T(128)} %broadcast_select_fusion.7.order_ref, bf16[3,1024,768]{2,1,0:T(8,128)(2,1)} %attention_backward.3.cj_ref, bf16[1024,768]{1,0:T(8,128)(2,1)} %get-tuple-element.171.n_ref, ...), custom_call_target="tpu_custom_call" | custom-call | flops 3623878656 | bytes 14680064 | tf_op jit(solution)/shard_map/joint_gradients/pallas_call | solution.py:1024
  278.1 2.7 fusion.6
  280.8 1.6 collective-permute-start.11
  282.3 5.0 collective-permute-start.13
  287.3 2.2 collective-permute-start.12
  289.5 31.7 %feed_backward.3 = (bf16[1024,3072]{1,0:T(8,128)(2,1)}, f32[1024,768]{1,0:T(8,128)}, bf16[1024,768]{1,0:T(8,128)(2,1)}, bf16[1024,768]{1,0:T(8,128)(2,1)}, bf16[...) custom-call(s32[1]{0:T(128)} %bitcast.sec_ref, ...), custom_call_target="tpu_custom_call" | custom-call | flops 10871635968 | bytes 52428800 | tf_op jit(solution)/shard_map/feed_backward/pallas_call | solution.py:771
  321.2 3.9 add_convert_fusion.10
  325.1 3.5 add_convert_fusion.6
  330.0 26.6 %feed_gradients.3 = (bf16[16,448,384]{2,1,0:T(8,128)(2,1)}, bf16[16,448,384]{2,1,0:T(8,128)(2,1)}) custom-call(s32[1]{0:T(128)} %bitcast.sec_ref, s32[32]{0:T(128)} %broadcast_select_fusion.7.order_ref, bf16[1024,3072]{1,0:T(8,128)(2,1)} %get-tuple-element.187.cb_ref, bf16[1024,3072]{1,0:T(8,128)(2,1)} %get-tuple-element.176.hid_ref, ...), custom_call_target="tpu_custom_call" | custom-call | flops 10871635968 | bytes 31457280 | tf_op jit(solution)/shard_map/feed_gradients/pallas_call | solution.py:967
  357.7 2.5 add_convert_fusion.14
  360.2 1.6 collective-permute-start.19
  362.9 19.2 %attention_backward.4.refs_7_ = bf16[3,1024,768]{2,1,0:T(8,128)(2,1)} custom-call(bf16[12,1024,128]{2,1,0:T(8,128)(2,1)} %get-tuple-element.164.refs_0_, bf16[12,1024,128]{2,1,0:T(8,128)(2,1)} %get-tuple-element.130.k_ref.refs_1_, bf16[12,1024,128]{2,1,0:T(8,128)(2,1)} %get-tuple-element.131.v_ref.refs_2_, bf16[1024,768]{1,0:T(8,128)(2,1)} %get-tuple-element.199.refs_3_, ...), custom_call_target="tpu_custom_call" | custom-call | flops 16106127360 | bytes 9437184 | tf_op jit(solution)/shard_map/attention_backward/pallas_call | solution.py:851
  384.0 5.9 %add_convert_fusion = (bf16[8,448,384]{2,1,0:T(8,128)(2,1)}, bf16[8,448,384]{2,1,0:T(8,128)(2,1)S(1)}) fusion(bf16[16,448,384]{2,1,0:T(8,128)(2,1)} %collective-permute-done.18, bf16[16,448,384]{2,1,0:T(8,128)(2,1)} %get-tuple-element.200), kind=kLoop, calls=%fused_computation | loop fusion | flops 11010048 | bytes 16515072 | tf_op jit(solution)/shard_map/convert_element_type | solution.py:1128
  389.9 1.5 collective-permute-start.23
  391.4 2.6 collective-permute-start.21
  394.5 19.2 %attention_backward.5.cj_ref = bf16[3,1024,768]{2,1,0:T(8,128)(2,1)} custom-call(bf16[12,1024,128]{2,1,0:T(8,128)(2,1)} %get-tuple-element.164.refs_0_, bf16[12,1024,128]{2,1,0:T(8,128)(2,1)} %get-tuple-element.130.k_ref.refs_1_, bf16[12,1024,128]{2,1,0:T(8,128)(2,1)} %get-tuple-element.131.v_ref.refs_2_, ...), custom_call_target="tpu_custom_call", output_to_operand_aliasing={{}: (7, {})} | custom-call | flops 16106127360 | bytes 9437184 | tf_op jit(solution)/shard_map/attention_backward/pallas_call | solution.py:851
  415.5 7.8 %collective-permute-done.23 = bf16[8,448,384]{2,1,0:T(8,128)(2,1)} collective-permute-done((bf16[8,448,384]{2,1,0:T(8,128)(2,1)}, bf16[8,448,384]{2,1,0:T(8,128)(2,1)}, u32[]{:S(2)}, u32[]{:S(2)}) %collective-permute-start.23) | collective-permute-done | bytes 2752544 | tf_op jit(solution)/shard_map/ppermute | solution.py:1119
  423.3 4.0 add_convert_fusion.4
  428.2 2.6 collective-permute-start.27
  430.8 11.1 %joint_backward.3 = (bf16[1024,768]{1,0:T(8,128)(2,1)}, f32[4,768]{1,0:T(4,128)}) custom-call(s32[1]{0:T(128)} %bitcast.sec_ref, bf16[3,1024,768]{2,1,0:T(8,128)(2,1)} %attention_backward.5.cj_ref, bf16[1024,768]{1,0:T(8,128)(2,1)} %get-tuple-element.134.x_ref, f32[1024,768]{1,0:T(8,128)} %get-tuple-element.215.cm_ref, ...), custom_call_target="tpu_custom_call" | custom-call | flops 3623878656 | bytes 16777216 | tf_op jit(solution)/shard_map/joint_backward/pallas_call | solution.py:898
  442.7 3.3 collective-permute-done.28
  445.9 2.5 add_convert_fusion.12
  448.5 11.0 %joint_gradients.3 = (bf16[16,160,384]{2,1,0:T(8,128)(2,1)}, bf16[16,160,384]{2,1,0:T(8,128)(2,1)}) custom-call(s32[1]{0:T(128)} %bitcast.sec_ref, s32[32]{0:T(128)} %broadcast_select_fusion.7.order_ref, bf16[3,1024,768]{2,1,0:T(8,128)(2,1)} %attention_backward.5.cj_ref, bf16[1024,768]{1,0:T(8,128)(2,1)} %get-tuple-element.227.n_ref, ...), custom_call_target="tpu_custom_call" | custom-call | flops 3623878656 | bytes 14680064 | tf_op jit(solution)/shard_map/joint_gradients/pallas_call | solution.py:1024
  459.5 2.7 select_bitcast_fusion.3
  462.3 1.3 collective-permute-start.26
  463.6 1.3 collective-permute-start.25
  464.9 1.8 pad_maximum_fusion
  467.0 1.9 maximum_bitcast_fusion
  468.9 2.9 collective-permute-start.24
  472.3 4.6 collective-permute-done.26
  478.3 2.0 add_convert_fusion.9
  480.3 9.3 %collective-permute-done.35 = bf16[2,448,384]{2,1,0:T(8,128)(2,1)S(1)} collective-permute-done((bf16[2,448,384]{2,1,0:T(8,128)(2,1)S(1)}, bf16[2,448,384]{2,1,0:T(8,128)(2,1)S(1)}, u32[]{:S(2)}, u32[]{:S(2)}) %collective-permute-start.35) | collective-permute-done | bytes 688160 | tf_op jit(solution)/shard_map/ppermute | solution.py:1119
  489.7 2.7 collective-permute-start.36
  494.0 13.4 %collective-permute-done.36 = bf16[1,448,384]{2,1,0:T(8,128)(2,1)S(1)} collective-permute-done((bf16[1,448,384]{2,1,0:T(8,128)(2,1)S(1)}, bf16[1,448,384]{2,1,0:T(8,128)(2,1)S(1)}, u32[]{:S(2)}, u32[]{:S(2)}) %collective-permute-start.36) | collective-permute-done | bytes 344096 | tf_op jit(solution)/shard_map/ppermute | solution.py:1119
  507.9 3.0 maximum_convert_fusion
  511.1 1.2 collective-permute-start.31
  515.1 4.9 collective-permute-done.31
  522.2 5.5 %collective-permute-done.32 = bf16[2,160,384]{2,1,0:T(8,128)(2,1)S(1)} collective-permute-done((bf16[2,160,384]{2,1,0:T(8,128)(2,1)S(1)}, bf16[2,160,384]{2,1,0:T(8,128)(2,1)S(1)}, u32[]{:S(2)}, u32[]{:S(2)}) %collective-permute-start.32) | collective-permute-done | bytes 245792 | tf_op jit(solution)/shard_map/ppermute | solution.py:1119
  527.7 1.5 collective-permute-start.33
  530.1 5.2 collective-permute-done.33
  (120 shorter events, 28.8 us)
Async XLA Ops:
  0.6 24.1 %collective-permute-start.2 = (bf16[768,2304]{1,0:T(8,128)(2,1)}, bf16[768,2304]{1,0:T(8,128)(2,1)S(1)}, u32[]{:S(2)}, u32[]{:S(2)}) collective-permute-start(bf16[768,2304]{1,0:T(8,128)(2,1)} %bitcast.92), channel_id=1, source_target_pairs={{0,16},{16,0},{1,17},{17,1},{2,18},{18,2},{3,19},{19,3},{4,20},{20... | collective-permute-start | bytes 10616840 | tf_op jit(solution)/shard_map/ppermute | solution.py:1194
  1.2 63.5 %collective-permute-start.4 = (bf16[768,3072]{1,0:T(8,128)(2,1)}, bf16[768,3072]{1,0:T(8,128)(2,1)}, u32[]{:S(2)}, u32[]{:S(2)}) collective-permute-start(bf16[768,3072]{1,0:T(8,128)(2,1)} %bitcast.82), channel_id=1, source_target_pairs={{0,16},{16,0},{1,17},{17,1},{2,18},{18,2},{3,19},{19,3},{4,20},{20... | collective-permute-start | bytes 14155784 | tf_op jit(solution)/shard_map/ppermute | solution.py:1194
  1.2 63.4 %collective-permute-start.5 = (bf16[3072,768]{1,0:T(8,128)(2,1)}, bf16[3072,768]{1,0:T(8,128)(2,1)}, u32[]{:S(2)}, u32[]{:S(2)}) collective-permute-start(bf16[3072,768]{1,0:T(8,128)(2,1)} %bitcast.87), channel_id=1, source_target_pairs={{0,16},{16,0},{1,17},{17,1},{2,18},{18,2},{3,19},{19,3},{4,20},{20... | collective-permute-start | bytes 14155784 | tf_op jit(solution)/shard_map/ppermute | solution.py:1194
  3.7 21.0 %collective-permute-start = (bf16[512,768]{1,0:T(8,128)(2,1)}, bf16[512,768]{1,0:T(8,128)(2,1)}, u32[]{:S(2)}, u32[]{:S(2)}) collective-permute-start(bf16[512,768]{1,0:T(8,128)(2,1)} %dynamic-slice_bitcast_fusion.6), channel_id=1, source_target_pairs={{0,1},{1,0},{2,3},{3,2},{4,5},{5,4},{6,7},{7,6},{8,9},{9,8},{10,11... | collective-permute-start | bytes 2359304 | tf_op jit(solution)/shard_map/ppermute | solution.py:1193
  11.2 9.8 %collective-permute-start.1 = (f32[1,12288]{1,0:T(1,128)}, f32[1,12288]{1,0:T(1,128)}, u32[]{:S(2)}, u32[]{:S(2)}) collective-permute-start(f32[1,12288]{1,0:T(1,128)} %get-tuple-element.125), channel_id=1, source_target_pairs={{0,16},{16,0},{1,17},{17,1},{2,18},{18,2},{3,19},{19,3},{4,20},{20... | collective-permute-start | bytes 147464 | tf_op jit(solution)/shard_map/ppermute | solution.py:1198
  20.9 43.7 %collective-permute-start.3 = (bf16[768,768]{1,0:T(8,128)(2,1)}, bf16[768,768]{1,0:T(8,128)(2,1)}, u32[]{:S(2)}, u32[]{:S(2)}) collective-permute-start(bf16[768,768]{1,0:T(8,128)(2,1)} %bitcast.98), channel_id=1, source_target_pairs={{0,16},{16,0},{1,17},{17,1},{2,18},{18,2},{3,19},{19,3},{4,20},{20... | collective-permute-start | bytes 3538952 | tf_op jit(solution)/shard_map/ppermute | solution.py:1194
  24.8 1.8 copy-start
  40.9 22.4 %collective-permute-start.6 = (bf16[512,768]{1,0:T(8,128)(2,1)S(1)}, bf16[512,768]{1,0:T(8,128)(2,1)S(1)}, u32[]{:S(2)}, u32[]{:S(2)}) collective-permute-start(bf16[512,768]{1,0:T(8,128)(2,1)S(1)} %get-tuple-element.279), channel_id=1, source_target_pairs={{0,1},{1,0},{2,3},{3,2},{4,5},{5,4},{6,7},{7,6},{8,9},{9,8},{10,11... | collective-permute-start | bytes 2359304 | tf_op jit(solution)/shard_map/ppermute | solution.py:1215
  123.1 24.9 %copy-start.1 = (bf16[1024,768]{1,0:T(8,128)(2,1)S(1)}, bf16[1024,768]{1,0:T(8,128)(2,1)}, u32[]{:S(2)}) copy-start(bf16[1024,768]{1,0:T(8,128)(2,1)} %get-tuple-element.135.y_ref.x_ref) | copy-start | bytes 4718596
  208.7 39.8 %collective-permute-start.10 = (bf16[16,448,384]{2,1,0:T(8,128)(2,1)}, bf16[16,448,384]{2,1,0:T(8,128)(2,1)}, u32[]{:S(2)}, u32[]{:S(2)}) collective-permute-start(bf16[16,448,384]{2,1,0:T(8,128)(2,1)} %get-tuple-element.167), channel_id=1, source_target_pairs={{0,16},{16,0},{1,17},{17,1},{2,18},{18,2},{3,19},{19,3},{4,20},{20... | collective-permute-start | bytes 16515080 | tf_op jit(solution)/shard_map/ppermute | solution.py:1111
  208.7 37.7 %collective-permute-start.7 = (bf16[512,768]{1,0:T(8,128)(2,1)}, bf16[512,768]{1,0:T(8,128)(2,1)S(1)}, u32[]{:S(2)}, u32[]{:S(2)}) collective-permute-start(bf16[512,768]{1,0:T(8,128)(2,1)} %get-tuple-element.158), channel_id=1, source_target_pairs={{0,1},{1,0},{16,17},{17,16},{2,3},{3,2},{18,19},{19,18},{4,5},{5,4... | collective-permute-start | bytes 2359304 | tf_op jit(solution)/shard_map/ppermute | solution.py:1234
  209.1 37.4 %collective-permute-start.8 = (bf16[512,768]{1,0:T(8,128)(2,1)S(1)}, bf16[512,768]{1,0:T(8,128)(2,1)S(1)}, u32[]{:S(2)}, u32[]{:S(2)}) collective-permute-start(bf16[512,768]{1,0:T(8,128)(2,1)S(1)} %get-tuple-element.159), channel_id=1, source_target_pairs={{0,16},{1,17},{16,0},{17,1},{2,18},{3,19},{18,2},{19,3},{4,20},{5,... | collective-permute-start | bytes 2359304 | tf_op jit(solution)/shard_map/ppermute | solution.py:1234
  209.3 37.2 %collective-permute-start.9 = (bf16[512,768]{1,0:T(8,128)(2,1)S(1)}, bf16[512,768]{1,0:T(8,128)(2,1)S(1)}, u32[]{:S(2)}, u32[]{:S(2)}) collective-permute-start(bf16[512,768]{1,0:T(8,128)(2,1)S(1)} %get-tuple-element.160), channel_id=1, source_target_pairs={{0,17},{1,16},{16,1},{17,0},{2,19},{3,18},{18,3},{19,2},{4,21},{5,... | collective-permute-start | bytes 2359304 | tf_op jit(solution)/shard_map/ppermute | solution.py:1234
  246.4 0.9 copy-start.8
  246.5 1.2 copy-start.9
  247.6 0.9 copy-start.10
  254.5 70.6 %collective-permute-start.14 = (bf16[8,448,384]{2,1,0:T(8,128)(2,1)}, bf16[8,448,384]{2,1,0:T(8,128)(2,1)}, u32[]{:S(2)}, u32[]{:S(2)}) collective-permute-start(bf16[8,448,384]{2,1,0:T(8,128)(2,1)} %get-tuple-element.184), channel_id=1, source_target_pairs={{0,2},{1,3},{2,0},{3,1},{4,6},{5,7},{6,4},{7,5},{8,10},{9,11},{10,... | collective-permute-start | bytes 8257544 | tf_op jit(solution)/shard_map/ppermute | solution.py:1119
  278.1 43.1 %collective-permute-start.15 = (bf16[16,160,384]{2,1,0:T(8,128)(2,1)}, bf16[16,160,384]{2,1,0:T(8,128)(2,1)}, u32[]{:S(2)}, u32[]{:S(2)}) collective-permute-start(bf16[16,160,384]{2,1,0:T(8,128)(2,1)} %get-tuple-element.186), channel_id=1, source_target_pairs={{0,16},{16,0},{1,17},{17,1},{2,18},{18,2},{3,19},{19,3},{4,20},{20... | collective-permute-start | bytes 5898248 | tf_op jit(solution)/shard_map/ppermute | solution.py:1111
  280.8 48.3 %collective-permute-start.11 = (bf16[512,768]{1,0:T(8,128)(2,1)}, bf16[512,768]{1,0:T(8,128)(2,1)}, u32[]{:S(2)}, u32[]{:S(2)}) collective-permute-start(bf16[512,768]{1,0:T(8,128)(2,1)} %get-tuple-element.293), channel_id=1, source_target_pairs={{16,17},{17,16},{18,19},{19,18},{20,21},{21,20},{22,23},{23,22},{2... | collective-permute-start | bytes 2359304 | tf_op jit(solution)/shard_map/ppermute | solution.py:1248
  282.3 46.8 %collective-permute-start.13 = (bf16[512,768]{1,0:T(8,128)(2,1)}, bf16[512,768]{1,0:T(8,128)(2,1)}, u32[]{:S(2)}, u32[]{:S(2)}) collective-permute-start(bf16[512,768]{1,0:T(8,128)(2,1)} %get-tuple-element.293), channel_id=1, source_target_pairs={{0,17},{1,16},{2,19},{3,18},{4,21},{5,20},{6,23},{7,22},{8,25},{9,... | collective-permute-start | bytes 2359304 | tf_op jit(solution)/shard_map/ppermute | solution.py:1248
  287.3 41.8 %collective-permute-start.12 = (bf16[512,768]{1,0:T(8,128)(2,1)}, bf16[512,768]{1,0:T(8,128)(2,1)}, u32[]{:S(2)}, u32[]{:S(2)}) collective-permute-start(bf16[512,768]{1,0:T(8,128)(2,1)} %get-tuple-element.217), channel_id=1, source_target_pairs={{0,16},{1,17},{2,18},{3,19},{4,20},{5,21},{6,22},{7,23},{8,24},{9,... | collective-permute-start | bytes 2359304 | tf_op jit(solution)/shard_map/ppermute | solution.py:1248
  328.6 29.1 %collective-permute-start.16 = (bf16[4,448,384]{2,1,0:T(8,128)(2,1)}, bf16[4,448,384]{2,1,0:T(8,128)(2,1)}, u32[]{:S(2)}, u32[]{:S(2)}) collective-permute-start(bf16[4,448,384]{2,1,0:T(8,128)(2,1)} %get-tuple-element.196), channel_id=1, source_target_pairs={{0,1},{1,0},{2,3},{3,2},{4,5},{5,4},{6,7},{7,6},{8,9},{9,8},{10,11... | collective-permute-start | bytes 4128776 | tf_op jit(solution)/shard_map/ppermute | solution.py:1119
  329.1 27.5 %collective-permute-start.17 = (bf16[8,160,384]{2,1,0:T(8,128)(2,1)}, bf16[8,160,384]{2,1,0:T(8,128)(2,1)S(1)}, u32[]{:S(2)}, u32[]{:S(2)}) collective-permute-start(bf16[8,160,384]{2,1,0:T(8,128)(2,1)} %get-tuple-element.198), channel_id=1, source_target_pairs={{0,2},{1,3},{2,0},{3,1},{4,6},{5,7},{6,4},{7,5},{8,10},{9,11},{10,... | collective-permute-start | bytes 2949128 | tf_op jit(solution)/shard_map/ppermute | solution.py:1119
  330.0 26.6 %copy-start.3 = (bf16[8,160,384]{2,1,0:T(8,128)(2,1)S(1)}, bf16[8,160,384]{2,1,0:T(8,128)(2,1)}, u32[]{:S(2)}) copy-start(bf16[8,160,384]{2,1,0:T(8,128)(2,1)} %get-tuple-element.197) | copy-start | bytes 2949124
  360.2 23.8 %collective-permute-start.18 = (bf16[16,448,384]{2,1,0:T(8,128)(2,1)}, bf16[16,448,384]{2,1,0:T(8,128)(2,1)}, u32[]{:S(2)}, u32[]{:S(2)}) collective-permute-start(bf16[16,448,384]{2,1,0:T(8,128)(2,1)} %get-tuple-element.201), channel_id=1, source_target_pairs={{0,16},{16,0},{1,17},{17,1},{2,18},{18,2},{3,19},{19,3},{4,20},{20... | collective-permute-start | bytes 16515080 | tf_op jit(solution)/shard_map/ppermute | solution.py:1111
  360.2 22.8 %collective-permute-start.19 = (bf16[2,448,384]{2,1,0:T(8,128)(2,1)}, bf16[2,448,384]{2,1,0:T(8,128)(2,1)S(1)}, u32[]{:S(2)}, u32[]{:S(2)}) collective-permute-start(bf16[2,448,384]{2,1,0:T(8,128)(2,1)} %get-tuple-element.203), channel_id=1, source_target_pairs={{0,4},{1,5},{2,6},{3,7},{4,0},{5,1},{6,2},{7,3},{8,12},{9,13},{10,... | collective-permute-start | bytes 2064392 | tf_op jit(solution)/shard_map/ppermute | solution.py:1119
  361.8 20.4 %collective-permute-start.20 = (bf16[4,160,384]{2,1,0:T(8,128)(2,1)}, bf16[4,160,384]{2,1,0:T(8,128)(2,1)S(1)}, u32[]{:S(2)}, u32[]{:S(2)}) collective-permute-start(bf16[4,160,384]{2,1,0:T(8,128)(2,1)} %get-tuple-element.205), channel_id=1, source_target_pairs={{0,1},{1,0},{2,3},{3,2},{4,5},{5,4},{6,7},{7,6},{8,9},{9,8},{10,11... | collective-permute-start | bytes 1474568 | tf_op jit(solution)/shard_map/ppermute | solution.py:1119
  389.9 24.5 %copy-start.7 = (bf16[1,448,384]{2,1,0:T(8,128)(2,1)S(1)}, bf16[1,448,384]{2,1,0:T(8,128)(2,1)}, u32[]{:S(2)}) copy-start(bf16[1,448,384]{2,1,0:T(8,128)(2,1)} %get-tuple-element.207) | copy-start | bytes 1032196
  389.9 33.4 %collective-permute-start.23 = (bf16[8,448,384]{2,1,0:T(8,128)(2,1)}, bf16[8,448,384]{2,1,0:T(8,128)(2,1)}, u32[]{:S(2)}, u32[]{:S(2)}) collective-permute-start(bf16[8,448,384]{2,1,0:T(8,128)(2,1)} %get-tuple-element.213), channel_id=1, source_target_pairs={{0,2},{1,3},{2,0},{3,1},{4,6},{5,7},{6,4},{7,5},{8,10},{9,11},{10,... | collective-permute-start | bytes 8257544 | tf_op jit(solution)/shard_map/ppermute | solution.py:1119
  391.4 23.0 %collective-permute-start.21 = (bf16[1,448,384]{2,1,0:T(8,128)(2,1)}, bf16[1,448,384]{2,1,0:T(8,128)(2,1)}, u32[]{:S(2)}, u32[]{:S(2)}) collective-permute-start(bf16[1,448,384]{2,1,0:T(8,128)(2,1)} %get-tuple-element.208), channel_id=1, source_target_pairs={{0,8},{1,9},{2,10},{3,11},{4,12},{5,13},{6,14},{7,15},{8,0},{9,1},... | collective-permute-start | bytes 1032200 | tf_op jit(solution)/shard_map/ppermute | solution.py:1119
  394.0 19.7 %collective-permute-start.22 = (bf16[2,160,384]{2,1,0:T(8,128)(2,1)}, bf16[2,160,384]{2,1,0:T(8,128)(2,1)S(1)}, u32[]{:S(2)}, u32[]{:S(2)}) collective-permute-start(bf16[2,160,384]{2,1,0:T(8,128)(2,1)} %get-tuple-element.211), channel_id=1, source_target_pairs={{0,4},{1,5},{2,6},{3,7},{4,0},{5,1},{6,2},{7,3},{8,12},{9,13},{10,... | collective-permute-start | bytes 737288 | tf_op jit(solution)/shard_map/ppermute | solution.py:1119
  427.3 18.6 %collective-permute-start.28 = (bf16[4,448,384]{2,1,0:T(8,128)(2,1)}, bf16[4,448,384]{2,1,0:T(8,128)(2,1)}, u32[]{:S(2)}, u32[]{:S(2)}) collective-permute-start(bf16[4,448,384]{2,1,0:T(8,128)(2,1)} %get-tuple-element.225), channel_id=1, source_target_pairs={{0,1},{1,0},{2,3},{3,2},{4,5},{5,4},{6,7},{7,6},{8,9},{9,8},{10,11... | collective-permute-start | bytes 4128776 | tf_op jit(solution)/shard_map/ppermute | solution.py:1119
  428.2 13.8 %collective-permute-start.27 = (bf16[1,160,384]{2,1,0:T(8,128)(2,1)}, bf16[1,160,384]{2,1,0:T(8,128)(2,1)S(1)}, u32[]{:S(2)}, u32[]{:S(2)}) collective-permute-start(bf16[1,160,384]{2,1,0:T(8,128)(2,1)} %get-tuple-element.222), channel_id=1, source_target_pairs={{0,8},{1,9},{2,10},{3,11},{4,12},{5,13},{6,14},{7,15},{8,0},{9,1},... | collective-permute-start | bytes 368648 | tf_op jit(solution)/shard_map/ppermute | solution.py:1119
  430.8 15.2 %copy-start.2 = (bf16[4,448,384]{2,1,0:T(8,128)(2,1)S(1)}, bf16[4,448,384]{2,1,0:T(8,128)(2,1)}, u32[]{:S(2)}) copy-start(bf16[4,448,384]{2,1,0:T(8,128)(2,1)} %get-tuple-element.224) | copy-start | bytes 4128772
  459.5 5.4 %copy-start.4 = (bf16[1,512,768]{2,1,0:T(8,128)(2,1)S(1)}, bf16[1,512,768]{2,1,0:T(8,128)(2,1)}, u32[]{:S(2)}) copy-start(bf16[1,512,768]{2,1,0:T(8,128)(2,1)} %get-tuple-element.274) | copy-start | bytes 2359300
  459.5 18.7 %collective-permute-start.29 = (bf16[16,160,384]{2,1,0:T(8,128)(2,1)}, bf16[16,160,384]{2,1,0:T(8,128)(2,1)}, u32[]{:S(2)}, u32[]{:S(2)}) collective-permute-start(bf16[16,160,384]{2,1,0:T(8,128)(2,1)} %get-tuple-element.230), channel_id=1, source_target_pairs={{0,16},{16,0},{1,17},{17,1},{2,18},{18,2},{3,19},{19,3},{4,20},{20... | collective-permute-start | bytes 5898248 | tf_op jit(solution)/shard_map/ppermute | solution.py:1111
  462.3 14.7 %collective-permute-start.26 = (bf16[512,768]{1,0:T(8,128)(2,1)}, bf16[512,768]{1,0:T(8,128)(2,1)}, u32[]{:S(2)}, u32[]{:S(2)}) collective-permute-start(bf16[512,768]{1,0:T(8,128)(2,1)} %get-tuple-element.291), channel_id=1, source_target_pairs={{16,1},{17,0},{18,3},{19,2},{20,5},{21,4},{22,7},{23,6},{24,9},{25... | collective-permute-start | bytes 2359304 | tf_op jit(solution)/shard_map/ppermute | solution.py:1248
  463.6 14.5 %collective-permute-start.25 = (bf16[512,768]{1,0:T(8,128)(2,1)}, bf16[512,768]{1,0:T(8,128)(2,1)S(1)}, u32[]{:S(2)}, u32[]{:S(2)}) collective-permute-start(bf16[512,768]{1,0:T(8,128)(2,1)} %get-tuple-element.292), channel_id=1, source_target_pairs={{16,0},{17,1},{18,2},{19,3},{20,4},{21,5},{22,6},{23,7},{24,8},{25... | collective-permute-start | bytes 2359304 | tf_op jit(solution)/shard_map/ppermute | solution.py:1248
  467.0 4.8 copy-start.11
  468.9 9.4 %copy-start.6 = (bf16[16,160,384]{2,1,0:T(8,128)(2,1)S(1)}, bf16[16,160,384]{2,1,0:T(8,128)(2,1)}, u32[]{:S(2)}) copy-start(bf16[16,160,384]{2,1,0:T(8,128)(2,1)} %get-tuple-element.229) | copy-start | bytes 5898244
  468.9 23.4 %collective-permute-start.24 = (bf16[512,768]{1,0:T(8,128)(2,1)}, bf16[512,768]{1,0:T(8,128)(2,1)S(1)}, u32[]{:S(2)}, u32[]{:S(2)}) collective-permute-start(bf16[512,768]{1,0:T(8,128)(2,1)} %get-tuple-element.291), channel_id=1, source_target_pairs={{0,1},{1,0},{2,3},{3,2},{4,5},{5,4},{6,7},{7,6},{8,9},{9,8},{10,11... | collective-permute-start | bytes 2359304 | tf_op jit(solution)/shard_map/ppermute | solution.py:1248
  471.8 17.8 %collective-permute-start.35 = (bf16[2,448,384]{2,1,0:T(8,128)(2,1)S(1)}, bf16[2,448,384]{2,1,0:T(8,128)(2,1)S(1)}, u32[]{:S(2)}, u32[]{:S(2)}) collective-permute-start(bf16[2,448,384]{2,1,0:T(8,128)(2,1)S(1)} %copy-done.11), channel_id=1, source_target_pairs={{0,4},{1,5},{2,6},{3,7},{4,0},{5,1},{6,2},{7,3},{8,12},{9,13},{10,... | collective-permute-start | bytes 2064392 | tf_op jit(solution)/shard_map/ppermute | solution.py:1119
  489.7 17.8 %collective-permute-start.36 = (bf16[1,448,384]{2,1,0:T(8,128)(2,1)S(1)}, bf16[1,448,384]{2,1,0:T(8,128)(2,1)S(1)}, u32[]{:S(2)}, u32[]{:S(2)}) collective-permute-start(bf16[1,448,384]{2,1,0:T(8,128)(2,1)S(1)} %add_convert_fusion.20), channel_id=1, source_target_pairs={{0,8},{1,9},{2,10},{3,11},{4,12},{5,13},{6,14},{7,15},{8,0},{9,1},... | collective-permute-start | bytes 1032200 | tf_op jit(solution)/shard_map/ppermute | solution.py:1119
  492.4 18.5 %collective-permute-start.30 = (bf16[8,160,384]{2,1,0:T(8,128)(2,1)S(1)}, bf16[8,160,384]{2,1,0:T(8,128)(2,1)S(1)}, u32[]{:S(2)}, u32[]{:S(2)}) collective-permute-start(bf16[8,160,384]{2,1,0:T(8,128)(2,1)S(1)} %get-tuple-element.263), channel_id=1, source_target_pairs={{0,2},{1,3},{2,0},{3,1},{4,6},{5,7},{6,4},{7,5},{8,10},{9,11},{10,... | collective-permute-start | bytes 2949128 | tf_op jit(solution)/shard_map/ppermute | solution.py:1119
  507.6 4.8 collective-permute-start.37
  511.1 8.9 %collective-permute-start.31 = (bf16[4,160,384]{2,1,0:T(8,128)(2,1)S(1)}, bf16[4,160,384]{2,1,0:T(8,128)(2,1)S(1)}, u32[]{:S(2)}, u32[]{:S(2)}) collective-permute-start(bf16[4,160,384]{2,1,0:T(8,128)(2,1)S(1)} %get-tuple-element.287), channel_id=1, source_target_pairs={{0,1},{1,0},{2,3},{3,2},{4,5},{5,4},{6,7},{7,6},{8,9},{9,8},{10,11... | collective-permute-start | bytes 1474568 | tf_op jit(solution)/shard_map/ppermute | solution.py:1119
  515.0 20.3 %copy-start.5 = (f32[160,384]{1,0:T(8,128)S(1)}, f32[160,384]{1,0:T(8,128)}, u32[]{:S(2)}) copy-start(f32[160,384]{1,0:T(8,128)} %add_bitcast_fusion.1) | copy-start | bytes 737284
  520.2 7.6 %collective-permute-start.32 = (bf16[2,160,384]{2,1,0:T(8,128)(2,1)S(1)}, bf16[2,160,384]{2,1,0:T(8,128)(2,1)S(1)}, u32[]{:S(2)}, u32[]{:S(2)}) collective-permute-start(bf16[2,160,384]{2,1,0:T(8,128)(2,1)S(1)} %get-tuple-element.298), channel_id=1, source_target_pairs={{0,4},{1,5},{2,6},{3,7},{4,0},{5,1},{6,2},{7,3},{8,12},{9,13},{10,... | collective-permute-start | bytes 737288 | tf_op jit(solution)/shard_map/ppermute | solution.py:1119
  527.7 7.6 %collective-permute-start.33 = (bf16[1,160,384]{2,1,0:T(8,128)(2,1)S(1)}, bf16[1,160,384]{2,1,0:T(8,128)(2,1)S(1)}, u32[]{:S(2)}, u32[]{:S(2)}) collective-permute-start(bf16[1,160,384]{2,1,0:T(8,128)(2,1)S(1)} %add_convert_fusion.28), channel_id=1, source_target_pairs={{0,8},{1,9},{2,10},{3,11},{4,12},{5,13},{6,14},{7,15},{8,0},{9,1},... | collective-permute-start | bytes 368648 | tf_op jit(solution)/shard_map/ppermute | solution.py:1119
  535.4 1.6 collective-permute-start.34

commit v3 on v2

--- a/solution.py
+++ b/solution.py
@@ -1156,6 +1156,250 @@
     return value
 
 
+def last_kernel(cj_ref, n_ref, x_ref, cm_ref, pack_ref, own_ref, other_ref, feed_keep, feed_send, done_ref,
+                out_ref, mine_ref, got_ref,
+                w_ref, back, cj_t, acc, j_keep, j_send, r0, r1, r2, r3, r4, k1, k2, k3, k4, s1, s2, s3, s4,
+                f1, f2, f3, fk2, fk3, fs2, fs3, swap_out, landed, send_sem, recv_sem, local_sem):
+    s, d, q = (lax.axis_index(name) for name in ("section", "dp", "seq"))
+    x = (s, d + 1 - 2 * (d % 2), q)
+    y = (s, d, 1 - q)
+    first = (s, (1 - s) * x[1] + s * d, (1 - s) * q + s * y[2])
+    second = (s, s * x[1] + (1 - s) * d, s * q + (1 - s) * y[2])
+    near = (s, d + 2 - 4 * (d // 2 % 2), q)
+    far = (s, d + 4 - 8 * (d // 4), q)
+    core = (1 - s, d, q)
+    parts, thick, half = j_keep.shape
+    thick -= 16
+    width = n_ref.shape[-1]
+    piece = got_ref.shape[1]
+
+    @pl.when(s == 0)
+    def _():
+        pltpu.make_async_copy(own_ref, w_ref, local_sem).start()
+
+    @pl.when(s == 1)
+    def _():
+        pltpu.make_async_copy(other_ref, w_ref, local_sem).start()
+
+    barrier = pltpu.get_barrier_semaphore()
+    across = (1 - s, d, 1 - q)
+    for other in (core, x, y, near, far, across):
+        pl.semaphore_signal(barrier, inc=1, device_id=other, device_id_type=pl.DeviceIdType.MESH)
+    pl.semaphore_wait(barrier, 6)
+
+    def ready(number, source, target, other):
+        return pltpu.make_async_remote_copy(
+            src_ref=source, dst_ref=target, send_sem=send_sem.at[number], recv_sem=recv_sem.at[number],
+            device_id=other, device_id_type=pl.DeviceIdType.MESH)
+
+    def send(number, source, target, other):
+        copy = ready(number, source, target, other)
+        copy.start()
+        return copy
+
+    def total(one, two):
+        return one.astype(F32) + two.astype(F32)
+
+    feed_rows = feed_keep.shape[1]
+    feed_blocks = [pl.ds(number * (feed_rows // 2), feed_rows // 2) for number in range(2)]
+    feed_flights = [send(number, feed_send.at[:, at], f1.at[:, at], second) for number, at in enumerate(feed_blocks)]
+    (gain_ref,) = vectors_of(pack_ref, width, FIRST_GAIN)
+    acc[...] = jnp.zeros_like(acc)
+    tb = piece // 2
+    rows = x_ref.shape[0]
+    order = [2, 3, 0, 1]
+
+    def slope_of(block):
+        at = pl.ds(block * tb, tb)
+        slope = nt(cj_ref[0, at], w_ref[:, 0:width])
+        for which in range(1, 3):
+            slope = slope + nt(cj_ref[which, at], w_ref[:, which * width:(which + 1) * width])
+        return slope
+
+    pltpu.make_async_copy(own_ref, w_ref, local_sem).wait()
+    to_y = ready(16, back.at[pl.ds(piece, piece)], got_ref.at[0], (0, d, 1 - q))
+    to_core = ready(17, back.at[pl.ds(0, piece)], got_ref.at[1], (0, d, q))
+    to_across = ready(18, back.at[pl.ds(piece, piece)], got_ref.at[2], (0, d, 1 - q))
+    later = slope_of(order[0])
+    for number, block in enumerate(order):
+        slope = later
+        if number + 1 < len(order):
+            later = slope_of(order[number + 1])
+        at = pl.ds(block * tb, tb)
+        unit, scale = normalize(x_ref[at, :].astype(F32))
+        acc[0] += fold(slope * unit)
+        for which in range(3):
+            acc[which + 1] += fold(cj_ref[which, at].astype(F32))
+        back[at, :] = (cm_ref[at, :] + norm_back(slope * gain_ref[...], unit, scale)).astype(BF16)
+        if number == 1:
+            @pl.when(s == 0)
+            def _():
+                to_y.start()
+    mine_ref[...] = back[0:piece, :]
+
+    sums = [jnp.sum(acc[number], axis=0, keepdims=True) for number in range(4)]
+    for which in range(3):
+        cj_t[which] = cj_ref[which].T
+
+    def position(part, owner):
+        bx, by = (part // 2 % 2 + d % 2) % 2, (part % 2 + q) % 2
+        bz, cz = (part // 4 + d // 2) % 2, (part // 8 + d // 4) % 2
+        depth = bz * 2 + cz
+        return (1 - owner) * ((bx * 2 + by) * 4 + depth) + owner * ((by * 2 + bx) * 4 + depth)
+
+    def gradients(target, owner):
+        for block in range(3):
+            found = nn(cj_t[block], n_ref[:, pl.ds(pl.multiple_of(owner * half, 128), half)]).astype(BF16)
+            for part in range(parts):
+                low, high = max(thick * part, width * block), min(thick * (part + 1), width * (block + 1))
+                if low < high:
+                    target[position(part, owner), low - thick * part:high - thick * part, :] = found[low - width * block:high - width * block]
+        for part in range(parts):
+            window = thick * part // half
+            lines = [sums[1 + w // 2][:, w % 2 * half:w % 2 * half + half] for w in (window, min(window + 1, 5))]
+            away = part // (parts // 2) * half
+            lines = jnp.concatenate(lines + [sums[0][:, away:away + half], jnp.zeros((13, half), F32)], axis=0)
+            target[position(part, owner), thick:, :] = lines.astype(BF16)
+
+    gradients(j_send, 1 - s)
+    blocks = [pl.ds(number * (thick + 16) // 2, (thick + 16) // 2) for number in range(2)]
+    flights = [send(2 + number, j_send.at[:, at], r0.at[:, at], core) for number, at in enumerate(blocks)]
+    for number, at in enumerate(feed_blocks):
+        feed_flights[number].wait()
+        fs2[:, at] = total(feed_keep[2:, at], f1[2:, at]).astype(BF16)
+        feed_flights[number] = send(4 + number, fs2.at[:, at], f2.at[:, at], near)
+        fk2[:, at] = total(feed_keep[:2, at], f1[:2, at]).astype(BF16)
+    gradients(j_keep, s)
+    kept, arrived = j_keep, r0
+    for stage, (sent, held, target, other) in enumerate(
+        ((s1, k1, r1, first), (s2, k2, r2, second), (s3, k3, r3, near), (s4, k4, r4, far))):
+        middle = kept.shape[0] // 2
+        for number, at in enumerate(blocks):
+            flights[number].wait()
+            sent[:, at] = total(kept[middle:, at], arrived[middle:, at]).astype(BF16)
+            flights[number] = send(8 + 2 * stage + number, sent.at[:, at], target.at[:, at], other)
+            held[:, at] = total(kept[:middle, at], arrived[:middle, at]).astype(BF16)
+        kept, arrived = held, target
+        if stage == 0:
+            for number, at in enumerate(feed_blocks):
+                feed_flights[number].wait()
+                fs3[:, at] = total(fk2[1:, at], f2[1:, at]).astype(BF16)
+                feed_flights[number] = send(6 + number, fs3.at[:, at], f3.at[:, at], far)
+                fk3[:, at] = total(fk2[:1, at], f2[:1, at])
+        if stage == 1:
+            @pl.when(s == 1)
+            def _():
+                to_core.start()
+                to_across.start()
+    own = jnp.full((1, 1), s) == 0
+
+    def settle(at, mine):
+        done = done_ref[at, :]
+        swap_out[at, :] = jnp.where(own, done, mine)
+        out_ref[pl.ds(s, 1), at, :] = jnp.where(own, mine, done)[None]
+
+    for number, at in enumerate(feed_blocks):
+        feed_flights[number].wait()
+        settle(at, fk3[0, at] + f3[0, at].astype(F32))
+    for number, at in enumerate(blocks):
+        flights[number].wait()
+        settle(pl.ds(feed_rows + number * (thick + 16) // 2, (thick + 16) // 2), total(kept[0, at], arrived[0, at]))
+    send(19, swap_out, landed, core).wait()
+    out_ref[pl.ds(1 - s, 1)] = landed[...][None]
+
+    @pl.when(s == 0)
+    def _():
+        to_y.wait_send()
+        for copy in (to_y, to_core, to_across):
+            copy.wait_recv()
+
+    @pl.when(s == 1)
+    def _():
+        to_core.wait_send()
+        to_across.wait_send()
+
+
+def last_step(cj, normed, state, cm, pack, own, other, feed_keep, feed_send, done, parts):
+    rows, width = state.shape
+    half, piece = width // 2, rows // 2
+    thick = 3 * width // parts + 16
+    feed_rows = feed_keep.shape[1]
+    vm = pl.BlockSpec(memory_space=pltpu.VMEM)
+    level = lambda n, m=thick, t=BF16: pltpu.VMEM((n, m, half), t)
+    steps = [parts >> number for number in range(1, 5)]
+    S = jax.ShapeDtypeStruct
+    return pl.pallas_call(
+        last_kernel,
+        in_specs=[vm] * 5 + [ANY] * 2 + [vm] * 3,
+        out_specs=[vm] * 3,
+        out_shape=[S((2, feed_rows + thick, half), F32), S((piece, width), BF16), S((3, piece, width), BF16)],
+        scratch_shapes=[pltpu.VMEM(own.shape, BF16), pltpu.VMEM((rows, width), BF16), pltpu.VMEM((3, width, rows), BF16),
+                        pltpu.VMEM((4, 8, width), F32)]
+        + [level(parts)] * 3 + [level(n) for n in steps] * 3
+        + [level(4, feed_rows), level(2, feed_rows), level(1, feed_rows), level(2, feed_rows), level(1, feed_rows, F32),
+           level(2, feed_rows), level(1, feed_rows)]
+        + [pltpu.VMEM((feed_rows + thick, half), F32)] * 2
+        + [pltpu.SemaphoreType.DMA((20,)), pltpu.SemaphoreType.DMA((20,)), pltpu.SemaphoreType.DMA],
+        compiler_params=pltpu.CompilerParams(collective_id=0, has_side_effects=True, vmem_limit_bytes=VLIM),
+        cost_estimate=pl.CostEstimate(flops=0, bytes_accessed=100 * 1024 * 1024, transcendentals=0),
+        name="last_step",
+    )(cj, normed, state, cm, pack, own, other, feed_keep, feed_send, done)
+
+
+def assemble_kernel(parts, index_ref, both_ref, joint_ref, jb_ref, out_ref, ob_ref, up_ref, ub_ref, down_ref, db_ref,
+                    fg_ref, ig_ref, sg_ref, hg_ref):
+    half = both_ref.shape[-1]
+    index = index_ref[0]
+    up_rows, thin, thick = up_ref.shape[0], out_ref.shape[0], joint_ref.shape[0]
+    steps = up_rows // thin
+    for side in range(2):
+        at = pl.ds(side * half, half)
+        up_ref[:, at] = both_ref[side, 0:up_rows, :]
+        for step in range(steps):
+            begin = up_rows + step * thin
+            down_ref[:, pl.ds((side * steps + step) * half, half)] = both_ref[side, begin:begin + thin, :]
+        begin = 2 * up_rows
+        out_ref[:, at] = both_ref[side, begin:begin + thin, :]
+        begin = 2 * up_rows + thin + 16
+        joint_ref[:, at] = both_ref[side, begin:begin + thick, :]
+
+    def cut(row, count, target):
+        begin = index * count % half
+        best = row[:, 0:count]
+        for number in range(1, half // count):
+            best = jnp.where(jnp.full((1, 1), begin) == number * count, row[:, number * count:(number + 1) * count], best)
+        target[...] = best
+
+    at = 2 * up_rows + thin
+    for number, (target, count) in enumerate(((hg_ref, up_rows), (ub_ref, up_rows), (db_ref, thin), (sg_ref, thin), (ob_ref, thin), (ig_ref, thin))):
+        cut(both_ref[0, at + number:at + number + 1, :], count, target)
+    at += 16 + thick
+    cut(both_ref[0, at + 2:at + 3, :], thin, fg_ref)
+    line = jnp.concatenate([both_ref[0, at:at + 1, :], both_ref[0, at + 1:at + 2, :]], axis=1)
+    best = line[:, 0:thick]
+    for part in range(1, parts):
+        begin = part * thick % half
+        best = jnp.where(jnp.full((1, 1), index) == part, line[:, begin:begin + thick], best)
+    jb_ref[...] = best
+
+
+def assemble(index, both, parts, width):
+    wide = 4 * width
+    S = lambda *shape: jax.ShapeDtypeStruct(shape, F32)
+    vm = pl.BlockSpec(memory_space=pltpu.VMEM)
+    thin, up_rows, thick = width // parts, wide // parts, 3 * width // parts
+    results = pl.pallas_call(
+        functools.partial(assemble_kernel, parts),
+        in_specs=[SMEM, vm],
+        out_specs=[vm] * 12,
+        out_shape=[S(thick, width), S(1, thick), S(thin, width), S(1, thin), S(up_rows, width), S(1, up_rows),
+                   S(thin, wide), S(1, thin), S(1, thin), S(1, thin), S(1, thin), S(1, up_rows)],
+        compiler_params=pltpu.CompilerParams(vmem_limit_bytes=VLIM),
+        name="gradient_outputs",
+    )(index.reshape(1).astype(jnp.int32), both)
+    return tuple(item.T[None] if number in (0, 2, 4, 6) else item for number, item in enumerate(results))
+
+
 def row_step(
     sizes,
     tokens,
@@ -1270,72 +1514,24 @@
             cj = advance(cj, flights[FEED, 0], flights[FEED, 1], flights[JOINT, 1])
             cj = attend_back(query, k, v, ch, attended, cosine, sine, count, None, cj)
             cj = advance(cj, flights[FEED, 1])
-            cj = advance(cj, flights[JOINT, 1], flights[FEED, 0])
+            flights[JOINT, 1].add()
+            flights[JOINT, 1].send()
+            flights[FEED, 0].add()
+        if layer == 0:
+            break
         back, sums = qkv_back(layer, sec, cj, state, cm, pack, *joint_pair)
         delivered[layer] = deliver(layer, back)
-        if layer == 0:
-            cj = advance(cj, flights[JOINT, 1])
-            cj = advance(cj, flights[FEED, 0])
         flights[JOINT, layer] = Reduction(*joint_grads(sec, order, cj, normed, sums), sizes)
         if layer == 1:
             back = advance(back, flights[JOINT, 1])
         slope = back
-    last, before = flights[JOINT, 0], flights[FEED, 0]
-    last.send()
-    last.add()
-    before.kept, _ = lax.optimization_barrier((before.kept, last.sent))
-    last.send()
+    before = flights[FEED, 0]
+    done = jnp.concatenate([flights[FEED, 1].finish(), flights[JOINT, 1].finish()], axis=0)
+    both, ours, got = last_step(cj, normed, state, cm, pack, *joint_pair, before.kept, before.sent, done, parts)
     hiddens = place([own] + gathered)
-    input_gradients = place([jnp.where(section == 0, a, b) for a, b in zip(*delivered)]).astype(F32)
-
-    def settle(name):
-        grads = [flights[name, layer].finish() for layer in range(2)]
-        ours = jnp.where(section == 0, grads[0], grads[1])
-        theirs = lax.ppermute(jnp.where(section == 0, grads[1], grads[0]), "section", swap)
-        return jnp.where(section == 0, ours, theirs), jnp.where(section == 0, theirs, ours)
-
-    left, right = settle(FEED)
-    up_rows, thin, thick = wide // parts, width // parts, 3 * width // parts
-
-    def rows_of(begin, count):
-        return jnp.concatenate([left[begin:begin + count], right[begin:begin + count]], axis=1)
-
-    up_grad = rows_of(0, up_rows).T
-    at = up_rows
-    steps = up_rows // thin
-    sides = [item[at:at + up_rows].reshape(steps, thin, half).transpose(0, 2, 1).reshape(steps * half, thin) for item in (left, right)]
-    down_grad = jnp.concatenate(sides, axis=0)
-    at += up_rows
-    output_grad = rows_of(at, thin).T
-    at += thin
-    index = 2 * data + part
-
-    def piece_of(row, count):
-        return lax.dynamic_slice_in_dim(row, index * count % half, count)
-
-    hg, ub = (piece_of(left[at + number], up_rows) for number in range(2))
-    db, sg, ob, ig = (piece_of(left[at + 2 + number], thin) for number in range(4))
-    left, right = settle(JOINT)
-    joint_grad = rows_of(0, thick).T
-    at = thick
-    jb = lax.dynamic_slice_in_dim(jnp.concatenate([left[at], left[at + 1]]), index * thick % half, thick)
-    fg = piece_of(left[at + 2], thin)
-    return (
-        hiddens,
-        input_gradients,
-        joint_grad[None],
-        jb[None],
-        output_grad[None],
-        ob[None],
-        up_grad[None],
-        ub[None],
-        down_grad[None],
-        db[None],
-        fg[None],
-        ig[None],
-        sg[None],
-        hg[None],
-    )
+    input_gradients = place([jnp.where(section == 0, a, b) for a, b in zip((ours, got[0], got[1], got[2]), delivered[1])]).astype(F32)
+
+    return (hiddens, input_gradients) + tuple(assemble(2 * data + part, both, parts, width))
 
 
 def choose(sizes, *arrays):

time: 547 us -> 515 us (0.941)
  waiting for transfers between devices: 65.5 us -> 18.3 us
  Pallas kernels: 355 us -> 401 us
  starting transfers between devices: 43.4 us -> 26 us
  other arithmetic: 57.6 us -> 48.5 us
    pallas_call x0 -> x2, Pallas kernels: none -> 67.8 us  [the longest x1 64 us: last_step(): pl.pallas_call(last_kernel, in_specs=[vm] * 5 + [ANY] * 2 + [vm] * 3, out...]
    ppermute x16 -> x9, waiting for transfers between devices: 49.4 us -> 7.46 us  [send(): lax.ppermute(self.sent, ('section', 'dp', 'seq'), swap_pairs(moves[self.s...]
    pallas_call x2 -> x1, Pallas kernels: 22.2 us -> 11.1 us  [qkv_back(): pl.pallas_call(functools.partial(qkv_back_kernel, layer), grid=(rows // t...]
    pallas_call x2 -> x1, Pallas kernels: 22.1 us -> 11 us  [joint_grads(): pl.pallas_call(joint_grads_kernel, grid_spec=pltpu.PrefetchScalarGridSpec...]
    ppermute x16 -> x9, starting transfers between devices: 20.9 us -> 10.7 us  [send(): lax.ppermute(self.sent, ('section', 'dp', 'seq'), swap_pairs(moves[self.s...]
    ppermute x6 -> x3, starting transfers between devices: 14.2 us -> 7.15 us  [deliver(): return [own] + [lax.ppermute(block, every, pairs) for block, pairs in moves]]
    convert_element_type x13 -> x10, other arithmetic: 32.1 us -> 31.9 us  [add(): (kept[middle:].astype(F32) + arrived[middle:].astype(F32)).astype(BF16)]
  transfers between devices with their start and end apart: 38 -> 25, of which waited for: 11 -> 3; matrix products, arithmetic and copies ran while one was open for 8% -> 6% of each run, Pallas kernels for 38% -> 38%
where the time goes in v3:
time: 515 us; the launch traced here: 506 us
  Pallas kernels  401 us (78%)
  other arithmetic  48.5 us (9%)
  starting transfers between devices  26 us (5%)
  waiting for transfers between devices  18.3 us (4%)
  local copies, waits for them, and re-layouts  11.6 us (2%)
    pallas_call x3, Pallas kernels, attend_back(): pl.pallas_call(kernel, grid=(count,), in_specs=[hd, hd, hd, col, col, con...  74.1 us
    pallas_call x1, Pallas kernels, last_step(): pl.pallas_call(last_kernel, in_specs=[vm] * 5 + [ANY] * 2 + [vm] * 3, out...  64 us
    pallas_call x2, Pallas kernels, feed_back(): pl.pallas_call(functools.partial(feed_back_kernel, layer), grid=(rows //...  63 us
    pallas_call x2, Pallas kernels, feed_grads(): pl.pallas_call(feed_grads_kernel, grid_spec=pltpu.PrefetchScalarGridSpec(...  53.2 us
    pallas_call x2, Pallas kernels, feed(): pl.pallas_call(functools.partial(feed_kernel, layer), grid=(rows // tb,),...  49.4 us
    pallas_call x2, Pallas kernels, attend(): pl.pallas_call(functools.partial(attend_kernel, qb), grid=(heads // 2,),...  41.4 us
    convert_element_type x10, other arithmetic, add(): (kept[middle:].astype(F32) + arrived[middle:].astype(F32)).astype(BF16)  31.9 us
    pallas_call x2, Pallas kernels, qkv(): pl.pallas_call(functools.partial(qkv_kernel, layer, blocks), grid_spec=pl...  25.8 us
  transfers between devices with their start and end apart: 25, of which 3 were waited for; matrix products, arithmetic and copies ran while one was open for 6% of the time, Pallas kernels for 38%

profile of v3, /device:TPU:0, one launch (start us, length us, event | category | flops | bytes accessed | tf_op | source)
XLA Modules:
  0.0 506.5 jit_solution(1133091886134014339)
XLA Ops:
  0.6 0.5 collective-permute-start.2
  1.2 0.4 collective-permute-start.5
  1.7 2.1 dynamic-slice_bitcast_fusion.6
  3.7 2.6 collective-permute-start
  6.3 0.6 broadcast_in_dim_tile.3.rate_ref
  6.9 4.2 row_tables.1
  11.3 0.6 broadcast_select_fusion.4.order_ref
  11.9 9.0 %collective-permute-done.1 = f32[1,12288]{1,0:T(1,128)} collective-permute-done((f32[1,12288]{1,0:T(1,128)}, f32[1,12288]{1,0:T(1,128)}, u32[]{:S(2)}, u32[]{:S(2)}) %collective-permute-start.1) | collective-permute-done | bytes 49184 | tf_op jit(solution)/shard_map/ppermute | solution.py:1442
  21.3 1.7 broadcast_select_fusion.3.pack_ref
  23.0 1.8 collective-permute-done.y_ref
  24.8 1.8 copy-done
  26.6 12.9 %joint_projection.2 = (bf16[1024,768]{1,0:T(8,128)(2,1)}, bf16[1024,768]{1,0:T(8,128)(2,1)}, bf16[12,1024,128]{2,1,0:T(8,128)(2,1)}, bf16[12,1024,128]{2,1,0:T(8,128)(2,1)}, bf16[12,1024,128]{2,1,0:T(8,128)(2,1)}) custom-call(s32[1]{0:T(128)} %bitcast.sec_ref, s32[1]{0:T(128)} %bitcast.1.mine_ref, bf16[4,512,768]{2,1,0:T(8,128)(2,1)} %bitcast.95, ...), custom_call_target="tpu_custom_call" | custom-call | flops 3623878656 | bytes 16777216 | tf_op jit(solution)/shard_map/joint_projection/pallas_call | solution.py:557
  39.5 1.5 dynamic-slice_bitcast_fusion.5
  41.0 1.8 collective-permute-start.6
  42.8 20.6 %attention_forward.2 = (f32[1024,768]{1,0:T(8,128)}, bf16[12,1024,128]{2,1,0:T(8,128)(2,1)}) custom-call(bf16[12,1024,128]{2,1,0:T(8,128)(2,1)} %get-tuple-element.129.q_ref, bf16[12,1024,128]{2,1,0:T(8,128)(2,1)} %get-tuple-element.130.k_ref.refs_1_, bf16[12,1024,128]{2,1,0:T(8,128)(2,1)} %get-tuple-element.131.v_ref.refs_2_), custom_call_target="tpu_custom_call" | custom-call | flops 12884901888 | bytes 16777216 | tf_op jit(solution)/shard_map/attention_forward/pallas_call | solution.py:610
  63.4 1.4 pad_maximum_fusion.2.c_ref
  64.8 24.6 %feed_forward.2 = (bf16[1024,768]{1,0:T(8,128)(2,1)}, f32[1024,768]{1,0:T(8,128)}, bf16[1024,3072]{1,0:T(8,128)(2,1)}, bf16[1024,3072]{1,0:T(8,128)(2,1)}, f32[1024,128]{1,0:T(8,128)}) custom-call(s32[1]{0:T(128)} %bitcast.sec_ref, f32[1024,768]{1,0:T(8,128)} %get-tuple-element.132.at_ref.refs_4_, bf16[1024,768]{1,0:T(8,128)(2,1)} %get-tuple-element.134.x_ref, ...), custom_call_target="tpu_custom_call" | custom-call | flops 10871635968 | bytes 41943040 | tf_op jit(solution)/shard_map/feed_forward/pallas_call | solution.py:677
  89.4 12.9 %joint_projection.3 = (bf16[1024,768]{1,0:T(8,128)(2,1)}, bf16[1024,768]{1,0:T(8,128)(2,1)}, bf16[12,1024,128]{2,1,0:T(8,128)(2,1)}, bf16[12,1024,128]{2,1,0:T(8,128)(2,1)}, bf16[12,1024,128]{2,1,0:T(8,128)(2,1)}) custom-call(s32[1]{0:T(128)} %bitcast.sec_ref, s32[1]{0:T(128)} %constant.124.clone.1.mine_ref, bf16[1,1024,768]{2,1,0:T(8,128)(2,1)} %bitcast.86, ...), custom_call_target="tpu_custom_call" | custom-call | flops 3623878656 | bytes 16777216 | tf_op jit(solution)/shard_map/joint_projection/pallas_call | solution.py:557
  102.4 20.8 %attention_forward.3 = (f32[1024,768]{1,0:T(8,128)}, bf16[12,1024,128]{2,1,0:T(8,128)(2,1)}) custom-call(bf16[12,1024,128]{2,1,0:T(8,128)(2,1)} %get-tuple-element.136.q_ref, bf16[12,1024,128]{2,1,0:T(8,128)(2,1)} %get-tuple-element.137.k_ref.refs_1_, bf16[12,1024,128]{2,1,0:T(8,128)(2,1)} %get-tuple-element.138.v_ref.refs_2_), custom_call_target="tpu_custom_call" | custom-call | flops 12884901888 | bytes 16777216 | tf_op jit(solution)/shard_map/attention_forward/pallas_call | solution.py:610
  123.2 24.8 %feed_forward.3 = (bf16[1024,768]{1,0:T(8,128)(2,1)}, f32[1024,768]{1,0:T(8,128)}, bf16[1024,3072]{1,0:T(8,128)(2,1)}, bf16[1024,3072]{1,0:T(8,128)(2,1)}, f32[1024,128]{1,0:T(8,128)}) custom-call(s32[1]{0:T(128)} %bitcast.sec_ref, f32[1024,768]{1,0:T(8,128)} %get-tuple-element.139.at_ref.refs_4_, bf16[1024,768]{1,0:T(8,128)(2,1)} %get-tuple-element.135.y_ref.x_ref, ...), custom_call_target="tpu_custom_call" | custom-call | flops 10871635968 | bytes 41943040 | tf_op jit(solution)/shard_map/feed_forward/pallas_call | solution.py:677
  148.0 2.8 select_bitcast_fusion.1
  150.7 31.4 %feed_backward.2 = (bf16[1024,3072]{1,0:T(8,128)(2,1)}, f32[1024,768]{1,0:T(8,128)}, bf16[1024,768]{1,0:T(8,128)(2,1)}, bf16[1024,768]{1,0:T(8,128)(2,1)}, bf16[...) custom-call(s32[1]{0:T(128)} %bitcast.sec_ref, ...), custom_call_target="tpu_custom_call" | custom-call | flops 10871635968 | bytes 52428800 | tf_op jit(solution)/shard_map/feed_backward/pallas_call | solution.py:771
  182.2 26.6 %feed_gradients.2 = (bf16[16,448,384]{2,1,0:T(8,128)(2,1)}, bf16[16,448,384]{2,1,0:T(8,128)(2,1)}) custom-call(s32[1]{0:T(128)} %bitcast.sec_ref, s32[32]{0:T(128)} %broadcast_select_fusion.4.order_ref, bf16[1024,3072]{1,0:T(8,128)(2,1)} %get-tuple-element.149.cb_ref, bf16[1024,3072]{1,0:T(8,128)(2,1)} %get-tuple-element.144.hid_ref, ...), custom_call_target="tpu_custom_call" | custom-call | flops 10871635968 | bytes 31457280 | tf_op jit(solution)/shard_map/feed_gradients/pallas_call | solution.py:967
  209.3 1.7 collective-permute-start.9
  211.0 35.5 %attention_backward.3.cj_ref = bf16[3,1024,768]{2,1,0:T(8,128)(2,1)} custom-call(bf16[12,1024,128]{2,1,0:T(8,128)(2,1)} %get-tuple-element.141.refs_0_, bf16[12,1024,128]{2,1,0:T(8,128)(2,1)} %get-tuple-element.137.k_ref.refs_1_, bf16[12,1024,128]{2,1,0:T(8,128)(2,1)} %get-tuple-element.138.v_ref.refs_2_, bf16[1024,768]{1,0:T(8,128)(2,1)} %get-tuple-element.157.refs_3_, ...), custom_call_target="tpu_custom_call" | custom-call | flops 32212254720 | bytes 18874368 | tf_op jit(solution)/shard_map/attention_backward/pallas_call | solution.py:851
  246.5 0.8 copy-done.7
  247.7 0.9 copy-done.9
  248.6 6.0 %add_convert_fusion.2 = (bf16[8,448,384]{2,1,0:T(8,128)(2,1)}, bf16[8,448,384]{2,1,0:T(8,128)(2,1)S(1)}) fusion(bf16[16,448,384]{2,1,0:T(8,128)(2,1)} %collective-permute-done.10, bf16[16,448,384]{2,1,0:T(8,128)(2,1)} %get-tuple-element.166), kind=kLoop, calls=%fused_computation.2 | loop fusion | flops 11010048 | bytes 16515072 | tf_op jit(solution)/shard_map/convert_element_type | solution.py:1128
  254.6 1.5 collective-permute-start.14
  256.1 11.1 %joint_backward.1 = (bf16[1024,768]{1,0:T(8,128)(2,1)}, f32[4,768]{1,0:T(4,128)}) custom-call(s32[1]{0:T(128)} %bitcast.sec_ref, bf16[3,1024,768]{2,1,0:T(8,128)(2,1)} %attention_backward.3.cj_ref, bf16[1024,768]{1,0:T(8,128)(2,1)} %get-tuple-element.135.y_ref.x_ref, f32[1024,768]{1,0:T(8,128)} %get-tuple-element.169.cm_ref, ...), custom_call_target="tpu_custom_call" | custom-call | flops 3623878656 | bytes 16777216 | tf_op jit(solution)/shard_map/joint_backward/pallas_call | solution.py:898
  267.2 11.0 %joint_gradients.1 = (bf16[16,160,384]{2,1,0:T(8,128)(2,1)}, bf16[16,160,384]{2,1,0:T(8,128)(2,1)}) custom-call(s32[1]{0:T(128)} %bitcast.sec_ref, s32[32]{0:T(128)} %broadcast_select_fusion.4.order_ref, bf16[3,1024,768]{2,1,0:T(8,128)(2,1)} %attention_backward.3.cj_ref, bf16[1024,768]{1,0:T(8,128)(2,1)} %get-tuple-element.171.n_ref, ...), custom_call_target="tpu_custom_call" | custom-call | flops 3623878656 | bytes 14680064 | tf_op jit(solution)/shard_map/joint_gradients/pallas_call | solution.py:1024
  278.2 2.6 fusion.9
  280.8 3.4 collective-permute-start.13
  284.2 1.5 collective-permute-start.11
  285.8 2.2 collective-permute-start.12
  288.0 31.6 %feed_backward.3 = (bf16[1024,3072]{1,0:T(8,128)(2,1)}, f32[1024,768]{1,0:T(8,128)}, bf16[1024,768]{1,0:T(8,128)(2,1)}, bf16[1024,768]{1,0:T(8,128)(2,1)}, bf16[...) custom-call(s32[1]{0:T(128)} %bitcast.sec_ref, ...), custom_call_target="tpu_custom_call" | custom-call | flops 10871635968 | bytes 52428800 | tf_op jit(solution)/shard_map/feed_backward/pallas_call | solution.py:771
  319.6 3.9 add_convert_fusion.8
  323.4 3.5 add_convert_fusion.6
  327.0 1.5 collective-permute-start.16
  328.5 0.6 collective-permute-start.17
  329.1 26.6 %feed_gradients.3 = (bf16[16,448,384]{2,1,0:T(8,128)(2,1)}, bf16[16,448,384]{2,1,0:T(8,128)(2,1)}) custom-call(s32[1]{0:T(128)} %bitcast.sec_ref, s32[32]{0:T(128)} %broadcast_select_fusion.4.order_ref, bf16[1024,3072]{1,0:T(8,128)(2,1)} %get-tuple-element.187.cb_ref, bf16[1024,3072]{1,0:T(8,128)(2,1)} %get-tuple-element.176.hid_ref, ...), custom_call_target="tpu_custom_call" | custom-call | flops 10871635968 | bytes 31457280 | tf_op jit(solution)/shard_map/feed_gradients/pallas_call | solution.py:967
  355.7 2.4 add_convert_fusion.12
  358.1 1.4 add_convert_fusion.10
  359.5 2.0 pad_maximum_fusion
  361.5 0.9 collective-permute-start.20
  362.5 1.6 collective-permute-start.19
  364.0 19.4 %attention_backward.4.refs_7_ = bf16[3,1024,768]{2,1,0:T(8,128)(2,1)} custom-call(bf16[12,1024,128]{2,1,0:T(8,128)(2,1)} %get-tuple-element.164.refs_0_, bf16[12,1024,128]{2,1,0:T(8,128)(2,1)} %get-tuple-element.130.k_ref.refs_1_, bf16[12,1024,128]{2,1,0:T(8,128)(2,1)} %get-tuple-element.131.v_ref.refs_2_, bf16[1024,768]{1,0:T(8,128)(2,1)} %get-tuple-element.199.refs_3_, ...), custom_call_target="tpu_custom_call" | custom-call | flops 16106127360 | bytes 9437184 | tf_op jit(solution)/shard_map/attention_backward/pallas_call | solution.py:851
  383.5 2.1 add_convert_fusion.16
  385.6 2.1 add_convert_fusion.14
  387.7 6.4 %add_convert_fusion = (bf16[8,448,384]{2,1,0:T(8,128)(2,1)}, bf16[8,448,384]{2,1,0:T(8,128)(2,1)}) fusion(bf16[16,448,384]{2,1,0:T(8,128)(2,1)} %collective-permute-done.18, bf16[16,448,384]{2,1,0:T(8,128)(2,1)} %get-tuple-element.200), kind=kLoop, calls=%fused_computation | loop fusion | flops 11010048 | bytes 16515072 | tf_op jit(solution)/shard_map/convert_element_type | solution.py:1128
  394.1 1.1 collective-permute-start.22
  395.4 1.9 maximum_bitcast_fusion
  397.3 0.4 collective-permute-start.23
  397.8 2.6 collective-permute-start.21
  400.3 19.2 %attention_backward.5.cj_ref = bf16[3,1024,768]{2,1,0:T(8,128)(2,1)} custom-call(bf16[12,1024,128]{2,1,0:T(8,128)(2,1)} %get-tuple-element.164.refs_0_, bf16[12,1024,128]{2,1,0:T(8,128)(2,1)} %get-tuple-element.130.k_ref.refs_1_, bf16[12,1024,128]{2,1,0:T(8,128)(2,1)} %get-tuple-element.131.v_ref.refs_2_, ...), custom_call_target="tpu_custom_call", output_to_operand_aliasing={{}: (7, {})} | custom-call | flops 16106127360 | bytes 9437184 | tf_op jit(solution)/shard_map/attention_backward/pallas_call | solution.py:851
  420.1 7.4 %collective-permute-done.24 = bf16[1,160,384]{2,1,0:T(8,128)(2,1)S(1)} collective-permute-done((bf16[1,160,384]{2,1,0:T(8,128)(2,1)S(1)}, bf16[1,160,384]{2,1,0:T(8,128)(2,1)S(1)}, u32[]{:S(2)}, u32[]{:S(2)}) %collective-permute-start.24) | collective-permute-done | bytes 122912 | tf_op jit(solution)/shard_map/ppermute | solution.py:1119
  427.6 1.0 pad_maximum_fusion.3.done_ref
  428.6 4.0 add_convert_fusion.4
  432.6 64.0 %last_step.1 = (f32[2,608,384]{2,1,0:T(8,128)}, bf16[512,768]{1,0:T(8,128)(2,1)}, bf16[3,512,768]{2,1,0:T(8,128)(2,1)}) custom-call(bf16[3,1024,768]{2,1,0:T(8,128)(2,1)} %attention_backward.5.cj_ref, bf16[1024,768]{1,0:T(8,128)(2,1)} %get-tuple-element.210.n_ref, bf16[1024,768]{1,0:T(8,128)(2,1)} %get-tuple-element.134.x_ref, ...), custom_call_target="tpu_custom_call" | custom-call | bytes 104857600 | tf_op jit(solution)/shard_map/last_step/pallas_call | solution.py:1331
  496.6 1.4 select_bitcast_fusion
  498.0 0.5 copy-done.5
  498.8 0.4 pad_maximum_fusion.1
  499.5 3.8 gradient_outputs.1
  503.3 3.0 maximum_convert_fusion
  (56 shorter events, 2.9 us)
Async XLA Ops:
  0.6 24.1 %collective-permute-start.2 = (bf16[768,2304]{1,0:T(8,128)(2,1)}, bf16[768,2304]{1,0:T(8,128)(2,1)S(1)}, u32[]{:S(2)}, u32[]{:S(2)}) collective-permute-start(bf16[768,2304]{1,0:T(8,128)(2,1)} %bitcast.81), channel_id=1, source_target_pairs={{0,16},{16,0},{1,17},{17,1},{2,18},{18,2},{3,19},{19,3},{4,20},{20... | collective-permute-start | bytes 10616840 | tf_op jit(solution)/shard_map/ppermute | solution.py:1438
  1.2 63.6 %collective-permute-start.4 = (bf16[768,3072]{1,0:T(8,128)(2,1)}, bf16[768,3072]{1,0:T(8,128)(2,1)}, u32[]{:S(2)}, u32[]{:S(2)}) collective-permute-start(bf16[768,3072]{1,0:T(8,128)(2,1)} %bitcast.71), channel_id=1, source_target_pairs={{0,16},{16,0},{1,17},{17,1},{2,18},{18,2},{3,19},{19,3},{4,20},{20... | collective-permute-start | bytes 14155784 | tf_op jit(solution)/shard_map/ppermute | solution.py:1438
  1.2 63.5 %collective-permute-start.5 = (bf16[3072,768]{1,0:T(8,128)(2,1)}, bf16[3072,768]{1,0:T(8,128)(2,1)}, u32[]{:S(2)}, u32[]{:S(2)}) collective-permute-start(bf16[3072,768]{1,0:T(8,128)(2,1)} %bitcast.76), channel_id=1, source_target_pairs={{0,16},{16,0},{1,17},{17,1},{2,18},{18,2},{3,19},{19,3},{4,20},{20... | collective-permute-start | bytes 14155784 | tf_op jit(solution)/shard_map/ppermute | solution.py:1438
  3.7 21.0 %collective-permute-start = (bf16[512,768]{1,0:T(8,128)(2,1)}, bf16[512,768]{1,0:T(8,128)(2,1)}, u32[]{:S(2)}, u32[]{:S(2)}) collective-permute-start(bf16[512,768]{1,0:T(8,128)(2,1)} %dynamic-slice_bitcast_fusion.6), channel_id=1, source_target_pairs={{0,1},{1,0},{2,3},{3,2},{4,5},{5,4},{6,7},{7,6},{8,9},{9,8},{10,11... | collective-permute-start | bytes 2359304 | tf_op jit(solution)/shard_map/ppermute | solution.py:1437
  11.2 9.8 %collective-permute-start.1 = (f32[1,12288]{1,0:T(1,128)}, f32[1,12288]{1,0:T(1,128)}, u32[]{:S(2)}, u32[]{:S(2)}) collective-permute-start(f32[1,12288]{1,0:T(1,128)} %get-tuple-element.125), channel_id=1, source_target_pairs={{0,16},{16,0},{1,17},{17,1},{2,18},{18,2},{3,19},{19,3},{4,20},{20... | collective-permute-start | bytes 147464 | tf_op jit(solution)/shard_map/ppermute | solution.py:1442
  20.9 43.8 %collective-permute-start.3 = (bf16[768,768]{1,0:T(8,128)(2,1)}, bf16[768,768]{1,0:T(8,128)(2,1)}, u32[]{:S(2)}, u32[]{:S(2)}) collective-permute-start(bf16[768,768]{1,0:T(8,128)(2,1)} %bitcast.87), channel_id=1, source_target_pairs={{0,16},{16,0},{1,17},{17,1},{2,18},{18,2},{3,19},{19,3},{4,20},{20... | collective-permute-start | bytes 3538952 | tf_op jit(solution)/shard_map/ppermute | solution.py:1438
  24.8 1.8 copy-start
  41.0 22.4 %collective-permute-start.6 = (bf16[512,768]{1,0:T(8,128)(2,1)S(1)}, bf16[512,768]{1,0:T(8,128)(2,1)S(1)}, u32[]{:S(2)}, u32[]{:S(2)}) collective-permute-start(bf16[512,768]{1,0:T(8,128)(2,1)S(1)} %get-tuple-element.273), channel_id=1, source_target_pairs={{0,1},{1,0},{2,3},{3,2},{4,5},{5,4},{6,7},{7,6},{8,9},{9,8},{10,11... | collective-permute-start | bytes 2359304 | tf_op jit(solution)/shard_map/ppermute | solution.py:1459
  123.2 24.8 %copy-start.2 = (bf16[1024,768]{1,0:T(8,128)(2,1)S(1)}, bf16[1024,768]{1,0:T(8,128)(2,1)}, u32[]{:S(2)}) copy-start(bf16[1024,768]{1,0:T(8,128)(2,1)} %get-tuple-element.135.y_ref.x_ref) | copy-start | bytes 4718596
  208.8 39.8 %collective-permute-start.10 = (bf16[16,448,384]{2,1,0:T(8,128)(2,1)}, bf16[16,448,384]{2,1,0:T(8,128)(2,1)}, u32[]{:S(2)}, u32[]{:S(2)}) collective-permute-start(bf16[16,448,384]{2,1,0:T(8,128)(2,1)} %get-tuple-element.167), channel_id=1, source_target_pairs={{0,16},{16,0},{1,17},{17,1},{2,18},{18,2},{3,19},{19,3},{4,20},{20... | collective-permute-start | bytes 16515080 | tf_op jit(solution)/shard_map/ppermute | solution.py:1111
  208.8 37.7 %collective-permute-start.7 = (bf16[512,768]{1,0:T(8,128)(2,1)}, bf16[512,768]{1,0:T(8,128)(2,1)S(1)}, u32[]{:S(2)}, u32[]{:S(2)}) collective-permute-start(bf16[512,768]{1,0:T(8,128)(2,1)} %get-tuple-element.158), channel_id=1, source_target_pairs={{0,1},{1,0},{16,17},{17,16},{2,3},{3,2},{18,19},{19,18},{4,5},{5,4... | collective-permute-start | bytes 2359304 | tf_op jit(solution)/shard_map/ppermute | solution.py:1478
  209.1 37.4 %collective-permute-start.8 = (bf16[512,768]{1,0:T(8,128)(2,1)S(1)}, bf16[512,768]{1,0:T(8,128)(2,1)S(1)}, u32[]{:S(2)}, u32[]{:S(2)}) collective-permute-start(bf16[512,768]{1,0:T(8,128)(2,1)S(1)} %get-tuple-element.159), channel_id=1, source_target_pairs={{0,16},{1,17},{16,0},{17,1},{2,18},{3,19},{18,2},{19,3},{4,20},{5,... | collective-permute-start | bytes 2359304 | tf_op jit(solution)/shard_map/ppermute | solution.py:1478
  209.3 37.2 %collective-permute-start.9 = (bf16[512,768]{1,0:T(8,128)(2,1)S(1)}, bf16[512,768]{1,0:T(8,128)(2,1)S(1)}, u32[]{:S(2)}, u32[]{:S(2)}) collective-permute-start(bf16[512,768]{1,0:T(8,128)(2,1)S(1)} %get-tuple-element.160), channel_id=1, source_target_pairs={{0,17},{1,16},{16,1},{17,0},{2,19},{3,18},{18,3},{19,2},{4,21},{5,... | collective-permute-start | bytes 2359304 | tf_op jit(solution)/shard_map/ppermute | solution.py:1478
  246.5 0.9 copy-start.7
  246.5 1.2 copy-start.8
  247.7 0.9 copy-start.9
  254.6 68.8 %collective-permute-start.14 = (bf16[8,448,384]{2,1,0:T(8,128)(2,1)}, bf16[8,448,384]{2,1,0:T(8,128)(2,1)}, u32[]{:S(2)}, u32[]{:S(2)}) collective-permute-start(bf16[8,448,384]{2,1,0:T(8,128)(2,1)} %get-tuple-element.184), channel_id=1, source_target_pairs={{0,2},{1,3},{2,0},{3,1},{4,6},{5,7},{6,4},{7,5},{8,10},{9,11},{10,... | collective-permute-start | bytes 8257544 | tf_op jit(solution)/shard_map/ppermute | solution.py:1119
  278.2 41.4 %collective-permute-start.15 = (bf16[16,160,384]{2,1,0:T(8,128)(2,1)}, bf16[16,160,384]{2,1,0:T(8,128)(2,1)}, u32[]{:S(2)}, u32[]{:S(2)}) collective-permute-start(bf16[16,160,384]{2,1,0:T(8,128)(2,1)} %get-tuple-element.186), channel_id=1, source_target_pairs={{0,16},{16,0},{1,17},{17,1},{2,18},{18,2},{3,19},{19,3},{4,20},{20... | collective-permute-start | bytes 5898248 | tf_op jit(solution)/shard_map/ppermute | solution.py:1111
  280.8 47.7 %collective-permute-start.13 = (bf16[512,768]{1,0:T(8,128)(2,1)}, bf16[512,768]{1,0:T(8,128)(2,1)}, u32[]{:S(2)}, u32[]{:S(2)}) collective-permute-start(bf16[512,768]{1,0:T(8,128)(2,1)} %get-tuple-element.281), channel_id=1, source_target_pairs={{0,17},{1,16},{2,19},{3,18},{4,21},{5,20},{6,23},{7,22},{8,25},{9,... | collective-permute-start | bytes 2359304 | tf_op jit(solution)/shard_map/ppermute | solution.py:1492
  284.2 44.3 %collective-permute-start.11 = (bf16[512,768]{1,0:T(8,128)(2,1)}, bf16[512,768]{1,0:T(8,128)(2,1)}, u32[]{:S(2)}, u32[]{:S(2)}) collective-permute-start(bf16[512,768]{1,0:T(8,128)(2,1)} %get-tuple-element.281), channel_id=1, source_target_pairs={{16,17},{17,16},{18,19},{19,18},{20,21},{21,20},{22,23},{23,22},{2... | collective-permute-start | bytes 2359304 | tf_op jit(solution)/shard_map/ppermute | solution.py:1492
  285.8 42.7 %collective-permute-start.12 = (bf16[512,768]{1,0:T(8,128)(2,1)}, bf16[512,768]{1,0:T(8,128)(2,1)}, u32[]{:S(2)}, u32[]{:S(2)}) collective-permute-start(bf16[512,768]{1,0:T(8,128)(2,1)} %get-tuple-element.218), channel_id=1, source_target_pairs={{0,16},{1,17},{2,18},{3,19},{4,20},{5,21},{6,22},{7,23},{8,24},{9,... | collective-permute-start | bytes 2359304 | tf_op jit(solution)/shard_map/ppermute | solution.py:1492
  327.0 31.1 %collective-permute-start.16 = (bf16[4,448,384]{2,1,0:T(8,128)(2,1)}, bf16[4,448,384]{2,1,0:T(8,128)(2,1)S(1)}, u32[]{:S(2)}, u32[]{:S(2)}) collective-permute-start(bf16[4,448,384]{2,1,0:T(8,128)(2,1)} %get-tuple-element.196), channel_id=1, source_target_pairs={{0,1},{1,0},{2,3},{3,2},{4,5},{5,4},{6,7},{7,6},{8,9},{9,8},{10,11... | collective-permute-start | bytes 4128776 | tf_op jit(solution)/shard_map/ppermute | solution.py:1119
  328.5 27.2 %collective-permute-start.17 = (bf16[8,160,384]{2,1,0:T(8,128)(2,1)}, bf16[8,160,384]{2,1,0:T(8,128)(2,1)}, u32[]{:S(2)}, u32[]{:S(2)}) collective-permute-start(bf16[8,160,384]{2,1,0:T(8,128)(2,1)} %get-tuple-element.198), channel_id=1, source_target_pairs={{0,2},{1,3},{2,0},{3,1},{4,6},{5,7},{6,4},{7,5},{8,10},{9,11},{10,... | collective-permute-start | bytes 2949128 | tf_op jit(solution)/shard_map/ppermute | solution.py:1119
  329.1 26.6 %copy-start.3 = (bf16[8,160,384]{2,1,0:T(8,128)(2,1)S(1)}, bf16[8,160,384]{2,1,0:T(8,128)(2,1)}, u32[]{:S(2)}) copy-start(bf16[8,160,384]{2,1,0:T(8,128)(2,1)} %get-tuple-element.197) | copy-start | bytes 2949124
  359.5 28.2 %collective-permute-start.18 = (bf16[16,448,384]{2,1,0:T(8,128)(2,1)}, bf16[16,448,384]{2,1,0:T(8,128)(2,1)}, u32[]{:S(2)}, u32[]{:S(2)}) collective-permute-start(bf16[16,448,384]{2,1,0:T(8,128)(2,1)} %get-tuple-element.201), channel_id=1, source_target_pairs={{0,16},{16,0},{1,17},{17,1},{2,18},{18,2},{3,19},{19,3},{4,20},{20... | collective-permute-start | bytes 16515080 | tf_op jit(solution)/shard_map/ppermute | solution.py:1111
  361.5 21.9 %collective-permute-start.20 = (bf16[4,160,384]{2,1,0:T(8,128)(2,1)}, bf16[4,160,384]{2,1,0:T(8,128)(2,1)}, u32[]{:S(2)}, u32[]{:S(2)}) collective-permute-start(bf16[4,160,384]{2,1,0:T(8,128)(2,1)} %get-tuple-element.205), channel_id=1, source_target_pairs={{0,1},{1,0},{2,3},{3,2},{4,5},{5,4},{6,7},{7,6},{8,9},{9,8},{10,11... | collective-permute-start | bytes 1474568 | tf_op jit(solution)/shard_map/ppermute | solution.py:1119
  362.5 23.1 %collective-permute-start.19 = (bf16[2,448,384]{2,1,0:T(8,128)(2,1)}, bf16[2,448,384]{2,1,0:T(8,128)(2,1)}, u32[]{:S(2)}, u32[]{:S(2)}) collective-permute-start(bf16[2,448,384]{2,1,0:T(8,128)(2,1)} %get-tuple-element.203), channel_id=1, source_target_pairs={{0,4},{1,5},{2,6},{3,7},{4,0},{5,1},{6,2},{7,3},{8,12},{9,13},{10,... | collective-permute-start | bytes 2064392 | tf_op jit(solution)/shard_map/ppermute | solution.py:1119
  364.0 21.6 %copy-start.4 = (bf16[2,448,384]{2,1,0:T(8,128)(2,1)S(1)}, bf16[2,448,384]{2,1,0:T(8,128)(2,1)}, u32[]{:S(2)}) copy-start(bf16[2,448,384]{2,1,0:T(8,128)(2,1)} %get-tuple-element.202) | copy-start | bytes 2064388
  394.1 34.5 %collective-permute-start.22 = (bf16[8,448,384]{2,1,0:T(8,128)(2,1)}, bf16[8,448,384]{2,1,0:T(8,128)(2,1)}, u32[]{:S(2)}, u32[]{:S(2)}) collective-permute-start(bf16[8,448,384]{2,1,0:T(8,128)(2,1)} %get-tuple-element.213), channel_id=1, source_target_pairs={{0,2},{1,3},{2,0},{3,1},{4,6},{5,7},{6,4},{7,5},{8,10},{9,11},{10,... | collective-permute-start | bytes 8257544 | tf_op jit(solution)/shard_map/ppermute | solution.py:1119
  397.3 22.7 %copy-start.6 = (bf16[1,448,384]{2,1,0:T(8,128)(2,1)S(1)}, bf16[1,448,384]{2,1,0:T(8,128)(2,1)}, u32[]{:S(2)}) copy-start(bf16[1,448,384]{2,1,0:T(8,128)(2,1)} %get-tuple-element.207) | copy-start | bytes 1032196
  397.3 22.2 %collective-permute-start.23 = (bf16[2,160,384]{2,1,0:T(8,128)(2,1)}, bf16[2,160,384]{2,1,0:T(8,128)(2,1)S(1)}, u32[]{:S(2)}, u32[]{:S(2)}) collective-permute-start(bf16[2,160,384]{2,1,0:T(8,128)(2,1)} %get-tuple-element.216), channel_id=1, source_target_pairs={{0,4},{1,5},{2,6},{3,7},{4,0},{5,1},{6,2},{7,3},{8,12},{9,13},{10,... | collective-permute-start | bytes 737288 | tf_op jit(solution)/shard_map/ppermute | solution.py:1119
  397.8 22.2 %collective-permute-start.21 = (bf16[1,448,384]{2,1,0:T(8,128)(2,1)}, bf16[1,448,384]{2,1,0:T(8,128)(2,1)S(1)}, u32[]{:S(2)}, u32[]{:S(2)}) collective-permute-start(bf16[1,448,384]{2,1,0:T(8,128)(2,1)} %get-tuple-element.208), channel_id=1, source_target_pairs={{0,8},{1,9},{2,10},{3,11},{4,12},{5,13},{6,14},{7,15},{8,0},{9,1},... | collective-permute-start | bytes 1032200 | tf_op jit(solution)/shard_map/ppermute | solution.py:1119
  419.5 9.1 %copy-start.1 = (bf16[8,448,384]{2,1,0:T(8,128)(2,1)S(1)}, bf16[8,448,384]{2,1,0:T(8,128)(2,1)}, u32[]{:S(2)}) copy-start(bf16[8,448,384]{2,1,0:T(8,128)(2,1)} %get-tuple-element.212) | copy-start | bytes 8257540
  419.6 7.9 %collective-permute-start.24 = (bf16[1,160,384]{2,1,0:T(8,128)(2,1)S(1)}, bf16[1,160,384]{2,1,0:T(8,128)(2,1)S(1)}, u32[]{:S(2)}, u32[]{:S(2)}) collective-permute-start(bf16[1,160,384]{2,1,0:T(8,128)(2,1)S(1)} %add_convert_fusion.18), channel_id=1, source_target_pairs={{0,8},{1,9},{2,10},{3,11},{4,12},{5,13},{6,14},{7,15},{8,0},{9,1},... | collective-permute-start | bytes 368648 | tf_op jit(solution)/shard_map/ppermute | solution.py:1119
  496.6 1.9 copy-start.5

commit v4 on v3

--- a/solution.py
+++ b/solution.py
@@ -567,7 +567,7 @@
         ),
         out_shape=[jax.ShapeDtypeStruct((rows, width), BF16)] * 2 + [jax.ShapeDtypeStruct((heads, rows, 128), BF16)] * 3,
         compiler_params=pltpu.CompilerParams(vmem_limit_bytes=VLIM),
-        cost_estimate=pl.CostEstimate(flops=2 * rows * width * 3 * width, bytes_accessed=16 * 1024 * 1024, transcendentals=0),
+        cost_estimate=pl.CostEstimate(flops=1 * 2 * rows * width * 3 * width, bytes_accessed=16 * 1024 * 1024, transcendentals=0),
         name="joint_projection",
     )(sec, mine.reshape(1).astype(jnp.int32), x, y, pack, own, other, cosine, sine, labels)
 
@@ -614,7 +614,7 @@
         out_specs=[pl.BlockSpec((rows, 128), lambda i: (0, i)), hd],
         out_shape=[jax.ShapeDtypeStruct((rows, heads * HEAD_DIM), F32), jax.ShapeDtypeStruct(q.shape, BF16)],
         compiler_params=pltpu.CompilerParams(vmem_limit_bytes=VLIM),
-        cost_estimate=pl.CostEstimate(flops=16 * heads * rows * rows * HEAD_DIM, bytes_accessed=16 * 1024 * 1024, transcendentals=0),
+        cost_estimate=pl.CostEstimate(flops=1 * 16 * heads * rows * rows * HEAD_DIM, bytes_accessed=16 * 1024 * 1024, transcendentals=0),
         name="attention_forward",
     )(q, k, v)
 
@@ -682,14 +682,14 @@
         out_shape=[S((rows, width), BF16), S((rows, width), F32), S((rows, wide), BF16), S((rows, wide), BF16), S((rows, 128), F32)],
         scratch_shapes=[pltpu.VMEM(wo[0].shape, BF16), pltpu.VMEM(wu[0].shape, BF16), pltpu.VMEM(wd[0].shape, BF16), pltpu.VMEM((tb, wide), F32), pltpu.SemaphoreType.DMA((3,))],
         compiler_params=pltpu.CompilerParams(vmem_limit_bytes=VLIM),
-        cost_estimate=pl.CostEstimate(flops=2 * rows * width * (2 * wide + width), bytes_accessed=40 * 1024 * 1024, transcendentals=0),
+        cost_estimate=pl.CostEstimate(flops=1 * 2 * rows * width * (2 * wide + width), bytes_accessed=40 * 1024 * 1024, transcendentals=0),
         name="feed_forward",
     )(sec, attended, x, pack, *wo, *wu, *wd)
 
 
 def feed_back_kernel(layer, sec_ref, c_ref, hid_ref, gp_ref, st_ref, mixed_ref, at_ref,
                      pack_ref, wo0, wo1, wu0, wu1, wd0, wd1,
-                     cb_ref, cm_ref, cl_ref, ch_ref, n2_ref, in_ref, wide_ref, thin_ref,
+                     cb_ref, cm_ref, ct_ref, cl_ref, ch_ref, n2_ref, in_ref, wide_ref, thin_ref,
                      wo, wu, wd, sloped, wide_acc, thin_acc, sem):
     now = pl.program_id(0)
     ig_ref, sg_ref, hg_ref = vectors_of(pack_ref, c_ref.shape[-1], INNER_GAIN, SECOND_GAIN, HIDDEN_GAIN)
@@ -699,8 +699,9 @@
         wide_acc[...] = jnp.zeros_like(wide_acc)
         thin_acc[...] = jnp.zeros_like(thin_acc)
 
-    arrive = fetch_weights(layer, sec_ref, [(wo0, wo1, wo), (wu0, wu1, wu), (wd0, wd1, wd)], sem)
+    arrive = fetch_weights(layer, sec_ref, [(wd0, wd1, wd), (wu0, wu1, wu), (wo0, wo1, wo)], sem)
     low = c_ref[...]
+    ct_ref[...] = low.T
     outer = low.astype(F32)
     thin_acc[0] += fold(outer)
     wide = hg_ref.shape[-1]
@@ -710,7 +711,7 @@
     def fall(chunk):
         return nt(low, wd[pl.ds(chunk * step, step), :])
 
-    arrive(2)
+    arrive(0)
     later = fall(0)
     sum_moved = 0.0
     sum_slope = 0.0
@@ -744,9 +745,9 @@
     mixed = outer + norm_back(slope_two * sg_ref[...], unit, scale)
     cm_ref[...] = mixed
     mixed_low = mixed.astype(BF16)
-    cl_ref[...] = mixed_low
+    cl_ref[...] = mixed_low.T
     thin_acc[2] += fold(mixed_low.astype(F32))
-    arrive(0)
+    arrive(2)
     slope = nt(mixed_low, wo[...])
     unit, scale = normalize(at_ref[...])
     in_ref[...] = (unit * ig_ref[...]).astype(BF16)
@@ -767,17 +768,18 @@
     wide = wd[0].shape[0]
     const = lambda n, m=1: pl.BlockSpec((m, n), lambda i: (0, 0))
     tok = lambda n: pl.BlockSpec((tb, n), lambda i: (i, 0))
+    turned = pl.BlockSpec((width, tb), lambda i: (0, i))
     S = jax.ShapeDtypeStruct
     return pl.pallas_call(
         functools.partial(feed_back_kernel, layer),
         grid=(rows // tb,),
         in_specs=[SMEM, tok(width), tok(wide), tok(wide), tok(128), tok(width), tok(width), pack_spec(layer, pack)] + [ANY] * 6,
-        out_specs=[tok(wide), tok(width), tok(width), tok(width), tok(width), tok(width), const(wide, 2), const(width, 4)],
-        out_shape=[S((rows, wide), BF16), S((rows, width), F32), S((rows, width), BF16), S((rows, width), BF16), S((rows, width), BF16), S((rows, width), BF16), S((2, wide), F32), S((4, width), F32)],
+        out_specs=[tok(wide), tok(width), turned, turned, tok(width), tok(width), tok(width), const(wide, 2), const(width, 4)],
+        out_shape=[S((rows, wide), BF16), S((rows, width), F32), S((width, rows), BF16), S((width, rows), BF16), S((rows, width), BF16), S((rows, width), BF16), S((rows, width), BF16), S((2, wide), F32), S((4, width), F32)],
         scratch_shapes=[pltpu.VMEM(wo[0].shape, BF16), pltpu.VMEM(wu[0].shape, BF16), pltpu.VMEM(wd[0].shape, BF16),
                         pltpu.VMEM((tb, wide), F32), pltpu.VMEM((2, 8, wide), F32), pltpu.VMEM((4, 8, width), F32), pltpu.SemaphoreType.DMA((3,))],
         compiler_params=pltpu.CompilerParams(vmem_limit_bytes=VLIM),
-        cost_estimate=pl.CostEstimate(flops=2 * rows * width * (2 * wide + width), bytes_accessed=50 * 1024 * 1024, transcendentals=0),
+        cost_estimate=pl.CostEstimate(flops=1 * 2 * rows * width * (2 * wide + width), bytes_accessed=50 * 1024 * 1024, transcendentals=0),
         name="feed_backward",
     )(sec, c, hidden, gp, st, mixed, attended, pack, *wo, *wu, *wd)
 
@@ -858,7 +860,7 @@
         scratch_shapes=[pltpu.VMEM((128, rows), F32), pltpu.VMEM((128, rows), F32), pltpu.VMEM((2, rows, 128), F32),
                         pltpu.VMEM((2, rows, rows), BF16), pltpu.VMEM((2, rows, rows), BF16)],
         compiler_params=pltpu.CompilerParams(vmem_limit_bytes=VLIM),
-        cost_estimate=pl.CostEstimate(flops=80 * count * rows * rows * HEAD_DIM, bytes_accessed=3 * count * 1024 * 1024, transcendentals=0),
+        cost_estimate=pl.CostEstimate(flops=1 * 80 * count * rows * rows * HEAD_DIM, bytes_accessed=3 * count * 1024 * 1024, transcendentals=0),
         name="attention_backward",
     )(q, k, v, ch, attended, cosine, sine, *extra)
 
@@ -903,66 +905,84 @@
         out_shape=[S((rows, width), BF16), S((4, width), F32)],
         scratch_shapes=[pltpu.VMEM(own.shape, BF16), pltpu.VMEM((4, 8, width), F32), pltpu.SemaphoreType.DMA((1,))],
         compiler_params=pltpu.CompilerParams(vmem_limit_bytes=VLIM),
-        cost_estimate=pl.CostEstimate(flops=2 * rows * width * 3 * width, bytes_accessed=16 * 1024 * 1024, transcendentals=0),
+        cost_estimate=pl.CostEstimate(flops=1 * 2 * rows * width * 3 * width, bytes_accessed=16 * 1024 * 1024, transcendentals=0),
         name="joint_backward",
     )(sec, cj, x, cm, pack, own, other)
 
 
-def feed_grads_kernel(sec_ref, order_ref, cb_ref, hid_ref, c_ref, n2_ref, cm_ref, in_ref, wide_ref, thin_ref,
-                      keep_ref, send_ref, c_t, cm_t):
+def feed_grads_kernel(sec_ref, order_ref, cb_ref, hid_ref, c_t, n2_ref, cm_t, in_ref, wide_ref, thin_ref,
+                      keep_ref, send_ref, held, sem):
     step = pl.program_id(0)
     sec = sec_ref[0]
     parts = order_ref.shape[0] // 2
-    half = n2_ref.shape[-1] // 2
-    up_rows = cb_ref.shape[-1] // 2
-    thin = c_ref.shape[-1] // parts
+    width = n2_ref.shape[-1]
+    half = width // 2
+    wide = wide_ref.shape[-1]
+    up_rows = wide // parts
+    thin = width // parts
+    span = cb_ref.shape[-1]
+    subs = span // up_rows
     steps = pl.num_programs(0) // 2
     outs = (keep_ref, send_ref)
+    last = 2 * up_rows + thin
     sides = [pl.ds(pl.multiple_of(which * half, 128), half) for which in (sec, 1 - sec)]
+
+    def leave(side, at, begin, count):
+        rows = pl.ds(begin, count)
+        pltpu.make_async_copy(held.at[side, at, rows], outs[side].at[at, rows], sem).start()
 
     @pl.when(step == 0)
     def _():
-        c_t[...] = c_ref[...].T
-        cm_t[...] = cm_ref[...].T
-        for window in range(parts // 2):
+        for window in range(wide // half):
             at = pl.ds(window * half, half)
-            far = pl.ds(window // (parts // 4) * half, half)
+            far = pl.ds(window // (wide // width // 1) * half, half)
             rows = jnp.concatenate([wide_ref[:, at], thin_ref[:, far], jnp.zeros((10, half), F32)], axis=0).astype(BF16)
             for side in range(2):
-                for sub in range(2):
-                    outs[side][order_ref[side * parts + window * 2 + sub], up_rows * 2 + thin:, :] = rows
+                for sub in range(half // up_rows):
+                    held[side, order_ref[side * parts + window * (half // up_rows) + sub], last:, :] = rows
+        for side in range(2):
+            out = nn(cm_t[...], in_ref[:, sides[side]]).astype(BF16)
+            for part in range(parts):
+                at = order_ref[side * parts + part]
+                held[side, at, 2 * up_rows:last, :] = out[thin * part:thin * (part + 1)]
+                leave(side, at, 2 * up_rows, thin + 16)
 
     for side in range(2):
         up = tn(cb_ref[...], n2_ref[:, sides[side]]).astype(BF16)
-        for sub in range(2):
-            at = order_ref[side * parts + step * 2 + sub]
-            outs[side][at, 0:up_rows, :] = up[sub * up_rows:(sub + 1) * up_rows]
+        for sub in range(subs):
+            at = order_ref[side * parts + step * subs + sub]
+            held[side, at, 0:up_rows, :] = up[sub * up_rows:(sub + 1) * up_rows]
+            leave(side, at, 0, up_rows)
 
     down = nn(c_t[...], hid_ref[...]).astype(BF16)
-    rows = pl.ds(pl.multiple_of(up_rows + thin * (step % steps), 16), thin)
-    for side in range(2):
-        @pl.when(step // steps == side)
+    side = step // steps
+    for which in range(span // half):
+        begin = pl.multiple_of(up_rows + thin * (step % steps * (span // half) + which), 16)
+        for part in range(parts):
+            held[side, order_ref[side * parts + part], pl.ds(begin, thin), :] = down[thin * part:thin * (part + 1), which * half:(which + 1) * half]
+
+    begin = pl.multiple_of(up_rows + thin * (step % steps * (span // half)), 16)
+    rows = pl.ds(begin, thin * (span // half))
+    for number in range(2):
+        @pl.when(side == number)
         def _():
-            for part in range(parts):
-                outs[side][order_ref[side * parts + part], rows, :] = down[thin * part:thin * (part + 1)]
-
-        @pl.when(step == side * steps)
-        def _():
-            out = nn(cm_t[...], in_ref[:, sides[side]]).astype(BF16)
-            for part in range(parts):
-                outs[side][order_ref[side * parts + part], 2 * up_rows:2 * up_rows + thin, :] = out[thin * part:thin * (part + 1)]
-
-
-def feed_grads(sec, order, cb, hidden, c, n2, cm, inner, wide_sums, thin_sums):
-    rows, width = c.shape
+            pltpu.make_async_copy(held.at[number, :, rows], outs[number].at[:, rows], sem).start()
+
+    @pl.when(step == pl.num_programs(0) - 1)
+    def _():
+        for number in range(2):
+            pltpu.make_async_copy(held.at[number], outs[number], sem).wait()
+
+
+def feed_grads(sec, order, cb, hidden, c_t, n2, cm_t, inner, wide_sums, thin_sums):
+    rows, width = n2.shape
     wide = cb.shape[-1]
     parts = order.shape[0] // 2
     half = width // 2
-    steps = wide // half
+    steps = wide // width
     up_rows = wide // parts
     total = 2 * up_rows + width // parts + 16
     full = lambda n, m=rows: pl.BlockSpec((m, n), lambda i, s, o: (0, 0))
-    out_spec = pl.BlockSpec((parts, total, half), lambda i, s, o: (0, 0, 0))
     out_shape = jax.ShapeDtypeStruct((parts, total, half), BF16)
     return pl.pallas_call(
         feed_grads_kernel,
@@ -970,21 +990,21 @@
             num_scalar_prefetch=2,
             grid=(steps,),
             in_specs=[
-                pl.BlockSpec((rows, half), lambda i, s, o: (0, i)),
-                pl.BlockSpec((rows, half), lambda i, s, o: (0, jnp.where(i < steps // 2, s[0], 1 - s[0]) * (steps // 2) + i % (steps // 2))),
-                full(width), full(width), full(width), full(width), full(wide, 2), full(width, 4),
+                pl.BlockSpec((rows, width), lambda i, s, o: (0, i)),
+                pl.BlockSpec((rows, width), lambda i, s, o: (0, jnp.where(i < steps // 2, s[0], 1 - s[0]) * (steps // 2) + i % (steps // 2))),
+                full(rows, width), full(width), full(rows, width), full(width), full(wide, 2), full(width, 4),
             ],
-            out_specs=[out_spec, out_spec],
-            scratch_shapes=[pltpu.VMEM((width, rows), BF16), pltpu.VMEM((width, rows), BF16)],
+            out_specs=[ANY, ANY],
+            scratch_shapes=[pltpu.VMEM((2, parts, total, half), BF16), pltpu.SemaphoreType.DMA],
         ),
         out_shape=[out_shape, out_shape],
         compiler_params=pltpu.CompilerParams(vmem_limit_bytes=VLIM),
-        cost_estimate=pl.CostEstimate(flops=2 * rows * width * (2 * wide + width), bytes_accessed=30 * 1024 * 1024, transcendentals=0),
+        cost_estimate=pl.CostEstimate(flops=1 * 2 * rows * width * (2 * wide + width), bytes_accessed=30 * 1024 * 1024, transcendentals=0),
         name="feed_gradients",
-    )(sec, order, cb, hidden, c, n2, cm, inner, wide_sums, thin_sums)
-
-
-def joint_grads_kernel(sec_ref, order_ref, cj_ref, n_ref, sums_ref, keep_ref, send_ref):
+    )(sec, order, cb, hidden, c_t, n2, cm_t, inner, wide_sums, thin_sums)
+
+
+def joint_grads_kernel(sec_ref, order_ref, cj_ref, n_ref, sums_ref, keep_ref, send_ref, found):
     step = pl.program_id(0)
     sec = sec_ref[0]
     parts = order_ref.shape[0] // 2
@@ -992,8 +1012,9 @@
     half = width // 2
     thick = 3 * width // parts
     outs = (keep_ref, send_ref)
+    found[...] = tn(cj_ref[0], n_ref[...]).astype(BF16)
     for side, which in enumerate((sec, 1 - sec)):
-        sums = tn(cj_ref[0], n_ref[:, pl.ds(pl.multiple_of(which * half, 128), half)]).astype(BF16)
+        columns = pl.ds(pl.multiple_of(which * half, 128), half)
         for block in range(3):
             @pl.when(step == block)
             def _():
@@ -1001,7 +1022,7 @@
                     low, high = max(thick * part, width * block), min(thick * (part + 1), width * (block + 1))
                     if low < high:
                         at = order_ref[side * parts + part]
-                        outs[side][at, low - thick * part:high - thick * part, :] = sums[low - width * block:high - width * block]
+                        outs[side][at, low - thick * part:high - thick * part, :] = found[low - width * block:high - width * block, columns]
 
     @pl.when(step == 0)
     def _():
@@ -1032,10 +1053,11 @@
                 pl.BlockSpec((4, width), lambda i, s, o: (0, 0)),
             ],
             out_specs=[out_spec, out_spec],
+            scratch_shapes=[pltpu.VMEM((width, width), BF16)],
         ),
         out_shape=[out_shape, out_shape],
         compiler_params=pltpu.CompilerParams(vmem_limit_bytes=VLIM),
-        cost_estimate=pl.CostEstimate(flops=6 * rows * width * width, bytes_accessed=14 * 1024 * 1024, transcendentals=0),
+        cost_estimate=pl.CostEstimate(flops=1 * 6 * rows * width * width, bytes_accessed=14 * 1024 * 1024, transcendentals=0),
         name="joint_gradients",
     )(sec, order, cj, normed, sums)
 
@@ -1496,11 +1518,11 @@
 
     for layer in (1, 0):
         state, normed, query, k, v, attended, mixed, hidden, bend, stats = kept[layer]
-        cb, cm, cm_low, ch, n2, inner, wide_sums, thin_sums = feed_back(
+        cb, cm, slope_t, mixed_t, ch, n2, inner, wide_sums, thin_sums = feed_back(
             layer, sec, slope, hidden, bend, stats, mixed, attended, pack, output_pair, up_pair, down_pair)
         if layer == 0:
             cb = advance(cb, flights[FEED, 1], flights[JOINT, 1])
-        flights[FEED, layer] = Reduction(*feed_grads(sec, order, cb, hidden, slope, n2, cm_low, inner, wide_sums, thin_sums), sizes)
+        flights[FEED, layer] = Reduction(*feed_grads(sec, order, cb, hidden, slope_t, n2, mixed_t, inner, wide_sums, thin_sums), sizes)
         if layer == 1:
             ch = advance(ch, flights[FEED, 1])
             cj = attend_back(query, k, v, ch, attended, cosine, sine)

time: 515 us -> 501 us (0.973)
  Pallas kernels: 401 us -> 383 us
    pallas_call x2, Pallas kernels: 53.2 us -> 40 us  [feed_grads(): pl.pallas_call(feed_grads_kernel, grid_spec=pltpu.PrefetchScalarGridSpec(...]
  transfers between devices with their start and end apart: 25 -> 25, of which waited for: 3 -> 4; matrix products, arithmetic and copies ran while one was open for 6% -> 6% of each run, Pallas kernels for 38% -> 37%
where the time goes in v4:
time: 501 us; the launch traced here: 493 us
  Pallas kernels  383 us (76%)
  other arithmetic  48.4 us (10%)
  starting transfers between devices  27.1 us (5%)
  waiting for transfers between devices  21.5 us (4%)
  local copies, waits for them, and re-layouts  11.6 us (2%)
    pallas_call x3, Pallas kernels, attend_back(): pl.pallas_call(kernel, grid=(count,), in_specs=[hd, hd, hd, col, col, con...  74 us
    pallas_call x1, Pallas kernels, last_step(): pl.pallas_call(last_kernel, in_specs=[vm] * 5 + [ANY] * 2 + [vm] * 3, out...  62.8 us
    pallas_call x2, Pallas kernels, feed_back(): pl.pallas_call(functools.partial(feed_back_kernel, layer), grid=(rows //...  61.1 us
    pallas_call x2, Pallas kernels, feed(): pl.pallas_call(functools.partial(feed_kernel, layer), grid=(rows // tb,),...  49.4 us
    pallas_call x2, Pallas kernels, attend(): pl.pallas_call(functools.partial(attend_kernel, qb), grid=(heads // 2,),...  41.4 us
    pallas_call x2, Pallas kernels, feed_grads(): pl.pallas_call(feed_grads_kernel, grid_spec=pltpu.PrefetchScalarGridSpec(...  40 us
    convert_element_type x10, other arithmetic, add(): (kept[middle:].astype(F32) + arrived[middle:].astype(F32)).astype(BF16)  31.9 us
    pallas_call x2, Pallas kernels, qkv(): pl.pallas_call(functools.partial(qkv_kernel, layer, blocks), grid_spec=pl...  25.8 us
  transfers between devices with their start and end apart: 25, of which 4 were waited for; matrix products, arithmetic and copies ran while one was open for 6% of the time, Pallas kernels for 37%

profile of v4, /device:TPU:0, one launch (start us, length us, event | category | flops | bytes accessed | tf_op | source)
XLA Modules:
  0.0 492.7 jit_solution(9293000432071222108)
XLA Ops:
  0.6 0.5 collective-permute-start.2
  1.7 2.1 dynamic-slice_bitcast_fusion.6
  3.7 2.6 collective-permute-start
  6.3 0.6 broadcast_in_dim_tile.3.rate_ref
  6.9 4.2 row_tables.1
  11.3 0.6 broadcast_select_fusion.4.order_ref
  11.9 9.0 %collective-permute-done.1 = f32[1,12288]{1,0:T(1,128)} collective-permute-done((f32[1,12288]{1,0:T(1,128)}, f32[1,12288]{1,0:T(1,128)}, u32[]{:S(2)}, u32[]{:S(2)}) %collective-permute-start.1) | collective-permute-done | bytes 49184 | tf_op jit(solution)/shard_map/ppermute | solution.py:1464
  21.3 1.7 broadcast_select_fusion.3.pack_ref
  23.0 1.8 collective-permute-done.y_ref
  24.8 1.8 copy-done
  26.6 12.9 %joint_projection.2 = (bf16[1024,768]{1,0:T(8,128)(2,1)}, bf16[1024,768]{1,0:T(8,128)(2,1)}, bf16[12,1024,128]{2,1,0:T(8,128)(2,1)}, bf16[12,1024,128]{2,1,0:T(8,128)(2,1)}, bf16[12,1024,128]{2,1,0:T(8,128)(2,1)}) custom-call(s32[1]{0:T(128)} %bitcast.sec_ref, s32[1]{0:T(128)} %bitcast.1.mine_ref, bf16[4,512,768]{2,1,0:T(8,128)(2,1)} %bitcast.95, ...), custom_call_target="tpu_custom_call" | custom-call | flops 3623878656 | bytes 16777216 | tf_op jit(solution)/shard_map/joint_projection/pallas_call | solution.py:557
  39.5 1.5 dynamic-slice_bitcast_fusion.5
  41.0 1.8 collective-permute-start.6
  42.8 20.6 %attention_forward.2 = (f32[1024,768]{1,0:T(8,128)}, bf16[12,1024,128]{2,1,0:T(8,128)(2,1)}) custom-call(bf16[12,1024,128]{2,1,0:T(8,128)(2,1)} %get-tuple-element.131.q_ref, bf16[12,1024,128]{2,1,0:T(8,128)(2,1)} %get-tuple-element.132.k_ref.refs_1_, bf16[12,1024,128]{2,1,0:T(8,128)(2,1)} %get-tuple-element.133.v_ref.refs_2_), custom_call_target="tpu_custom_call" | custom-call | flops 12884901888 | bytes 16777216 | tf_op jit(solution)/shard_map/attention_forward/pallas_call | solution.py:610
  63.4 1.3 pad_maximum_fusion.2.c_ref
  64.7 24.6 %feed_forward.2 = (bf16[1024,768]{1,0:T(8,128)(2,1)}, f32[1024,768]{1,0:T(8,128)}, bf16[1024,3072]{1,0:T(8,128)(2,1)}, bf16[1024,3072]{1,0:T(8,128)(2,1)}, f32[1024,128]{1,0:T(8,128)}) custom-call(s32[1]{0:T(128)} %bitcast.sec_ref, f32[1024,768]{1,0:T(8,128)} %get-tuple-element.134.at_ref.refs_4_, bf16[1024,768]{1,0:T(8,128)(2,1)} %get-tuple-element.136.x_ref, ...), custom_call_target="tpu_custom_call" | custom-call | flops 10871635968 | bytes 41943040 | tf_op jit(solution)/shard_map/feed_forward/pallas_call | solution.py:677
  89.3 12.9 %joint_projection.3 = (bf16[1024,768]{1,0:T(8,128)(2,1)}, bf16[1024,768]{1,0:T(8,128)(2,1)}, bf16[12,1024,128]{2,1,0:T(8,128)(2,1)}, bf16[12,1024,128]{2,1,0:T(8,128)(2,1)}, bf16[12,1024,128]{2,1,0:T(8,128)(2,1)}) custom-call(s32[1]{0:T(128)} %bitcast.sec_ref, s32[1]{0:T(128)} %constant.124.clone.1.mine_ref, bf16[1,1024,768]{2,1,0:T(8,128)(2,1)} %bitcast.86, ...), custom_call_target="tpu_custom_call" | custom-call | flops 3623878656 | bytes 16777216 | tf_op jit(solution)/shard_map/joint_projection/pallas_call | solution.py:557
  102.3 20.8 %attention_forward.3 = (f32[1024,768]{1,0:T(8,128)}, bf16[12,1024,128]{2,1,0:T(8,128)(2,1)}) custom-call(bf16[12,1024,128]{2,1,0:T(8,128)(2,1)} %get-tuple-element.138.q_ref, bf16[12,1024,128]{2,1,0:T(8,128)(2,1)} %get-tuple-element.139.k_ref.refs_1_, bf16[12,1024,128]{2,1,0:T(8,128)(2,1)} %get-tuple-element.140.v_ref.refs_2_), custom_call_target="tpu_custom_call" | custom-call | flops 12884901888 | bytes 16777216 | tf_op jit(solution)/shard_map/attention_forward/pallas_call | solution.py:610
  123.1 24.8 %feed_forward.3 = (bf16[1024,768]{1,0:T(8,128)(2,1)}, f32[1024,768]{1,0:T(8,128)}, bf16[1024,3072]{1,0:T(8,128)(2,1)}, bf16[1024,3072]{1,0:T(8,128)(2,1)}, f32[1024,128]{1,0:T(8,128)}) custom-call(s32[1]{0:T(128)} %bitcast.sec_ref, f32[1024,768]{1,0:T(8,128)} %get-tuple-element.141.at_ref.refs_4_, bf16[1024,768]{1,0:T(8,128)(2,1)} %get-tuple-element.137.y_ref.x_ref, ...), custom_call_target="tpu_custom_call" | custom-call | flops 10871635968 | bytes 41943040 | tf_op jit(solution)/shard_map/feed_forward/pallas_call | solution.py:677
  147.9 2.8 select_bitcast_fusion.1
  150.7 30.4 %feed_backward.2 = (bf16[1024,3072]{1,0:T(8,128)(2,1)}, f32[1024,768]{1,0:T(8,128)}, bf16[768,1024]{1,0:T(8,128)(2,1)}, bf16[768,1024]{1,0:T(8,128)(2,1)}, bf16[...) custom-call(s32[1]{0:T(128)} %bitcast.sec_ref, ...), custom_call_target="tpu_custom_call" | custom-call | flops 10871635968 | bytes 52428800 | tf_op jit(solution)/shard_map/feed_backward/pallas_call | solution.py:773
  181.1 20.0 %feed_gradients.2 = (bf16[16,448,384]{2,1,0:T(8,128)(2,1)}, bf16[16,448,384]{2,1,0:T(8,128)(2,1)}) custom-call(s32[1]{0:T(128)} %bitcast.sec_ref, s32[32]{0:T(128)} %broadcast_select_fusion.4.order_ref, bf16[1024,3072]{1,0:T(8,128)(2,1)} %get-tuple-element.151.cb_ref, bf16[1024,3072]{1,0:T(8,128)(2,1)} %get-tuple-element.146.hid_ref, ...), custom_call_target="tpu_custom_call" | custom-call | flops 10871635968 | bytes 31457280 | tf_op jit(solution)/shard_map/feed_gradients/pallas_call | solution.py:987
  201.6 1.7 collective-permute-start.9
  203.3 35.5 %attention_backward.3.cj_ref = bf16[3,1024,768]{2,1,0:T(8,128)(2,1)} custom-call(bf16[12,1024,128]{2,1,0:T(8,128)(2,1)} %get-tuple-element.143.refs_0_, bf16[12,1024,128]{2,1,0:T(8,128)(2,1)} %get-tuple-element.139.k_ref.refs_1_, bf16[12,1024,128]{2,1,0:T(8,128)(2,1)} %get-tuple-element.140.v_ref.refs_2_, bf16[1024,768]{1,0:T(8,128)(2,1)} %get-tuple-element.160.refs_3_, ...), custom_call_target="tpu_custom_call" | custom-call | flops 32212254720 | bytes 18874368 | tf_op jit(solution)/shard_map/attention_backward/pallas_call | solution.py:853
  238.9 0.8 copy-done.7
  240.0 0.9 copy-done.9
  241.0 6.0 %add_convert_fusion.2 = (bf16[8,448,384]{2,1,0:T(8,128)(2,1)}, bf16[8,448,384]{2,1,0:T(8,128)(2,1)S(1)}) fusion(bf16[16,448,384]{2,1,0:T(8,128)(2,1)} %collective-permute-done.10, bf16[16,448,384]{2,1,0:T(8,128)(2,1)} %get-tuple-element.169), kind=kLoop, calls=%fused_computation.2 | loop fusion | flops 11010048 | bytes 16515072 | tf_op jit(solution)/shard_map/convert_element_type | solution.py:1150
  247.0 1.5 collective-permute-start.14
  248.5 11.1 %joint_backward.1 = (bf16[1024,768]{1,0:T(8,128)(2,1)}, f32[4,768]{1,0:T(4,128)}) custom-call(s32[1]{0:T(128)} %bitcast.sec_ref, bf16[3,1024,768]{2,1,0:T(8,128)(2,1)} %attention_backward.3.cj_ref, bf16[1024,768]{1,0:T(8,128)(2,1)} %get-tuple-element.137.y_ref.x_ref, f32[1024,768]{1,0:T(8,128)} %get-tuple-element.172.cm_ref, ...), custom_call_target="tpu_custom_call" | custom-call | flops 3623878656 | bytes 16777216 | tf_op jit(solution)/shard_map/joint_backward/pallas_call | solution.py:900
  259.6 9.2 %joint_gradients.1 = (bf16[16,160,384]{2,1,0:T(8,128)(2,1)}, bf16[16,160,384]{2,1,0:T(8,128)(2,1)}) custom-call(s32[1]{0:T(128)} %bitcast.sec_ref, s32[32]{0:T(128)} %broadcast_select_fusion.4.order_ref, bf16[3,1024,768]{2,1,0:T(8,128)(2,1)} %attention_backward.3.cj_ref, bf16[1024,768]{1,0:T(8,128)(2,1)} %get-tuple-element.174.n_ref, ...), custom_call_target="tpu_custom_call" | custom-call | flops 3623878656 | bytes 14680064 | tf_op jit(solution)/shard_map/joint_gradients/pallas_call | solution.py:1045
  268.8 2.6 fusion.9
  271.4 1.5 collective-permute-start.11
  272.9 5.0 %collective-permute-start.13 = (bf16[512,768]{1,0:T(8,128)(2,1)}, bf16[512,768]{1,0:T(8,128)(2,1)}, u32[]{:S(2)}, u32[]{:S(2)}) collective-permute-start(bf16[512,768]{1,0:T(8,128)(2,1)} %get-tuple-element.285), channel_id=1, source_target_pairs={{0,17},{1,16},{2,19},{3,18},{4,21},{5,20},{6,23},{7,22},{8,25},{9,... | collective-permute-start | bytes 2359304 | tf_op jit(solution)/shard_map/ppermute | solution.py:1514
  278.0 2.2 collective-permute-start.12
  280.2 30.7 %feed_backward.3 = (bf16[1024,3072]{1,0:T(8,128)(2,1)}, f32[1024,768]{1,0:T(8,128)}, bf16[768,1024]{1,0:T(8,128)(2,1)}, bf16[768,1024]{1,0:T(8,128)(2,1)}, bf16[...) custom-call(s32[1]{0:T(128)} %bitcast.sec_ref, ...), custom_call_target="tpu_custom_call" | custom-call | flops 10871635968 | bytes 52428800 | tf_op jit(solution)/shard_map/feed_backward/pallas_call | solution.py:773
  310.9 3.9 add_convert_fusion.8
  314.8 3.5 add_convert_fusion.6
  318.3 0.5 collective-permute-start.16
  318.8 1.0 collective-permute-start.17
  319.8 20.1 %feed_gradients.3 = (bf16[16,448,384]{2,1,0:T(8,128)(2,1)}, bf16[16,448,384]{2,1,0:T(8,128)(2,1)}) custom-call(s32[1]{0:T(128)} %bitcast.sec_ref, s32[32]{0:T(128)} %broadcast_select_fusion.4.order_ref, bf16[1024,3072]{1,0:T(8,128)(2,1)} %get-tuple-element.190.cb_ref, bf16[1024,3072]{1,0:T(8,128)(2,1)} %get-tuple-element.179.hid_ref, ...), custom_call_target="tpu_custom_call" | custom-call | flops 10871635968 | bytes 31457280 | tf_op jit(solution)/shard_map/feed_gradients/pallas_call | solution.py:987
  339.8 3.2 collective-permute-done.17
  343.0 2.4 add_convert_fusion.12
  345.4 1.4 add_convert_fusion.10
  346.8 2.0 pad_maximum_fusion
  348.9 1.6 collective-permute-start.19
  350.5 1.5 collective-permute-start.20
  352.0 19.4 %attention_backward.4.refs_7_ = bf16[3,1024,768]{2,1,0:T(8,128)(2,1)} custom-call(bf16[12,1024,128]{2,1,0:T(8,128)(2,1)} %get-tuple-element.167.refs_0_, bf16[12,1024,128]{2,1,0:T(8,128)(2,1)} %get-tuple-element.132.k_ref.refs_1_, bf16[12,1024,128]{2,1,0:T(8,128)(2,1)} %get-tuple-element.133.v_ref.refs_2_, bf16[1024,768]{1,0:T(8,128)(2,1)} %get-tuple-element.203.refs_3_, ...), custom_call_target="tpu_custom_call" | custom-call | flops 16106127360 | bytes 9437184 | tf_op jit(solution)/shard_map/attention_backward/pallas_call | solution.py:853
  371.5 2.1 add_convert_fusion.16
  373.6 2.1 add_convert_fusion.14
  375.7 6.4 %add_convert_fusion = (bf16[8,448,384]{2,1,0:T(8,128)(2,1)}, bf16[8,448,384]{2,1,0:T(8,128)(2,1)}) fusion(bf16[16,448,384]{2,1,0:T(8,128)(2,1)} %collective-permute-done.18, bf16[16,448,384]{2,1,0:T(8,128)(2,1)} %get-tuple-element.204), kind=kLoop, calls=%fused_computation | loop fusion | flops 11010048 | bytes 16515072 | tf_op jit(solution)/shard_map/convert_element_type | solution.py:1150
  382.1 0.5 collective-permute-start.22
  382.8 1.9 maximum_bitcast_fusion
  384.7 2.6 collective-permute-start.21
  387.3 0.4 collective-permute-start.23
  387.7 19.2 %attention_backward.5.cj_ref = bf16[3,1024,768]{2,1,0:T(8,128)(2,1)} custom-call(bf16[12,1024,128]{2,1,0:T(8,128)(2,1)} %get-tuple-element.167.refs_0_, bf16[12,1024,128]{2,1,0:T(8,128)(2,1)} %get-tuple-element.132.k_ref.refs_1_, bf16[12,1024,128]{2,1,0:T(8,128)(2,1)} %get-tuple-element.133.v_ref.refs_2_, ...), custom_call_target="tpu_custom_call", output_to_operand_aliasing={{}: (7, {})} | custom-call | flops 16106127360 | bytes 9437184 | tf_op jit(solution)/shard_map/attention_backward/pallas_call | solution.py:853
  407.5 7.4 %collective-permute-done.24 = bf16[1,160,384]{2,1,0:T(8,128)(2,1)S(1)} collective-permute-done((bf16[1,160,384]{2,1,0:T(8,128)(2,1)S(1)}, bf16[1,160,384]{2,1,0:T(8,128)(2,1)S(1)}, u32[]{:S(2)}, u32[]{:S(2)}) %collective-permute-start.24) | collective-permute-done | bytes 122912 | tf_op jit(solution)/shard_map/ppermute | solution.py:1141
  414.9 1.0 pad_maximum_fusion.3.done_ref
  416.0 4.0 add_convert_fusion.4
  420.0 62.8 %last_step.1 = (f32[2,608,384]{2,1,0:T(8,128)}, bf16[512,768]{1,0:T(8,128)(2,1)}, bf16[3,512,768]{2,1,0:T(8,128)(2,1)}) custom-call(bf16[3,1024,768]{2,1,0:T(8,128)(2,1)} %attention_backward.5.cj_ref, bf16[1024,768]{1,0:T(8,128)(2,1)} %get-tuple-element.214.n_ref, bf16[1024,768]{1,0:T(8,128)(2,1)} %get-tuple-element.136.x_ref, ...), custom_call_target="tpu_custom_call" | custom-call | bytes 104857600 | tf_op jit(solution)/shard_map/last_step/pallas_call | solution.py:1353
  482.8 1.4 select_bitcast_fusion
  484.2 0.5 copy-done.5
  485.0 0.4 pad_maximum_fusion.1
  485.7 3.8 gradient_outputs.1
  489.5 3.0 maximum_convert_fusion
  (56 shorter events, 3.3 us)
Async XLA Ops:
  0.6 24.1 %collective-permute-start.2 = (bf16[768,2304]{1,0:T(8,128)(2,1)}, bf16[768,2304]{1,0:T(8,128)(2,1)S(1)}, u32[]{:S(2)}, u32[]{:S(2)}) collective-permute-start(bf16[768,2304]{1,0:T(8,128)(2,1)} %bitcast.81), channel_id=1, source_target_pairs={{0,16},{16,0},{1,17},{17,1},{2,18},{18,2},{3,19},{19,3},{4,20},{20... | collective-permute-start | bytes 10616840 | tf_op jit(solution)/shard_map/ppermute | solution.py:1460
  1.2 63.5 %collective-permute-start.4 = (bf16[768,3072]{1,0:T(8,128)(2,1)}, bf16[768,3072]{1,0:T(8,128)(2,1)}, u32[]{:S(2)}, u32[]{:S(2)}) collective-permute-start(bf16[768,3072]{1,0:T(8,128)(2,1)} %bitcast.71), channel_id=1, source_target_pairs={{0,16},{16,0},{1,17},{17,1},{2,18},{18,2},{3,19},{19,3},{4,20},{20... | collective-permute-start | bytes 14155784 | tf_op jit(solution)/shard_map/ppermute | solution.py:1460
  1.2 63.4 %collective-permute-start.5 = (bf16[3072,768]{1,0:T(8,128)(2,1)}, bf16[3072,768]{1,0:T(8,128)(2,1)}, u32[]{:S(2)}, u32[]{:S(2)}) collective-permute-start(bf16[3072,768]{1,0:T(8,128)(2,1)} %bitcast.76), channel_id=1, source_target_pairs={{0,16},{16,0},{1,17},{17,1},{2,18},{18,2},{3,19},{19,3},{4,20},{20... | collective-permute-start | bytes 14155784 | tf_op jit(solution)/shard_map/ppermute | solution.py:1460
  3.7 21.0 %collective-permute-start = (bf16[512,768]{1,0:T(8,128)(2,1)}, bf16[512,768]{1,0:T(8,128)(2,1)}, u32[]{:S(2)}, u32[]{:S(2)}) collective-permute-start(bf16[512,768]{1,0:T(8,128)(2,1)} %dynamic-slice_bitcast_fusion.6), channel_id=1, source_target_pairs={{0,1},{1,0},{2,3},{3,2},{4,5},{5,4},{6,7},{7,6},{8,9},{9,8},{10,11... | collective-permute-start | bytes 2359304 | tf_op jit(solution)/shard_map/ppermute | solution.py:1459
  11.2 9.8 %collective-permute-start.1 = (f32[1,12288]{1,0:T(1,128)}, f32[1,12288]{1,0:T(1,128)}, u32[]{:S(2)}, u32[]{:S(2)}) collective-permute-start(f32[1,12288]{1,0:T(1,128)} %get-tuple-element.127), channel_id=1, source_target_pairs={{0,16},{16,0},{1,17},{17,1},{2,18},{18,2},{3,19},{19,3},{4,20},{20... | collective-permute-start | bytes 147464 | tf_op jit(solution)/shard_map/ppermute | solution.py:1464
  20.9 43.8 %collective-permute-start.3 = (bf16[768,768]{1,0:T(8,128)(2,1)}, bf16[768,768]{1,0:T(8,128)(2,1)}, u32[]{:S(2)}, u32[]{:S(2)}) collective-permute-start(bf16[768,768]{1,0:T(8,128)(2,1)} %bitcast.87), channel_id=1, source_target_pairs={{0,16},{16,0},{1,17},{17,1},{2,18},{18,2},{3,19},{19,3},{4,20},{20... | collective-permute-start | bytes 3538952 | tf_op jit(solution)/shard_map/ppermute | solution.py:1460
  24.8 1.8 copy-start
  41.0 22.4 %collective-permute-start.6 = (bf16[512,768]{1,0:T(8,128)(2,1)S(1)}, bf16[512,768]{1,0:T(8,128)(2,1)S(1)}, u32[]{:S(2)}, u32[]{:S(2)}) collective-permute-start(bf16[512,768]{1,0:T(8,128)(2,1)S(1)} %get-tuple-element.277), channel_id=1, source_target_pairs={{0,1},{1,0},{2,3},{3,2},{4,5},{5,4},{6,7},{7,6},{8,9},{9,8},{10,11... | collective-permute-start | bytes 2359304 | tf_op jit(solution)/shard_map/ppermute | solution.py:1481
  123.1 24.8 %copy-start.2 = (bf16[1024,768]{1,0:T(8,128)(2,1)S(1)}, bf16[1024,768]{1,0:T(8,128)(2,1)}, u32[]{:S(2)}) copy-start(bf16[1024,768]{1,0:T(8,128)(2,1)} %get-tuple-element.137.y_ref.x_ref) | copy-start | bytes 4718596
  201.1 39.9 %collective-permute-start.10 = (bf16[16,448,384]{2,1,0:T(8,128)(2,1)}, bf16[16,448,384]{2,1,0:T(8,128)(2,1)}, u32[]{:S(2)}, u32[]{:S(2)}) collective-permute-start(bf16[16,448,384]{2,1,0:T(8,128)(2,1)} %get-tuple-element.170), channel_id=1, source_target_pairs={{0,16},{16,0},{1,17},{17,1},{2,18},{18,2},{3,19},{19,3},{4,20},{20... | collective-permute-start | bytes 16515080 | tf_op jit(solution)/shard_map/ppermute | solution.py:1133
  201.1 37.7 %collective-permute-start.7 = (bf16[512,768]{1,0:T(8,128)(2,1)}, bf16[512,768]{1,0:T(8,128)(2,1)S(1)}, u32[]{:S(2)}, u32[]{:S(2)}) collective-permute-start(bf16[512,768]{1,0:T(8,128)(2,1)} %get-tuple-element.161), channel_id=1, source_target_pairs={{0,1},{1,0},{16,17},{17,16},{2,3},{3,2},{18,19},{19,18},{4,5},{5,4... | collective-permute-start | bytes 2359304 | tf_op jit(solution)/shard_map/ppermute | solution.py:1500
  201.5 37.4 %collective-permute-start.8 = (bf16[512,768]{1,0:T(8,128)(2,1)S(1)}, bf16[512,768]{1,0:T(8,128)(2,1)S(1)}, u32[]{:S(2)}, u32[]{:S(2)}) collective-permute-start(bf16[512,768]{1,0:T(8,128)(2,1)S(1)} %get-tuple-element.162), channel_id=1, source_target_pairs={{0,16},{1,17},{16,0},{17,1},{2,18},{3,19},{18,2},{19,3},{4,20},{5,... | collective-permute-start | bytes 2359304 | tf_op jit(solution)/shard_map/ppermute | solution.py:1500
  201.6 37.2 %collective-permute-start.9 = (bf16[512,768]{1,0:T(8,128)(2,1)S(1)}, bf16[512,768]{1,0:T(8,128)(2,1)S(1)}, u32[]{:S(2)}, u32[]{:S(2)}) collective-permute-start(bf16[512,768]{1,0:T(8,128)(2,1)S(1)} %get-tuple-element.163), channel_id=1, source_target_pairs={{0,17},{1,16},{16,1},{17,0},{2,19},{3,18},{18,3},{19,2},{4,21},{5,... | collective-permute-start | bytes 2359304 | tf_op jit(solution)/shard_map/ppermute | solution.py:1500
  238.8 0.9 copy-start.7
  238.8 1.2 copy-start.8
  240.0 0.9 copy-start.9
  247.0 67.8 %collective-permute-start.14 = (bf16[8,448,384]{2,1,0:T(8,128)(2,1)}, bf16[8,448,384]{2,1,0:T(8,128)(2,1)}, u32[]{:S(2)}, u32[]{:S(2)}) collective-permute-start(bf16[8,448,384]{2,1,0:T(8,128)(2,1)} %get-tuple-element.187), channel_id=1, source_target_pairs={{0,2},{1,3},{2,0},{3,1},{4,6},{5,7},{6,4},{7,5},{8,10},{9,11},{10,... | collective-permute-start | bytes 8257544 | tf_op jit(solution)/shard_map/ppermute | solution.py:1141
  268.8 42.1 %collective-permute-start.15 = (bf16[16,160,384]{2,1,0:T(8,128)(2,1)}, bf16[16,160,384]{2,1,0:T(8,128)(2,1)}, u32[]{:S(2)}, u32[]{:S(2)}) collective-permute-start(bf16[16,160,384]{2,1,0:T(8,128)(2,1)} %get-tuple-element.189), channel_id=1, source_target_pairs={{0,16},{16,0},{1,17},{17,1},{2,18},{18,2},{3,19},{19,3},{4,20},{20... | collective-permute-start | bytes 5898248 | tf_op jit(solution)/shard_map/ppermute | solution.py:1133
  271.4 47.4 %collective-permute-start.11 = (bf16[512,768]{1,0:T(8,128)(2,1)}, bf16[512,768]{1,0:T(8,128)(2,1)}, u32[]{:S(2)}, u32[]{:S(2)}) collective-permute-start(bf16[512,768]{1,0:T(8,128)(2,1)} %get-tuple-element.285), channel_id=1, source_target_pairs={{16,17},{17,16},{18,19},{19,18},{20,21},{21,20},{22,23},{23,22},{2... | collective-permute-start | bytes 2359304 | tf_op jit(solution)/shard_map/ppermute | solution.py:1514
  272.9 45.8 %collective-permute-start.13 = (bf16[512,768]{1,0:T(8,128)(2,1)}, bf16[512,768]{1,0:T(8,128)(2,1)}, u32[]{:S(2)}, u32[]{:S(2)}) collective-permute-start(bf16[512,768]{1,0:T(8,128)(2,1)} %get-tuple-element.285), channel_id=1, source_target_pairs={{0,17},{1,16},{2,19},{3,18},{4,21},{5,20},{6,23},{7,22},{8,25},{9,... | collective-permute-start | bytes 2359304 | tf_op jit(solution)/shard_map/ppermute | solution.py:1514
  278.0 40.8 %collective-permute-start.12 = (bf16[512,768]{1,0:T(8,128)(2,1)}, bf16[512,768]{1,0:T(8,128)(2,1)}, u32[]{:S(2)}, u32[]{:S(2)}) collective-permute-start(bf16[512,768]{1,0:T(8,128)(2,1)} %get-tuple-element.222), channel_id=1, source_target_pairs={{0,16},{1,17},{2,18},{3,19},{4,20},{5,21},{6,22},{7,23},{8,24},{9,... | collective-permute-start | bytes 2359304 | tf_op jit(solution)/shard_map/ppermute | solution.py:1514
  318.3 27.1 %collective-permute-start.16 = (bf16[4,448,384]{2,1,0:T(8,128)(2,1)}, bf16[4,448,384]{2,1,0:T(8,128)(2,1)S(1)}, u32[]{:S(2)}, u32[]{:S(2)}) collective-permute-start(bf16[4,448,384]{2,1,0:T(8,128)(2,1)} %get-tuple-element.200), channel_id=1, source_target_pairs={{0,1},{1,0},{2,3},{3,2},{4,5},{5,4},{6,7},{7,6},{8,9},{9,8},{10,11... | collective-permute-start | bytes 4128776 | tf_op jit(solution)/shard_map/ppermute | solution.py:1141
  318.8 24.2 %collective-permute-start.17 = (bf16[8,160,384]{2,1,0:T(8,128)(2,1)}, bf16[8,160,384]{2,1,0:T(8,128)(2,1)}, u32[]{:S(2)}, u32[]{:S(2)}) collective-permute-start(bf16[8,160,384]{2,1,0:T(8,128)(2,1)} %get-tuple-element.202), channel_id=1, source_target_pairs={{0,2},{1,3},{2,0},{3,1},{4,6},{5,7},{6,4},{7,5},{8,10},{9,11},{10,... | collective-permute-start | bytes 2949128 | tf_op jit(solution)/shard_map/ppermute | solution.py:1141
  319.8 23.3 %copy-start.3 = (bf16[8,160,384]{2,1,0:T(8,128)(2,1)S(1)}, bf16[8,160,384]{2,1,0:T(8,128)(2,1)}, u32[]{:S(2)}) copy-start(bf16[8,160,384]{2,1,0:T(8,128)(2,1)} %get-tuple-element.201) | copy-start | bytes 2949124
  346.8 28.9 %collective-permute-start.18 = (bf16[16,448,384]{2,1,0:T(8,128)(2,1)}, bf16[16,448,384]{2,1,0:T(8,128)(2,1)}, u32[]{:S(2)}, u32[]{:S(2)}) collective-permute-start(bf16[16,448,384]{2,1,0:T(8,128)(2,1)} %get-tuple-element.205), channel_id=1, source_target_pairs={{0,16},{16,0},{1,17},{17,1},{2,18},{18,2},{3,19},{19,3},{4,20},{20... | collective-permute-start | bytes 16515080 | tf_op jit(solution)/shard_map/ppermute | solution.py:1133
  348.9 24.7 %collective-permute-start.19 = (bf16[2,448,384]{2,1,0:T(8,128)(2,1)}, bf16[2,448,384]{2,1,0:T(8,128)(2,1)}, u32[]{:S(2)}, u32[]{:S(2)}) collective-permute-start(bf16[2,448,384]{2,1,0:T(8,128)(2,1)} %get-tuple-element.207), channel_id=1, source_target_pairs={{0,4},{1,5},{2,6},{3,7},{4,0},{5,1},{6,2},{7,3},{8,12},{9,13},{10,... | collective-permute-start | bytes 2064392 | tf_op jit(solution)/shard_map/ppermute | solution.py:1141
  350.5 20.9 %collective-permute-start.20 = (bf16[4,160,384]{2,1,0:T(8,128)(2,1)}, bf16[4,160,384]{2,1,0:T(8,128)(2,1)}, u32[]{:S(2)}, u32[]{:S(2)}) collective-permute-start(bf16[4,160,384]{2,1,0:T(8,128)(2,1)} %get-tuple-element.209), channel_id=1, source_target_pairs={{0,1},{1,0},{2,3},{3,2},{4,5},{5,4},{6,7},{7,6},{8,9},{9,8},{10,11... | collective-permute-start | bytes 1474568 | tf_op jit(solution)/shard_map/ppermute | solution.py:1141
  352.0 21.5 %copy-start.4 = (bf16[2,448,384]{2,1,0:T(8,128)(2,1)S(1)}, bf16[2,448,384]{2,1,0:T(8,128)(2,1)}, u32[]{:S(2)}) copy-start(bf16[2,448,384]{2,1,0:T(8,128)(2,1)} %get-tuple-element.206) | copy-start | bytes 2064388
  382.1 33.9 %collective-permute-start.22 = (bf16[8,448,384]{2,1,0:T(8,128)(2,1)}, bf16[8,448,384]{2,1,0:T(8,128)(2,1)}, u32[]{:S(2)}, u32[]{:S(2)}) collective-permute-start(bf16[8,448,384]{2,1,0:T(8,128)(2,1)} %get-tuple-element.217), channel_id=1, source_target_pairs={{0,2},{1,3},{2,0},{3,1},{4,6},{5,7},{6,4},{7,5},{8,10},{9,11},{10,... | collective-permute-start | bytes 8257544 | tf_op jit(solution)/shard_map/ppermute | solution.py:1141
  384.7 22.7 %copy-start.6 = (bf16[1,448,384]{2,1,0:T(8,128)(2,1)S(1)}, bf16[1,448,384]{2,1,0:T(8,128)(2,1)}, u32[]{:S(2)}) copy-start(bf16[1,448,384]{2,1,0:T(8,128)(2,1)} %get-tuple-element.211) | copy-start | bytes 1032196
  384.7 22.7 %collective-permute-start.21 = (bf16[1,448,384]{2,1,0:T(8,128)(2,1)}, bf16[1,448,384]{2,1,0:T(8,128)(2,1)S(1)}, u32[]{:S(2)}, u32[]{:S(2)}) collective-permute-start(bf16[1,448,384]{2,1,0:T(8,128)(2,1)} %get-tuple-element.212), channel_id=1, source_target_pairs={{0,8},{1,9},{2,10},{3,11},{4,12},{5,13},{6,14},{7,15},{8,0},{9,1},... | collective-permute-start | bytes 1032200 | tf_op jit(solution)/shard_map/ppermute | solution.py:1141
  387.3 19.6 %collective-permute-start.23 = (bf16[2,160,384]{2,1,0:T(8,128)(2,1)}, bf16[2,160,384]{2,1,0:T(8,128)(2,1)S(1)}, u32[]{:S(2)}, u32[]{:S(2)}) collective-permute-start(bf16[2,160,384]{2,1,0:T(8,128)(2,1)} %get-tuple-element.220), channel_id=1, source_target_pairs={{0,4},{1,5},{2,6},{3,7},{4,0},{5,1},{6,2},{7,3},{8,12},{9,13},{10,... | collective-permute-start | bytes 737288 | tf_op jit(solution)/shard_map/ppermute | solution.py:1141
  406.9 9.1 %copy-start.1 = (bf16[8,448,384]{2,1,0:T(8,128)(2,1)S(1)}, bf16[8,448,384]{2,1,0:T(8,128)(2,1)}, u32[]{:S(2)}) copy-start(bf16[8,448,384]{2,1,0:T(8,128)(2,1)} %get-tuple-element.216) | copy-start | bytes 8257540
  407.0 7.9 %collective-permute-start.24 = (bf16[1,160,384]{2,1,0:T(8,128)(2,1)S(1)}, bf16[1,160,384]{2,1,0:T(8,128)(2,1)S(1)}, u32[]{:S(2)}, u32[]{:S(2)}) collective-permute-start(bf16[1,160,384]{2,1,0:T(8,128)(2,1)S(1)} %add_convert_fusion.18), channel_id=1, source_target_pairs={{0,8},{1,9},{2,10},{3,11},{4,12},{5,13},{6,14},{7,15},{8,0},{9,1},... | collective-permute-start | bytes 368648 | tf_op jit(solution)/shard_map/ppermute | solution.py:1141
  482.8 1.9 copy-start.5

commit v5 on v4

--- a/solution.py
+++ b/solution.py
@@ -1531,7 +1531,7 @@
         else:
             ch, delivered[1] = lax.optimization_barrier((ch, delivered[1]))
             ch = advance(ch, flights[FEED, 0], flights[FEED, 1], flights[JOINT, 1])
-            count = query.shape[0] // 4
+            count = 2
             cj = attend_back(query, k, v, ch, attended, cosine, sine, 0, count)
             cj = advance(cj, flights[FEED, 0], flights[FEED, 1], flights[JOINT, 1])
             cj = attend_back(query, k, v, ch, attended, cosine, sine, count, None, cj)

time: 501 us -> 500 us (level)
  transfers between devices with their start and end apart: 25 -> 25, of which waited for: 4 -> 5; matrix products, arithmetic and copies ran while one was open for 6% -> 5% of each run, Pallas kernels for 37% -> 37%
where the time goes in v5:
time: 500 us; the launch traced here: 491 us
  Pallas kernels  382 us (76%)
  other arithmetic  46.4 us (9%)
  starting transfers between devices  28.6 us (6%)
  waiting for transfers between devices  21.9 us (4%)
  local copies, waits for them, and re-layouts  11.6 us (2%)
    pallas_call x3, Pallas kernels, attend_back(): pl.pallas_call(kernel, grid=(count,), in_specs=[hd, hd, hd, col, col, con...  73.7 us
    pallas_call x1, Pallas kernels, last_step(): pl.pallas_call(last_kernel, in_specs=[vm] * 5 + [ANY] * 2 + [vm] * 3, out...  61.9 us
    pallas_call x2, Pallas kernels, feed_back(): pl.pallas_call(functools.partial(feed_back_kernel, layer), grid=(rows //...  61.1 us
    pallas_call x2, Pallas kernels, feed(): pl.pallas_call(functools.partial(feed_kernel, layer), grid=(rows // tb,),...  49.4 us
    pallas_call x2, Pallas kernels, attend(): pl.pallas_call(functools.partial(attend_kernel, qb), grid=(heads // 2,),...  41.4 us
    pallas_call x2, Pallas kernels, feed_grads(): pl.pallas_call(feed_grads_kernel, grid_spec=pltpu.PrefetchScalarGridSpec(...  40 us
    convert_element_type x10, other arithmetic, add(): (kept[middle:].astype(F32) + arrived[middle:].astype(F32)).astype(BF16)  28.8 us
    pallas_call x2, Pallas kernels, qkv(): pl.pallas_call(functools.partial(qkv_kernel, layer, blocks), grid_spec=pl...  25.8 us
  transfers between devices with their start and end apart: 25, of which 5 were waited for; matrix products, arithmetic and copies ran while one was open for 5% of the time, Pallas kernels for 37%

profile of v5, /device:TPU:0, one launch (start us, length us, event | category | flops | bytes accessed | tf_op | source)
XLA Modules:
  0.0 491.3 jit_solution(10155125625798072423)
XLA Ops:
  0.6 0.5 collective-permute-start.2
  1.7 2.1 dynamic-slice_bitcast_fusion.6
  3.7 2.6 collective-permute-start
  6.3 0.6 broadcast_in_dim_tile.3.rate_ref
  6.9 4.2 row_tables.1
  11.3 0.6 broadcast_select_fusion.4.order_ref
  11.9 9.0 %collective-permute-done.1 = f32[1,12288]{1,0:T(1,128)} collective-permute-done((f32[1,12288]{1,0:T(1,128)}, f32[1,12288]{1,0:T(1,128)}, u32[]{:S(2)}, u32[]{:S(2)}) %collective-permute-start.1) | collective-permute-done | bytes 49184 | tf_op jit(solution)/shard_map/ppermute | solution.py:1464
  21.3 1.7 broadcast_select_fusion.3.pack_ref
  23.0 1.8 collective-permute-done.y_ref
  24.8 1.8 copy-done
  26.6 12.9 %joint_projection.2 = (bf16[1024,768]{1,0:T(8,128)(2,1)}, bf16[1024,768]{1,0:T(8,128)(2,1)}, bf16[12,1024,128]{2,1,0:T(8,128)(2,1)}, bf16[12,1024,128]{2,1,0:T(8,128)(2,1)}, bf16[12,1024,128]{2,1,0:T(8,128)(2,1)}) custom-call(s32[1]{0:T(128)} %bitcast.sec_ref, s32[1]{0:T(128)} %bitcast.1.mine_ref, bf16[4,512,768]{2,1,0:T(8,128)(2,1)} %bitcast.95, ...), custom_call_target="tpu_custom_call" | custom-call | flops 3623878656 | bytes 16777216 | tf_op jit(solution)/shard_map/joint_projection/pallas_call | solution.py:557
  39.5 1.5 dynamic-slice_bitcast_fusion.5
  41.0 1.8 collective-permute-start.6
  42.8 20.6 %attention_forward.2 = (f32[1024,768]{1,0:T(8,128)}, bf16[12,1024,128]{2,1,0:T(8,128)(2,1)}) custom-call(bf16[12,1024,128]{2,1,0:T(8,128)(2,1)} %get-tuple-element.131.q_ref, bf16[12,1024,128]{2,1,0:T(8,128)(2,1)} %get-tuple-element.132.k_ref.refs_1_, bf16[12,1024,128]{2,1,0:T(8,128)(2,1)} %get-tuple-element.133.v_ref.refs_2_), custom_call_target="tpu_custom_call" | custom-call | flops 12884901888 | bytes 16777216 | tf_op jit(solution)/shard_map/attention_forward/pallas_call | solution.py:610
  63.4 1.3 pad_maximum_fusion.2.c_ref
  64.7 24.6 %feed_forward.2 = (bf16[1024,768]{1,0:T(8,128)(2,1)}, f32[1024,768]{1,0:T(8,128)}, bf16[1024,3072]{1,0:T(8,128)(2,1)}, bf16[1024,3072]{1,0:T(8,128)(2,1)}, f32[1024,128]{1,0:T(8,128)}) custom-call(s32[1]{0:T(128)} %bitcast.sec_ref, f32[1024,768]{1,0:T(8,128)} %get-tuple-element.134.at_ref.refs_4_, bf16[1024,768]{1,0:T(8,128)(2,1)} %get-tuple-element.136.x_ref, ...), custom_call_target="tpu_custom_call" | custom-call | flops 10871635968 | bytes 41943040 | tf_op jit(solution)/shard_map/feed_forward/pallas_call | solution.py:677
  89.3 12.9 %joint_projection.3 = (bf16[1024,768]{1,0:T(8,128)(2,1)}, bf16[1024,768]{1,0:T(8,128)(2,1)}, bf16[12,1024,128]{2,1,0:T(8,128)(2,1)}, bf16[12,1024,128]{2,1,0:T(8,128)(2,1)}, bf16[12,1024,128]{2,1,0:T(8,128)(2,1)}) custom-call(s32[1]{0:T(128)} %bitcast.sec_ref, s32[1]{0:T(128)} %constant.124.clone.1.mine_ref, bf16[1,1024,768]{2,1,0:T(8,128)(2,1)} %bitcast.86, ...), custom_call_target="tpu_custom_call" | custom-call | flops 3623878656 | bytes 16777216 | tf_op jit(solution)/shard_map/joint_projection/pallas_call | solution.py:557
  102.3 20.8 %attention_forward.3 = (f32[1024,768]{1,0:T(8,128)}, bf16[12,1024,128]{2,1,0:T(8,128)(2,1)}) custom-call(bf16[12,1024,128]{2,1,0:T(8,128)(2,1)} %get-tuple-element.138.q_ref, bf16[12,1024,128]{2,1,0:T(8,128)(2,1)} %get-tuple-element.139.k_ref.refs_1_, bf16[12,1024,128]{2,1,0:T(8,128)(2,1)} %get-tuple-element.140.v_ref.refs_2_), custom_call_target="tpu_custom_call" | custom-call | flops 12884901888 | bytes 16777216 | tf_op jit(solution)/shard_map/attention_forward/pallas_call | solution.py:610
  123.1 24.8 %feed_forward.3 = (bf16[1024,768]{1,0:T(8,128)(2,1)}, f32[1024,768]{1,0:T(8,128)}, bf16[1024,3072]{1,0:T(8,128)(2,1)}, bf16[1024,3072]{1,0:T(8,128)(2,1)}, f32[1024,128]{1,0:T(8,128)}) custom-call(s32[1]{0:T(128)} %bitcast.sec_ref, f32[1024,768]{1,0:T(8,128)} %get-tuple-element.141.at_ref.refs_4_, bf16[1024,768]{1,0:T(8,128)(2,1)} %get-tuple-element.137.y_ref.x_ref, ...), custom_call_target="tpu_custom_call" | custom-call | flops 10871635968 | bytes 41943040 | tf_op jit(solution)/shard_map/feed_forward/pallas_call | solution.py:677
  147.9 2.8 select_bitcast_fusion.1
  150.7 30.4 %feed_backward.2 = (bf16[1024,3072]{1,0:T(8,128)(2,1)}, f32[1024,768]{1,0:T(8,128)}, bf16[768,1024]{1,0:T(8,128)(2,1)}, bf16[768,1024]{1,0:T(8,128)(2,1)}, bf16[...) custom-call(s32[1]{0:T(128)} %bitcast.sec_ref, ...), custom_call_target="tpu_custom_call" | custom-call | flops 10871635968 | bytes 52428800 | tf_op jit(solution)/shard_map/feed_backward/pallas_call | solution.py:773
  181.1 20.0 %feed_gradients.2 = (bf16[16,448,384]{2,1,0:T(8,128)(2,1)}, bf16[16,448,384]{2,1,0:T(8,128)(2,1)}) custom-call(s32[1]{0:T(128)} %bitcast.sec_ref, s32[32]{0:T(128)} %broadcast_select_fusion.4.order_ref, bf16[1024,3072]{1,0:T(8,128)(2,1)} %get-tuple-element.151.cb_ref, bf16[1024,3072]{1,0:T(8,128)(2,1)} %get-tuple-element.146.hid_ref, ...), custom_call_target="tpu_custom_call" | custom-call | flops 10871635968 | bytes 31457280 | tf_op jit(solution)/shard_map/feed_gradients/pallas_call | solution.py:987
  201.6 1.7 collective-permute-start.9
  203.3 35.5 %attention_backward.3.cj_ref = bf16[3,1024,768]{2,1,0:T(8,128)(2,1)} custom-call(bf16[12,1024,128]{2,1,0:T(8,128)(2,1)} %get-tuple-element.143.refs_0_, bf16[12,1024,128]{2,1,0:T(8,128)(2,1)} %get-tuple-element.139.k_ref.refs_1_, bf16[12,1024,128]{2,1,0:T(8,128)(2,1)} %get-tuple-element.140.v_ref.refs_2_, bf16[1024,768]{1,0:T(8,128)(2,1)} %get-tuple-element.160.refs_3_, ...), custom_call_target="tpu_custom_call" | custom-call | flops 32212254720 | bytes 18874368 | tf_op jit(solution)/shard_map/attention_backward/pallas_call | solution.py:853
  238.9 0.8 copy-done.5
  240.0 0.9 copy-done.7
  241.0 6.0 %add_convert_fusion.2 = (bf16[8,448,384]{2,1,0:T(8,128)(2,1)}, bf16[8,448,384]{2,1,0:T(8,128)(2,1)S(1)}) fusion(bf16[16,448,384]{2,1,0:T(8,128)(2,1)} %collective-permute-done.10, bf16[16,448,384]{2,1,0:T(8,128)(2,1)} %get-tuple-element.169), kind=kLoop, calls=%fused_computation.2 | loop fusion | flops 11010048 | bytes 16515072 | tf_op jit(solution)/shard_map/convert_element_type | solution.py:1150
  247.0 1.5 collective-permute-start.14
  248.5 11.1 %joint_backward.1 = (bf16[1024,768]{1,0:T(8,128)(2,1)}, f32[4,768]{1,0:T(4,128)}) custom-call(s32[1]{0:T(128)} %bitcast.sec_ref, bf16[3,1024,768]{2,1,0:T(8,128)(2,1)} %attention_backward.3.cj_ref, bf16[1024,768]{1,0:T(8,128)(2,1)} %get-tuple-element.137.y_ref.x_ref, f32[1024,768]{1,0:T(8,128)} %get-tuple-element.172.cm_ref, ...), custom_call_target="tpu_custom_call" | custom-call | flops 3623878656 | bytes 16777216 | tf_op jit(solution)/shard_map/joint_backward/pallas_call | solution.py:900
  259.6 9.2 %joint_gradients.1 = (bf16[16,160,384]{2,1,0:T(8,128)(2,1)}, bf16[16,160,384]{2,1,0:T(8,128)(2,1)}) custom-call(s32[1]{0:T(128)} %bitcast.sec_ref, s32[32]{0:T(128)} %broadcast_select_fusion.4.order_ref, bf16[3,1024,768]{2,1,0:T(8,128)(2,1)} %attention_backward.3.cj_ref, bf16[1024,768]{1,0:T(8,128)(2,1)} %get-tuple-element.174.n_ref, ...), custom_call_target="tpu_custom_call" | custom-call | flops 3623878656 | bytes 14680064 | tf_op jit(solution)/shard_map/joint_gradients/pallas_call | solution.py:1045
  268.8 2.6 fusion.9
  271.4 1.5 collective-permute-start.11
  272.9 5.0 %collective-permute-start.13 = (bf16[512,768]{1,0:T(8,128)(2,1)}, bf16[512,768]{1,0:T(8,128)(2,1)}, u32[]{:S(2)}, u32[]{:S(2)}) collective-permute-start(bf16[512,768]{1,0:T(8,128)(2,1)} %get-tuple-element.285), channel_id=1, source_target_pairs={{0,17},{1,16},{2,19},{3,18},{4,21},{5,20},{6,23},{7,22},{8,25},{9,... | collective-permute-start | bytes 2359304 | tf_op jit(solution)/shard_map/ppermute | solution.py:1514
  278.0 2.2 collective-permute-start.12
  280.1 30.7 %feed_backward.3 = (bf16[1024,3072]{1,0:T(8,128)(2,1)}, f32[1024,768]{1,0:T(8,128)}, bf16[768,1024]{1,0:T(8,128)(2,1)}, bf16[768,1024]{1,0:T(8,128)(2,1)}, bf16[...) custom-call(s32[1]{0:T(128)} %bitcast.sec_ref, ...), custom_call_target="tpu_custom_call" | custom-call | flops 10871635968 | bytes 52428800 | tf_op jit(solution)/shard_map/feed_backward/pallas_call | solution.py:773
  310.9 3.9 add_convert_fusion.8
  314.7 3.5 add_convert_fusion.6
  318.2 0.5 collective-permute-start.16
  318.7 1.0 collective-permute-start.17
  319.7 20.1 %feed_gradients.3 = (bf16[16,448,384]{2,1,0:T(8,128)(2,1)}, bf16[16,448,384]{2,1,0:T(8,128)(2,1)}) custom-call(s32[1]{0:T(128)} %bitcast.sec_ref, s32[32]{0:T(128)} %broadcast_select_fusion.4.order_ref, bf16[1024,3072]{1,0:T(8,128)(2,1)} %get-tuple-element.190.cb_ref, bf16[1024,3072]{1,0:T(8,128)(2,1)} %get-tuple-element.179.hid_ref, ...), custom_call_target="tpu_custom_call" | custom-call | flops 10871635968 | bytes 31457280 | tf_op jit(solution)/shard_map/feed_gradients/pallas_call | solution.py:987
  339.8 3.1 collective-permute-done.17
  342.9 1.0 add_convert_fusion.12
  343.9 2.6 add_convert_fusion.10
  346.5 1.8 pad_maximum_fusion
  348.5 2.3 maximum_bitcast_fusion
  350.8 1.6 collective-permute-start.19
  352.5 1.5 collective-permute-start.20
  354.0 13.7 %attention_backward.4.refs_7_ = bf16[3,1024,768]{2,1,0:T(8,128)(2,1)} custom-call(bf16[12,1024,128]{2,1,0:T(8,128)(2,1)} %get-tuple-element.167.refs_0_, bf16[12,1024,128]{2,1,0:T(8,128)(2,1)} %get-tuple-element.132.k_ref.refs_1_, bf16[12,1024,128]{2,1,0:T(8,128)(2,1)} %get-tuple-element.133.v_ref.refs_2_, bf16[1024,768]{1,0:T(8,128)(2,1)} %get-tuple-element.203.refs_3_, ...), custom_call_target="tpu_custom_call" | custom-call | flops 10737418240 | bytes 6291456 | tf_op jit(solution)/shard_map/attention_backward/pallas_call | solution.py:853
  367.7 0.8 add_convert_fusion.16
  368.9 5.9 %add_convert_fusion = (bf16[8,448,384]{2,1,0:T(8,128)(2,1)}, bf16[8,448,384]{2,1,0:T(8,128)(2,1)S(1)}) fusion(bf16[16,448,384]{2,1,0:T(8,128)(2,1)} %collective-permute-done.18, bf16[16,448,384]{2,1,0:T(8,128)(2,1)} %get-tuple-element.204), kind=kLoop, calls=%fused_computation | loop fusion | flops 11010048 | bytes 16515072 | tf_op jit(solution)/shard_map/convert_element_type | solution.py:1150
  374.9 2.6 collective-permute-start.21
  377.4 0.9 collective-permute-start.22
  378.3 1.6 collective-permute-start.23
  379.9 24.5 %attention_backward.5.cj_ref = bf16[3,1024,768]{2,1,0:T(8,128)(2,1)} custom-call(bf16[12,1024,128]{2,1,0:T(8,128)(2,1)} %get-tuple-element.167.refs_0_, bf16[12,1024,128]{2,1,0:T(8,128)(2,1)} %get-tuple-element.132.k_ref.refs_1_, bf16[12,1024,128]{2,1,0:T(8,128)(2,1)} %get-tuple-element.133.v_ref.refs_2_, ...), custom_call_target="tpu_custom_call", output_to_operand_aliasing={{}: (7, {})} | custom-call | flops 21474836480 | bytes 12582912 | tf_op jit(solution)/shard_map/attention_backward/pallas_call | solution.py:853
  404.4 0.9 add_convert_fusion.18
  405.9 7.7 %collective-permute-done.24 = bf16[1,160,384]{2,1,0:T(8,128)(2,1)S(1)} collective-permute-done((bf16[1,160,384]{2,1,0:T(8,128)(2,1)S(1)}, bf16[1,160,384]{2,1,0:T(8,128)(2,1)S(1)}, u32[]{:S(2)}, u32[]{:S(2)}) %collective-permute-start.24) | collective-permute-done | bytes 122912 | tf_op jit(solution)/shard_map/ppermute | solution.py:1141
  413.6 0.9 add_bitcast_fusion.1
  414.5 1.0 pad_maximum_fusion.3.done_ref
  415.5 4.0 add_convert_fusion.4
  419.5 61.9 %last_step.1 = (f32[2,608,384]{2,1,0:T(8,128)}, bf16[512,768]{1,0:T(8,128)(2,1)}, bf16[3,512,768]{2,1,0:T(8,128)(2,1)}) custom-call(bf16[3,1024,768]{2,1,0:T(8,128)(2,1)} %attention_backward.5.cj_ref, bf16[1024,768]{1,0:T(8,128)(2,1)} %get-tuple-element.214.n_ref, bf16[1024,768]{1,0:T(8,128)(2,1)} %get-tuple-element.136.x_ref, ...), custom_call_target="tpu_custom_call" | custom-call | bytes 104857600 | tf_op jit(solution)/shard_map/last_step/pallas_call | solution.py:1353
  481.5 1.4 select_bitcast_fusion
  482.9 0.5 copy-done.4
  484.4 3.8 gradient_outputs.1
  488.2 3.0 maximum_convert_fusion
  (56 shorter events, 4.1 us)
Async XLA Ops:
  0.6 24.1 %collective-permute-start.2 = (bf16[768,2304]{1,0:T(8,128)(2,1)}, bf16[768,2304]{1,0:T(8,128)(2,1)S(1)}, u32[]{:S(2)}, u32[]{:S(2)}) collective-permute-start(bf16[768,2304]{1,0:T(8,128)(2,1)} %bitcast.81), channel_id=1, source_target_pairs={{0,16},{16,0},{1,17},{17,1},{2,18},{18,2},{3,19},{19,3},{4,20},{20... | collective-permute-start | bytes 10616840 | tf_op jit(solution)/shard_map/ppermute | solution.py:1460
  1.2 63.5 %collective-permute-start.4 = (bf16[768,3072]{1,0:T(8,128)(2,1)}, bf16[768,3072]{1,0:T(8,128)(2,1)}, u32[]{:S(2)}, u32[]{:S(2)}) collective-permute-start(bf16[768,3072]{1,0:T(8,128)(2,1)} %bitcast.71), channel_id=1, source_target_pairs={{0,16},{16,0},{1,17},{17,1},{2,18},{18,2},{3,19},{19,3},{4,20},{20... | collective-permute-start | bytes 14155784 | tf_op jit(solution)/shard_map/ppermute | solution.py:1460
  1.2 63.4 %collective-permute-start.5 = (bf16[3072,768]{1,0:T(8,128)(2,1)}, bf16[3072,768]{1,0:T(8,128)(2,1)}, u32[]{:S(2)}, u32[]{:S(2)}) collective-permute-start(bf16[3072,768]{1,0:T(8,128)(2,1)} %bitcast.76), channel_id=1, source_target_pairs={{0,16},{16,0},{1,17},{17,1},{2,18},{18,2},{3,19},{19,3},{4,20},{20... | collective-permute-start | bytes 14155784 | tf_op jit(solution)/shard_map/ppermute | solution.py:1460
  3.7 21.0 %collective-permute-start = (bf16[512,768]{1,0:T(8,128)(2,1)}, bf16[512,768]{1,0:T(8,128)(2,1)}, u32[]{:S(2)}, u32[]{:S(2)}) collective-permute-start(bf16[512,768]{1,0:T(8,128)(2,1)} %dynamic-slice_bitcast_fusion.6), channel_id=1, source_target_pairs={{0,1},{1,0},{2,3},{3,2},{4,5},{5,4},{6,7},{7,6},{8,9},{9,8},{10,11... | collective-permute-start | bytes 2359304 | tf_op jit(solution)/shard_map/ppermute | solution.py:1459
  11.2 9.8 %collective-permute-start.1 = (f32[1,12288]{1,0:T(1,128)}, f32[1,12288]{1,0:T(1,128)}, u32[]{:S(2)}, u32[]{:S(2)}) collective-permute-start(f32[1,12288]{1,0:T(1,128)} %get-tuple-element.127), channel_id=1, source_target_pairs={{0,16},{16,0},{1,17},{17,1},{2,18},{18,2},{3,19},{19,3},{4,20},{20... | collective-permute-start | bytes 147464 | tf_op jit(solution)/shard_map/ppermute | solution.py:1464
  20.9 43.8 %collective-permute-start.3 = (bf16[768,768]{1,0:T(8,128)(2,1)}, bf16[768,768]{1,0:T(8,128)(2,1)}, u32[]{:S(2)}, u32[]{:S(2)}) collective-permute-start(bf16[768,768]{1,0:T(8,128)(2,1)} %bitcast.87), channel_id=1, source_target_pairs={{0,16},{16,0},{1,17},{17,1},{2,18},{18,2},{3,19},{19,3},{4,20},{20... | collective-permute-start | bytes 3538952 | tf_op jit(solution)/shard_map/ppermute | solution.py:1460
  24.8 1.8 copy-start
  41.0 22.4 %collective-permute-start.6 = (bf16[512,768]{1,0:T(8,128)(2,1)S(1)}, bf16[512,768]{1,0:T(8,128)(2,1)S(1)}, u32[]{:S(2)}, u32[]{:S(2)}) collective-permute-start(bf16[512,768]{1,0:T(8,128)(2,1)S(1)} %get-tuple-element.277), channel_id=1, source_target_pairs={{0,1},{1,0},{2,3},{3,2},{4,5},{5,4},{6,7},{7,6},{8,9},{9,8},{10,11... | collective-permute-start | bytes 2359304 | tf_op jit(solution)/shard_map/ppermute | solution.py:1481
  123.1 24.8 %copy-start.1 = (bf16[1024,768]{1,0:T(8,128)(2,1)S(1)}, bf16[1024,768]{1,0:T(8,128)(2,1)}, u32[]{:S(2)}) copy-start(bf16[1024,768]{1,0:T(8,128)(2,1)} %get-tuple-element.137.y_ref.x_ref) | copy-start | bytes 4718596
  201.1 39.9 %collective-permute-start.10 = (bf16[16,448,384]{2,1,0:T(8,128)(2,1)}, bf16[16,448,384]{2,1,0:T(8,128)(2,1)}, u32[]{:S(2)}, u32[]{:S(2)}) collective-permute-start(bf16[16,448,384]{2,1,0:T(8,128)(2,1)} %get-tuple-element.170), channel_id=1, source_target_pairs={{0,16},{16,0},{1,17},{17,1},{2,18},{18,2},{3,19},{19,3},{4,20},{20... | collective-permute-start | bytes 16515080 | tf_op jit(solution)/shard_map/ppermute | solution.py:1133
  201.1 37.7 %collective-permute-start.7 = (bf16[512,768]{1,0:T(8,128)(2,1)}, bf16[512,768]{1,0:T(8,128)(2,1)S(1)}, u32[]{:S(2)}, u32[]{:S(2)}) collective-permute-start(bf16[512,768]{1,0:T(8,128)(2,1)} %get-tuple-element.161), channel_id=1, source_target_pairs={{0,1},{1,0},{16,17},{17,16},{2,3},{3,2},{18,19},{19,18},{4,5},{5,4... | collective-permute-start | bytes 2359304 | tf_op jit(solution)/shard_map/ppermute | solution.py:1500
  201.5 37.4 %collective-permute-start.8 = (bf16[512,768]{1,0:T(8,128)(2,1)S(1)}, bf16[512,768]{1,0:T(8,128)(2,1)S(1)}, u32[]{:S(2)}, u32[]{:S(2)}) collective-permute-start(bf16[512,768]{1,0:T(8,128)(2,1)S(1)} %get-tuple-element.162), channel_id=1, source_target_pairs={{0,16},{1,17},{16,0},{17,1},{2,18},{3,19},{18,2},{19,3},{4,20},{5,... | collective-permute-start | bytes 2359304 | tf_op jit(solution)/shard_map/ppermute | solution.py:1500
  201.6 37.2 %collective-permute-start.9 = (bf16[512,768]{1,0:T(8,128)(2,1)S(1)}, bf16[512,768]{1,0:T(8,128)(2,1)S(1)}, u32[]{:S(2)}, u32[]{:S(2)}) collective-permute-start(bf16[512,768]{1,0:T(8,128)(2,1)S(1)} %get-tuple-element.163), channel_id=1, source_target_pairs={{0,17},{1,16},{16,1},{17,0},{2,19},{3,18},{18,3},{19,2},{4,21},{5,... | collective-permute-start | bytes 2359304 | tf_op jit(solution)/shard_map/ppermute | solution.py:1500
  238.8 0.9 copy-start.5
  238.8 1.2 copy-start.6
  240.0 0.9 copy-start.7
  247.0 67.7 %collective-permute-start.14 = (bf16[8,448,384]{2,1,0:T(8,128)(2,1)}, bf16[8,448,384]{2,1,0:T(8,128)(2,1)}, u32[]{:S(2)}, u32[]{:S(2)}) collective-permute-start(bf16[8,448,384]{2,1,0:T(8,128)(2,1)} %get-tuple-element.187), channel_id=1, source_target_pairs={{0,2},{1,3},{2,0},{3,1},{4,6},{5,7},{6,4},{7,5},{8,10},{9,11},{10,... | collective-permute-start | bytes 8257544 | tf_op jit(solution)/shard_map/ppermute | solution.py:1141
  268.8 42.1 %collective-permute-start.15 = (bf16[16,160,384]{2,1,0:T(8,128)(2,1)}, bf16[16,160,384]{2,1,0:T(8,128)(2,1)}, u32[]{:S(2)}, u32[]{:S(2)}) collective-permute-start(bf16[16,160,384]{2,1,0:T(8,128)(2,1)} %get-tuple-element.189), channel_id=1, source_target_pairs={{0,16},{16,0},{1,17},{17,1},{2,18},{18,2},{3,19},{19,3},{4,20},{20... | collective-permute-start | bytes 5898248 | tf_op jit(solution)/shard_map/ppermute | solution.py:1133
  271.4 47.3 %collective-permute-start.11 = (bf16[512,768]{1,0:T(8,128)(2,1)}, bf16[512,768]{1,0:T(8,128)(2,1)}, u32[]{:S(2)}, u32[]{:S(2)}) collective-permute-start(bf16[512,768]{1,0:T(8,128)(2,1)} %get-tuple-element.285), channel_id=1, source_target_pairs={{16,17},{17,16},{18,19},{19,18},{20,21},{21,20},{22,23},{23,22},{2... | collective-permute-start | bytes 2359304 | tf_op jit(solution)/shard_map/ppermute | solution.py:1514
  272.9 45.8 %collective-permute-start.13 = (bf16[512,768]{1,0:T(8,128)(2,1)}, bf16[512,768]{1,0:T(8,128)(2,1)}, u32[]{:S(2)}, u32[]{:S(2)}) collective-permute-start(bf16[512,768]{1,0:T(8,128)(2,1)} %get-tuple-element.285), channel_id=1, source_target_pairs={{0,17},{1,16},{2,19},{3,18},{4,21},{5,20},{6,23},{7,22},{8,25},{9,... | collective-permute-start | bytes 2359304 | tf_op jit(solution)/shard_map/ppermute | solution.py:1514
  278.0 40.8 %collective-permute-start.12 = (bf16[512,768]{1,0:T(8,128)(2,1)}, bf16[512,768]{1,0:T(8,128)(2,1)}, u32[]{:S(2)}, u32[]{:S(2)}) collective-permute-start(bf16[512,768]{1,0:T(8,128)(2,1)} %get-tuple-element.222), channel_id=1, source_target_pairs={{0,16},{1,17},{2,18},{3,19},{4,20},{5,21},{6,22},{7,23},{8,24},{9,... | collective-permute-start | bytes 2359304 | tf_op jit(solution)/shard_map/ppermute | solution.py:1514
  318.2 25.7 %collective-permute-start.16 = (bf16[4,448,384]{2,1,0:T(8,128)(2,1)}, bf16[4,448,384]{2,1,0:T(8,128)(2,1)}, u32[]{:S(2)}, u32[]{:S(2)}) collective-permute-start(bf16[4,448,384]{2,1,0:T(8,128)(2,1)} %get-tuple-element.200), channel_id=1, source_target_pairs={{0,1},{1,0},{2,3},{3,2},{4,5},{5,4},{6,7},{7,6},{8,9},{9,8},{10,11... | collective-permute-start | bytes 4128776 | tf_op jit(solution)/shard_map/ppermute | solution.py:1141
  318.7 24.1 %collective-permute-start.17 = (bf16[8,160,384]{2,1,0:T(8,128)(2,1)}, bf16[8,160,384]{2,1,0:T(8,128)(2,1)S(1)}, u32[]{:S(2)}, u32[]{:S(2)}) collective-permute-start(bf16[8,160,384]{2,1,0:T(8,128)(2,1)} %get-tuple-element.202), channel_id=1, source_target_pairs={{0,2},{1,3},{2,0},{3,1},{4,6},{5,7},{6,4},{7,5},{8,10},{9,11},{10,... | collective-permute-start | bytes 2949128 | tf_op jit(solution)/shard_map/ppermute | solution.py:1141
  319.7 23.2 %copy-start.2 = (bf16[8,160,384]{2,1,0:T(8,128)(2,1)S(1)}, bf16[8,160,384]{2,1,0:T(8,128)(2,1)}, u32[]{:S(2)}) copy-start(bf16[8,160,384]{2,1,0:T(8,128)(2,1)} %get-tuple-element.201) | copy-start | bytes 2949124
  343.9 2.6 copy-start.3
  346.5 22.4 %collective-permute-start.18 = (bf16[16,448,384]{2,1,0:T(8,128)(2,1)}, bf16[16,448,384]{2,1,0:T(8,128)(2,1)}, u32[]{:S(2)}, u32[]{:S(2)}) collective-permute-start(bf16[16,448,384]{2,1,0:T(8,128)(2,1)} %get-tuple-element.205), channel_id=1, source_target_pairs={{0,16},{16,0},{1,17},{17,1},{2,18},{18,2},{3,19},{19,3},{4,20},{20... | collective-permute-start | bytes 16515080 | tf_op jit(solution)/shard_map/ppermute | solution.py:1133
  348.5 2.3 copy-start.8
  348.5 3.9 copy-start.9
  350.8 17.9 %collective-permute-start.19 = (bf16[2,448,384]{2,1,0:T(8,128)(2,1)S(1)}, bf16[2,448,384]{2,1,0:T(8,128)(2,1)S(1)}, u32[]{:S(2)}, u32[]{:S(2)}) collective-permute-start(bf16[2,448,384]{2,1,0:T(8,128)(2,1)S(1)} %copy-done.8), channel_id=1, source_target_pairs={{0,4},{1,5},{2,6},{3,7},{4,0},{5,1},{6,2},{7,3},{8,12},{9,13},{10,... | collective-permute-start | bytes 2064392 | tf_op jit(solution)/shard_map/ppermute | solution.py:1141
  352.5 15.2 %collective-permute-start.20 = (bf16[4,160,384]{2,1,0:T(8,128)(2,1)S(1)}, bf16[4,160,384]{2,1,0:T(8,128)(2,1)S(1)}, u32[]{:S(2)}, u32[]{:S(2)}) collective-permute-start(bf16[4,160,384]{2,1,0:T(8,128)(2,1)S(1)} %copy-done.9), channel_id=1, source_target_pairs={{0,1},{1,0},{2,3},{3,2},{4,5},{5,4},{6,7},{7,6},{8,9},{9,8},{10,11... | collective-permute-start | bytes 1474568 | tf_op jit(solution)/shard_map/ppermute | solution.py:1141
  374.9 30.9 %collective-permute-start.21 = (bf16[1,448,384]{2,1,0:T(8,128)(2,1)S(1)}, bf16[1,448,384]{2,1,0:T(8,128)(2,1)S(1)}, u32[]{:S(2)}, u32[]{:S(2)}) collective-permute-start(bf16[1,448,384]{2,1,0:T(8,128)(2,1)S(1)} %get-tuple-element.212), channel_id=1, source_target_pairs={{0,8},{1,9},{2,10},{3,11},{4,12},{5,13},{6,14},{7,15},{8,0},{9,1},... | collective-permute-start | bytes 1032200 | tf_op jit(solution)/shard_map/ppermute | solution.py:1141
  377.4 38.1 %collective-permute-start.22 = (bf16[8,448,384]{2,1,0:T(8,128)(2,1)}, bf16[8,448,384]{2,1,0:T(8,128)(2,1)}, u32[]{:S(2)}, u32[]{:S(2)}) collective-permute-start(bf16[8,448,384]{2,1,0:T(8,128)(2,1)} %get-tuple-element.217), channel_id=1, source_target_pairs={{0,2},{1,3},{2,0},{3,1},{4,6},{5,7},{6,4},{7,5},{8,10},{9,11},{10,... | collective-permute-start | bytes 8257544 | tf_op jit(solution)/shard_map/ppermute | solution.py:1141
  378.3 26.1 %collective-permute-start.23 = (bf16[2,160,384]{2,1,0:T(8,128)(2,1)}, bf16[2,160,384]{2,1,0:T(8,128)(2,1)}, u32[]{:S(2)}, u32[]{:S(2)}) collective-permute-start(bf16[2,160,384]{2,1,0:T(8,128)(2,1)} %get-tuple-element.220), channel_id=1, source_target_pairs={{0,4},{1,5},{2,6},{3,7},{4,0},{5,1},{6,2},{7,3},{8,12},{9,13},{10,... | collective-permute-start | bytes 737288 | tf_op jit(solution)/shard_map/ppermute | solution.py:1141
  405.4 8.2 %collective-permute-start.24 = (bf16[1,160,384]{2,1,0:T(8,128)(2,1)S(1)}, bf16[1,160,384]{2,1,0:T(8,128)(2,1)S(1)}, u32[]{:S(2)}, u32[]{:S(2)}) collective-permute-start(bf16[1,160,384]{2,1,0:T(8,128)(2,1)S(1)} %add_convert_fusion.18), channel_id=1, source_target_pairs={{0,8},{1,9},{2,10},{3,11},{4,12},{5,13},{6,14},{7,15},{8,0},{9,1},... | collective-permute-start | bytes 368648 | tf_op jit(solution)/shard_map/ppermute | solution.py:1141
  481.5 1.9 copy-start.4
